TPU v7x, 512 devices: a whole 4x8x8 slice. The times are simulated.
512 devices in a mesh: dp: 16 (over z, core), fsdp: 32 (over y, x).
Axes of the slice: x: 4, y: 8, z: 8, core: 2. Of those that a mesh axis runs over, the one named last changes fastest.
Arguments:
- out_grad: bfloat16 [4096, 4096], P(('dp', 'fsdp')), may hold values from -6 to 6
- gate_pre: bfloat16 [4096, 14848], P('dp', 'fsdp'), may hold values from -6 to 6
- up_pre: bfloat16 [4096, 14848], P('dp', 'fsdp'), may hold values from -6 to 6
- down_weight: bfloat16 [14848, 4096], P('fsdp', 'dp'), may hold values from -0.09375 to 0.09375
- momentum: float32 [16, 14848, 256], P('dp', 'fsdp'), may hold values from -6 to 6
- band_index: int32 [16, 14848, 32], P('dp', 'fsdp'), may hold values from 0 to 255, as said below
- band_count: int32 [16, 14848], P('dp', 'fsdp'), may hold values from 1 to 32, as said below
Outputs:
- gate_grad: bfloat16 [4096, 14848], P('dp', 'fsdp')
- up_grad: bfloat16 [4096, 14848], P('dp', 'fsdp')
- new_momentum: float32 [16, 14848, 256], P('dp', 'fsdp')
- update: float32 [14848, 256], P('fsdp')
Inputs may be any that keep to these rules, and one draw needn't show every extreme that they name: `band_index`: for each worker and block the 32 entries of the list are different frequencies. `band_count`: on every worker some block uses all 32 entries and some block uses one.
All inputs are finite; a program needn't handle non-finite values.
Results may differ from a plain program's by a relative error of at most 0.0019.
Values may be sent and summed in bfloat16 or wider, within the bound.
No kernel may reach another device: no remote copies, remote signals or barrier semaphores. Data moves between devices by JAX's collectives and lax.ppermute only.
A program may use at most 64 MiB of HBM per device.

v0:
```python
import math

import jax
import jax.numpy as jnp
from jax import lax
from jax.experimental import pallas as pl
from jax.experimental.pallas import tpu as pltpu
from jax.sharding import Mesh
from jax.sharding import PartitionSpec as P


DP = ("z", "core")
FSDP = ("y", "x")
momentum_decay = 0.9


def cosine_matrix(length):
    frequency = jnp.arange(length, dtype=jnp.int32).astype(jnp.float32)[:, None]
    position = jnp.arange(length, dtype=jnp.int32).astype(jnp.float32)[None, :]
    angles = math.pi * (position + 0.5) * frequency / length
    row_weight = jnp.where(frequency == 0.0, math.sqrt(1.0 / length), math.sqrt(2.0 / length))
    return jnp.cos(angles) * row_weight


def gathered(value, axis):
    count = lax.axis_size(axis)
    copies = jnp.broadcast_to(value[None], (count, *value.shape))
    return lax.all_to_all(copies, axis, 0, 0)


def product_kernel(order_ref, *refs):
    pieces, refs = refs[:4], refs[4:]
    weight_ref, gate_ref, up_ref, gate_grad_ref, up_grad_ref, total_ref, act_ref, slope_ref, rows_ref = refs
    step = pl.program_id(0)
    last = pl.num_programs(0) - 1

    @pl.when(step == 0)
    def _():
        gate = gate_ref[...].astype(jnp.float32)
        sigmoid = jax.nn.sigmoid(gate)
        act_ref[...] = gate * sigmoid
        slope_ref[...] = up_ref[...].astype(jnp.float32) * sigmoid * (1.0 + gate * (1.0 - sigmoid))

    for i, piece in enumerate(pieces):
        rows_ref[:, order_ref[i]] = piece[...]
    width = weight_ref.shape[2]
    rows = rows_ref[...].reshape(-1, rows_ref.shape[3])
    total = None
    for b in range(weight_ref.shape[0]):
        term = lax.dot_general(
            weight_ref[b],
            rows[:, b * width : (b + 1) * width],
            (((1,), (1,)), ((), ())),
            preferred_element_type=jnp.float32,
        )
        total = term if total is None else total + term

    @pl.when(step == 0)
    def _():
        total_ref[...] = total

    @pl.when((step > 0) & (step < last))
    def _():
        total_ref[...] += total

    @pl.when(step == last)
    def _():
        hidden_grad = total_ref[...] + total
        up_grad_ref[...] = (hidden_grad * act_ref[...]).astype(jnp.bfloat16)
        gate_grad_ref[...] = (hidden_grad * slope_ref[...]).astype(jnp.bfloat16)


def product(order, pieces, weight, gate, up):
    blocks, rows, width = weight.shape
    tokens = gate.shape[1]
    groups, depth, features = pieces[0].shape
    per_step = blocks // 2
    whole = pl.BlockSpec((rows, tokens), lambda k, order: (0, 0))
    piece = pl.BlockSpec((groups, depth, per_step * width), lambda k, order: (0, 0, k))
    return pl.pallas_call(
        product_kernel,
        grid_spec=pltpu.PrefetchScalarGridSpec(
            num_scalar_prefetch=1,
            grid=(blocks // per_step,),
            in_specs=[piece] * 4
            + [pl.BlockSpec((per_step, rows, width), lambda k, order: (k, 0, 0)), whole, whole],
            out_specs=[whole, whole],
            scratch_shapes=[pltpu.VMEM((rows, tokens), jnp.float32)] * 3
            + [pltpu.VMEM((groups, 4, depth, per_step * width), jnp.bfloat16)],
        ),
        out_shape=[jax.ShapeDtypeStruct((rows, tokens), jnp.bfloat16)] * 2,
        compiler_params=pltpu.CompilerParams(dimension_semantics=("arbitrary",)),
        cost_estimate=pl.CostEstimate(
            flops=2 * rows * tokens * features,
            bytes_accessed=2 * (tokens + rows) * features + 8 * rows * tokens,
            transcendentals=rows * tokens,
        ),
    )(order, *pieces, weight, gate, up)


def per_device_body(out_grad, gate_pre, up_pre, down_weight, momentum, band_index, band_count):
    worker_rows = gate_pre.shape[0]
    own_rows = gate_pre.shape[1]
    window = momentum.shape[2]
    workers = lax.axis_size(DP)
    block_count = band_index.shape[1]
    length = own_rows * window // block_count

    window_grad = gathered(out_grad[:, :window], FSDP).reshape(worker_rows, window)
    weight = lax.all_gather(down_weight, DP)
    own_piece = gathered(out_grad, "y")
    shifts = (0, 1, 3, 2)
    order = (lax.axis_index("x") + 4 - jnp.array(shifts, jnp.int32)) & 3
    pieces = [own_piece]
    for s in shifts[1:]:
        pieces.append(lax.ppermute(own_piece, "x", [(i, (i + s) % 4) for i in range(4)]))

    gate_float = gate_pre.astype(jnp.float32)
    hidden = (gate_float * jax.nn.sigmoid(gate_float) * up_pre.astype(jnp.float32)).astype(
        jnp.bfloat16
    )
    grad_scale = 1.0 / math.sqrt(worker_rows)
    worker_grad = (
        lax.dot_general(
            hidden, window_grad, (((0,), (0,)), ((), ())), preferred_element_type=jnp.float32
        )
        * grad_scale
    )
    slot_list = band_index[0]
    slot_ids = jnp.arange(slot_list.shape[1], dtype=jnp.int32)
    used = jnp.where(slot_ids[None, :] < band_count[0][:, None], slot_list, -1)
    frequency = jnp.arange(length, dtype=jnp.int32)
    mask = jnp.any(used[:, :, None] == frequency[None, None, :], axis=1)

    cosine_table = cosine_matrix(length)
    mixed = momentum_decay * momentum[0] + worker_grad
    spectrum = jnp.dot(mixed, cosine_table.T, precision=lax.Precision.HIGHEST)
    sent = jnp.where(mask, spectrum, 0.0)
    new_momentum = mixed - jnp.dot(sent, cosine_table, precision=lax.Precision.HIGHEST)

    share = -(-block_count // workers)
    share = -(-share // 8) * 8
    padded = jnp.pad(sent, ((0, share * workers - block_count), (0, 0)))
    parts = lax.all_to_all(padded.reshape(workers, share, length), DP, 0, 0)
    averaged = parts.sum(0) / workers
    own_update = jnp.dot(averaged, cosine_table, precision=lax.Precision.HIGHEST)
    update = gathered(own_update, DP).reshape(workers * share, length)[:block_count]

    gate_grad, up_grad = product(order, pieces, weight, gate_pre.T, up_pre.T)
    return (gate_grad.T, up_grad.T, new_momentum[None], update)


def solution(mesh):
    torus = Mesh(mesh.devices.reshape(8, 2, 8, 4), ("z", "core", "y", "x"))
    both = ("z", "core", "y", "x")
    return jax.shard_map(
        per_device_body,
        mesh=torus,
        in_specs=(
            P(both, None),
            P(DP, FSDP),
            P(DP, FSDP),
            P(FSDP, DP),
            P(DP, FSDP, None),
            P(DP, FSDP, None),
            P(DP, FSDP),
        ),
        out_specs=(P(DP, FSDP), P(DP, FSDP), P(DP, FSDP, None), P(FSDP, None)),
        check_vma=False,
    )
```

profile of v0, /device:TPU:1, one launch (start us, length us, event | category | flops | bytes accessed | tf_op | source)
XLA Modules:
  0.0 134.7 jit_solution(8785922920807136327)
XLA Ops:
  7.2 0.7 all-gather.3.cloned.1.call-update
  7.9 0.7 slice.6
  8.6 0.7 broadcast_in_dim.25
  9.3 10.5 %all-to-all-start.1 = ((bf16[32,8,256]{2,1,0:T(8,128)(2,1)}), bf16[32,8,256]{2,1,0:T(8,128)(2,1)S(1)}, u32[]{:S(2)}, u32[]{:S(2)}) async-start(bf16[32,8,256]{2,1,0:T(8,128)(2,1)} %broadcast_in_dim.25), calls=%async_computation.1 | async-start | bytes 262144 | tf_op jit(solution)/shard_map/all_to_all | solution.py:28
  19.8 0.9 bitcast_select_fusion
  20.8 6.2 %fusion = pred[464,256]{1,0:T(8,128)(4,1)S(1)} fusion(s32[464,32]{1,0:T(8,128)S(1)} %copy.13), kind=kLoop, calls=%fused_computation.1 | loop fusion | flops 7483392 | bytes 178176 | tf_op jit(solution)/shard_map/reduce_or | solution.py:133
  27.0 2.1 %all-to-all-done.1 = bf16[32,8,256]{2,1,0:T(8,128)(2,1)S(1)} async-done(((bf16[32,8,256]{2,1,0:T(8,128)(2,1)}), bf16[32,8,256]{2,1,0:T(8,128)(2,1)S(1)}, u32[]{:S(2)}, u32[]{:S(2)}) %all-to-all-start.1) | async-done | bytes 131104 | tf_op jit(solution)/shard_map/all_to_all | solution.py:28
  29.1 1.6 %fusion.1 = f32[464,256]{1,0:T(8,128)S(1)} fusion(f32[1,464,256]{2,1,0:T(8,128)} %param.12, bf16[256,464]{0,1:T(8,128)(2,1)} %param.10, bf16[256,464]{0,1:T(8,128)(2,1)} %param.9, bf16[32,8,256]{2,1,0:T(8,128)(2,1)S(1)} %all-to-all-done.1), kind=kOutput, calls=%fused_computation.3 | convolution fusion | flops 62124032 | bytes 1556480 | tf_op jit(solution)/shard_map/dot_general | solution.py:124
  30.8 1.5 %convolution_select_fusion = f32[464,256]{1,0:T(8,128)S(1)} fusion(pred[464,256]{1,0:T(8,128)(4,1)S(1)} %fusion, f32[464,256]{1,0:T(8,128)S(1)} %fusion.1, f32[256]{0:T(256)S(1)} %get-tuple-element.8, f32[256]{0:T(256)S(1)} %iota_convert_fusion, f32[256]{0:T(256)S(1)} %get-tuple-element.9), kind=kOutput, calls=%fused_computation.6 | convolution fusion | flops 365219840 | bytes 1072128 | tf_op jit(solution)/shard_map/dot_general | solution.py:137
  32.3 33.4 %all_to_all.20 = f32[16,32,256]{2,1,0:T(8,128)S(1)} all-to-all(f32[16,32,256]{2,1,0:T(8,128)S(1)} %bitcast.20), channel_id=1, replica_groups=mesh['z'=8,'core'=2,'y'=8,'x'=4] {'z','core'}, dimensions={0} | all-to-all | bytes 1048576 | tf_op jit(solution)/shard_map/all_to_all | solution.py:144
  65.7 0.8 broadcast_in_dim.24
  66.5 4.1 %all-to-all-start = ((bf16[8,8,4096]{2,1,0:T(8,128)(2,1)}), bf16[8,8,4096]{2,1,0:T(8,128)(2,1)S(1)}, u32[]{:S(2)}, u32[]{:S(2)}) async-start(bf16[8,8,4096]{2,1,0:T(8,128)(2,1)} %broadcast_in_dim.24), calls=%async_computation | async-start | bytes 1048576 | tf_op jit(solution)/shard_map/all_to_all | solution.py:28
  70.7 1.2 fusion.8
  71.9 16.7 %all-to-all-done.refs_0_ = bf16[8,8,4096]{2,1,0:T(8,128)(2,1)S(1)} async-done(((bf16[8,8,4096]{2,1,0:T(8,128)(2,1)}), bf16[8,8,4096]{2,1,0:T(8,128)(2,1)S(1)}, u32[]{:S(2)}, u32[]{:S(2)}) %all-to-all-start) | async-done | bytes 524320 | tf_op jit(solution)/shard_map/all_to_all | solution.py:28
  88.6 0.9 broadcast_in_dim.49
  89.5 4.1 %all-to-all-start.3 = ((f32[16,32,256]{2,1,0:T(8,128)}), f32[16,32,256]{2,1,0:T(8,128)S(1)}, u32[]{:S(2)}, u32[]{:S(2)}) async-start(f32[16,32,256]{2,1,0:T(8,128)} %broadcast_in_dim.49), calls=%async_computation.3 | async-start | bytes 1048576 | tf_op jit(solution)/shard_map/all_to_all | solution.py:28
  93.6 3.1 %collective-permute-start = (bf16[8,8,4096]{2,1,0:T(8,128)(2,1)S(1)}, bf16[8,8,4096]{2,1,0:T(8,128)(2,1)S(1)}, u32[]{:S(2)}, u32[]{:S(2)}) collective-permute-start(bf16[8,8,4096]{2,1,0:T(8,128)(2,1)S(1)} %all-to-all-done.refs_0_), channel_id=1, source_target_pairs={{0,1},{1,2},{2,3},{3,0},{4,5},{5,6},{6,7},{7,4},{8,9},{9,10},{10,1... | collective-permute-start | bytes 1572872 | tf_op jit(solution)/shard_map/ppermute | solution.py:116
  96.7 3.4 %collective-permute-start.1 = (bf16[8,8,4096]{2,1,0:T(8,128)(2,1)S(1)}, bf16[8,8,4096]{2,1,0:T(8,128)(2,1)S(1)}, u32[]{:S(2)}, u32[]{:S(2)}) collective-permute-start(bf16[8,8,4096]{2,1,0:T(8,128)(2,1)S(1)} %all-to-all-done.refs_0_), channel_id=1, source_target_pairs={{0,3},{1,0},{2,1},{3,2},{4,7},{5,4},{6,5},{7,6},{8,11},{9,8},{10,9... | collective-permute-start | bytes 1572872 | tf_op jit(solution)/shard_map/ppermute | solution.py:116
  100.1 3.4 %collective-permute-start.2 = (bf16[8,8,4096]{2,1,0:T(8,128)(2,1)S(1)}, bf16[8,8,4096]{2,1,0:T(8,128)(2,1)}, u32[]{:S(2)}, u32[]{:S(2)}) collective-permute-start(bf16[8,8,4096]{2,1,0:T(8,128)(2,1)S(1)} %all-to-all-done.refs_0_), channel_id=1, source_target_pairs={{0,2},{1,3},{2,0},{3,1},{4,6},{5,7},{6,4},{7,5},{8,10},{9,11},{10,... | collective-permute-start | bytes 1572872 | tf_op jit(solution)/shard_map/ppermute | solution.py:116
  104.1 2.3 %fusion.2 = f32[1,464,256]{2,1,0:T(8,128)} fusion(f32[464,256]{1,0:T(8,128)S(1)} %fusion.1, f32[464,256]{1,0:T(8,128)S(1)} %convolution_select_fusion, f32[256]{0:T(256)S(1)} %get-tuple-element.8, f32[256]{0:T(256)S(1)} %iota_convert_fusion, f32[256]{0:T(256)S(1)} %get-tuple-element.9), kind=kOutput, calls=%fused_computation.5 | convolution fusion | flops 365219840 | bytes 1428480 | tf_op jit(solution)/shard_map/dot_general | solution.py:139
  106.4 4.4 %all-to-all-done.3 = f32[16,32,256]{2,1,0:T(8,128)S(1)} async-done(((f32[16,32,256]{2,1,0:T(8,128)}), f32[16,32,256]{2,1,0:T(8,128)S(1)}, u32[]{:S(2)}, u32[]{:S(2)}) %all-to-all-start.3) | async-done | bytes 524320 | tf_op jit(solution)/shard_map/all_to_all | solution.py:28
  110.8 0.8 slice.8
  111.7 10.7 %collective-permute-done.2.refs_3_ = bf16[8,8,4096]{2,1,0:T(8,128)(2,1)} collective-permute-done((bf16[8,8,4096]{2,1,0:T(8,128)(2,1)S(1)}, bf16[8,8,4096]{2,1,0:T(8,128)(2,1)}, u32[]{:S(2)}, u32[]{:S(2)}) %collective-permute-start.2) | collective-permute-done | bytes 524320 | tf_op jit(solution)/shard_map/ppermute | solution.py:116
  122.3 5.5 %shard_map.111 = (bf16[464,256]{1,0:T(8,128)(2,1)}, bf16[464,256]{1,0:T(8,128)(2,1)}) custom-call(s32[4]{0:T(128)} %add_and_fusion.order_ref, bf16[8,8,4096]{2,1,0:T(8,128)(2,1)} %copy-done, bf16[8,8,4096]{2,1,0:T(8,128)(2,1)} %copy-done.1, bf16[8,8,4096]{2,1,0:T(8,128)(2,1)} %copy-done.2, bf16[8,8,4096]{2,1,0:T(8,128)(2,1)} %collective-permute-done.2.refs_3_, ...), custom_call_target="tpu_custom_call" | custom-call | flops 973078528 | bytes 6848512 | tf_op jit(solution)/shard_map/pallas_call | solution.py:80
  (20 shorter events, 0.9 us)
Async XLA Ops:
  7.2 58.6 %copy-start.3 = (bf16[8,4096]{1,0:T(8,128)(2,1)S(1)}, bf16[8,4096]{1,0:T(8,128)(2,1)}, u32[]{:S(2)}) copy-start(bf16[8,4096]{1,0:T(8,128)(2,1)} %param.8) | copy-start | bytes 196612
  7.2 115.2 %all-gather.3.cloned.1.call-start = ((), (), s32[]{:S(2)}) async-start(), calls=%async_computation.4 | async-start | bytes 4038656 | tf_op jit(solution)/shard_map/all_gather | solution.py:110
  9.3 19.8 %all-to-all-start.1 = ((bf16[32,8,256]{2,1,0:T(8,128)(2,1)}), bf16[32,8,256]{2,1,0:T(8,128)(2,1)S(1)}, u32[]{:S(2)}, u32[]{:S(2)}) async-start(bf16[32,8,256]{2,1,0:T(8,128)(2,1)} %broadcast_in_dim.25), calls=%async_computation.1 | async-start | bytes 262144 | tf_op jit(solution)/shard_map/all_to_all | solution.py:28
  30.8 72.8 %copy-start.4 = (s32[4]{0:T(128)S(1)}, s32[4]{0:T(128)}, u32[]{:S(2)}) copy-start(s32[4]{0:T(128)} %constant.47) | copy-start | bytes 52
  66.5 22.0 %all-to-all-start = ((bf16[8,8,4096]{2,1,0:T(8,128)(2,1)}), bf16[8,8,4096]{2,1,0:T(8,128)(2,1)S(1)}, u32[]{:S(2)}, u32[]{:S(2)}) async-start(bf16[8,8,4096]{2,1,0:T(8,128)(2,1)} %broadcast_in_dim.24), calls=%async_computation | async-start | bytes 1048576 | tf_op jit(solution)/shard_map/all_to_all | solution.py:28
  88.6 33.8 %copy-start = (bf16[8,8,4096]{2,1,0:T(8,128)(2,1)}, bf16[8,8,4096]{2,1,0:T(8,128)(2,1)S(1)}, u32[]{:S(2)}) copy-start(bf16[8,8,4096]{2,1,0:T(8,128)(2,1)S(1)} %all-to-all-done.refs_0_) | copy-start | bytes 1572868
  89.5 21.3 %all-to-all-start.3 = ((f32[16,32,256]{2,1,0:T(8,128)}), f32[16,32,256]{2,1,0:T(8,128)S(1)}, u32[]{:S(2)}, u32[]{:S(2)}) async-start(f32[16,32,256]{2,1,0:T(8,128)} %broadcast_in_dim.49), calls=%async_computation.3 | async-start | bytes 1048576 | tf_op jit(solution)/shard_map/all_to_all | solution.py:28
  93.6 18.0 %collective-permute-start = (bf16[8,8,4096]{2,1,0:T(8,128)(2,1)S(1)}, bf16[8,8,4096]{2,1,0:T(8,128)(2,1)S(1)}, u32[]{:S(2)}, u32[]{:S(2)}) collective-permute-start(bf16[8,8,4096]{2,1,0:T(8,128)(2,1)S(1)} %all-to-all-done.refs_0_), channel_id=1, source_target_pairs={{0,1},{1,2},{2,3},{3,0},{4,5},{5,6},{6,7},{7,4},{8,9},{9,10},{10,1... | collective-permute-start | bytes 1572872 | tf_op jit(solution)/shard_map/ppermute | solution.py:116
  96.7 15.0 %collective-permute-start.1 = (bf16[8,8,4096]{2,1,0:T(8,128)(2,1)S(1)}, bf16[8,8,4096]{2,1,0:T(8,128)(2,1)S(1)}, u32[]{:S(2)}, u32[]{:S(2)}) collective-permute-start(bf16[8,8,4096]{2,1,0:T(8,128)(2,1)S(1)} %all-to-all-done.refs_0_), channel_id=1, source_target_pairs={{0,3},{1,0},{2,1},{3,2},{4,7},{5,4},{6,5},{7,6},{8,11},{9,8},{10,9... | collective-permute-start | bytes 1572872 | tf_op jit(solution)/shard_map/ppermute | solution.py:116
  100.1 22.2 %collective-permute-start.2 = (bf16[8,8,4096]{2,1,0:T(8,128)(2,1)S(1)}, bf16[8,8,4096]{2,1,0:T(8,128)(2,1)}, u32[]{:S(2)}, u32[]{:S(2)}) collective-permute-start(bf16[8,8,4096]{2,1,0:T(8,128)(2,1)S(1)} %all-to-all-done.refs_0_), channel_id=1, source_target_pairs={{0,2},{1,3},{2,0},{3,1},{4,6},{5,7},{6,4},{7,5},{8,10},{9,11},{10,... | collective-permute-start | bytes 1572872 | tf_op jit(solution)/shard_map/ppermute | solution.py:116
  111.6 10.7 %copy-start.1 = (bf16[8,8,4096]{2,1,0:T(8,128)(2,1)}, bf16[8,8,4096]{2,1,0:T(8,128)(2,1)S(1)}, u32[]{:S(2)}) copy-start(bf16[8,8,4096]{2,1,0:T(8,128)(2,1)S(1)} %collective-permute-done.refs_1_) | copy-start | bytes 1572868
  111.7 10.7 %copy-start.2 = (bf16[8,8,4096]{2,1,0:T(8,128)(2,1)}, bf16[8,8,4096]{2,1,0:T(8,128)(2,1)S(1)}, u32[]{:S(2)}) copy-start(bf16[8,8,4096]{2,1,0:T(8,128)(2,1)S(1)} %collective-permute-done.1.refs_2_) | copy-start | bytes 1572868
Sparse Core Ops, SparseCore 0:
  10.1 59.8 all-gather.2
where the time goes:
time: 137 us; the launch traced here: 135 us
  waiting for transfers between devices  34.6 us (25%)
  blocking collectives  33.4 us (24%)
  starting transfers between devices  28.6 us (21%)
  between operations  14.2 us (10%)
  other arithmetic  7.72 us (6%)
  matrix products  6.65 us (5%)
  Pallas kernels  5.45 us (4%)
  local copies, waits for them, and re-layouts  4.08 us (3%)
    all_to_all x1, blocking collectives, per_device_body(): parts = lax.all_to_all(padded.reshape(workers, share, length), DP, 0, 0)  33.4 us
    all_to_all x3, waiting for transfers between devices, gathered(): return lax.all_to_all(copies, axis, 0, 0)  23.2 us
    all_to_all x3, starting transfers between devices, gathered(): return lax.all_to_all(copies, axis, 0, 0)  18.7 us
    ppermute x3, waiting for transfers between devices, per_device_body(): lax.ppermute(own_piece, 'x', [(i, (i + s) % 4) for i in range(4)])  10.7 us
    ppermute x3, starting transfers between devices, per_device_body(): lax.ppermute(own_piece, 'x', [(i, (i + s) % 4) for i in range(4)])  9.87 us
    reduce_or x1, other arithmetic, per_device_body(): mask = jnp.any(used[:, :, None] == frequency[None, None, :], axis=1)  6.23 us
    pallas_call x1, Pallas kernels, product(): pl.pallas_call(product_kernel, grid_spec=pltpu.PrefetchScalarGridSpec(num...  5.45 us
  transfers between devices with their start and end apart: 7, of which 4 were waited for; matrix products, arithmetic and copies ran while one was open for 14% of the time, Pallas kernels for 0%

commit v1 on v0

--- a/solution.py
+++ b/solution.py
@@ -26,6 +26,53 @@
     count = lax.axis_size(axis)
     copies = jnp.broadcast_to(value[None], (count, *value.shape))
     return lax.all_to_all(copies, axis, 0, 0)
+
+
+def gathered_over_y(value):
+    me = lax.axis_index("y")
+    even = (me & 1) == 0
+    blocks = jnp.zeros((4, 2, *value.shape), value.dtype)
+
+    def put(blocks, pair, at):
+        return lax.dynamic_update_slice(blocks, pair[None], (at, 0, 0, 0))
+
+    got = lax.ppermute(value, "y", [(i, i ^ 1) for i in range(8)])
+    pair = jnp.where(even, jnp.stack([value, got]), jnp.stack([got, value]))
+    own = me >> 1
+    blocks = put(blocks, pair, own)
+    links = [(i, (i - 1) % 8 if i % 2 == 0 else (i + 1) % 8) for i in range(8)]
+    got_pair = lax.ppermute(pair, "y", links)
+    blocks = put(blocks, got_pair, (own + jnp.where(even, 3, 1)) & 3)
+    links = [(i, (i + 3) % 8 if i % 2 == 0 else (i - 3) % 8) for i in range(8)]
+    got_four = lax.ppermute(jnp.stack([pair, got_pair]), "y", links)
+    far = ((me + jnp.where(even, 3, 5)) & 7) >> 1
+    blocks = put(blocks, got_four[0], far)
+    blocks = put(blocks, got_four[1], (far + jnp.where(even, 1, 3)) & 3)
+    return blocks.reshape(8, *value.shape)
+
+
+def mask_kernel(index_ref, count_ref, mask_ref):
+    slots, blocks = index_ref.shape
+    length = mask_ref.shape[1]
+    slot = lax.broadcasted_iota(jnp.int32, (slots, blocks), 0)
+    used = jnp.where(slot < count_ref[...], index_ref[...], -1)
+    frequency = lax.broadcasted_iota(jnp.int32, (length, blocks), 0)
+    found = used[0:1] == frequency
+    for j in range(1, slots):
+        found = found | (used[j : j + 1] == frequency)
+    mask_ref[...] = jnp.zeros_like(mask_ref)
+    mask_ref[:blocks] = jnp.where(found, 1.0, 0.0).astype(jnp.float32).T
+
+
+def band_mask(index, count, rows, length):
+    slots, blocks = index.shape
+    return pl.pallas_call(
+        mask_kernel,
+        out_shape=jax.ShapeDtypeStruct((rows, length), jnp.float32),
+        cost_estimate=pl.CostEstimate(
+            flops=2 * slots * blocks * length, bytes_accessed=4 * rows * length, transcendentals=0
+        ),
+    )(index, count)
 
 
 def product_kernel(order_ref, *refs):
@@ -108,7 +155,7 @@
 
     window_grad = gathered(out_grad[:, :window], FSDP).reshape(worker_rows, window)
     weight = lax.all_gather(down_weight, DP)
-    own_piece = gathered(out_grad, "y")
+    own_piece = gathered_over_y(out_grad)
     shifts = (0, 1, 3, 2)
     order = (lax.axis_index("x") + 4 - jnp.array(shifts, jnp.int32)) & 3
     pieces = [own_piece]
@@ -120,31 +167,27 @@
         jnp.bfloat16
     )
     grad_scale = 1.0 / math.sqrt(worker_rows)
-    worker_grad = (
-        lax.dot_general(
-            hidden, window_grad, (((0,), (0,)), ((), ())), preferred_element_type=jnp.float32
-        )
-        * grad_scale
-    )
-    slot_list = band_index[0]
-    slot_ids = jnp.arange(slot_list.shape[1], dtype=jnp.int32)
-    used = jnp.where(slot_ids[None, :] < band_count[0][:, None], slot_list, -1)
-    frequency = jnp.arange(length, dtype=jnp.int32)
-    mask = jnp.any(used[:, :, None] == frequency[None, None, :], axis=1)
+    worker_grad = grad_scale * lax.dot_general(
+        hidden, window_grad, (((0,), (0,)), ((), ())), preferred_element_type=jnp.float32
+    )
+    share = -(-block_count // workers)
+    share = -(-share // 8) * 8
+    rows = share * workers
+    mask = band_mask(band_index[0].T, band_count, rows, length)
 
     cosine_table = cosine_matrix(length)
     mixed = momentum_decay * momentum[0] + worker_grad
-    spectrum = jnp.dot(mixed, cosine_table.T, precision=lax.Precision.HIGHEST)
-    sent = jnp.where(mask, spectrum, 0.0)
-    new_momentum = mixed - jnp.dot(sent, cosine_table, precision=lax.Precision.HIGHEST)
-
-    share = -(-block_count // workers)
-    share = -(-share // 8) * 8
-    padded = jnp.pad(sent, ((0, share * workers - block_count), (0, 0)))
-    parts = lax.all_to_all(padded.reshape(workers, share, length), DP, 0, 0)
+    spread = jnp.pad(mixed, ((0, rows - block_count), (0, 0)))
+    spectrum = jnp.dot(spread, cosine_table.T, precision=lax.Precision.HIGHEST)
+    sent = jnp.where(mask > 0.0, spectrum, 0.0)
+    new_momentum = mixed - jnp.dot(
+        sent[:block_count], cosine_table, precision=lax.Precision.HIGHEST
+    )
+
+    parts = lax.all_to_all(sent.reshape(workers, share, length), DP, 0, 0)
     averaged = parts.sum(0) / workers
     own_update = jnp.dot(averaged, cosine_table, precision=lax.Precision.HIGHEST)
-    update = gathered(own_update, DP).reshape(workers * share, length)[:block_count]
+    update = gathered(own_update, DP).reshape(rows, length)[:block_count]
 
     gate_grad, up_grad = product(order, pieces, weight, gate_pre.T, up_pre.T)
     return (gate_grad.T, up_grad.T, new_momentum[None], update)

time: 137 us -> 122 us (0.89); the launches traced: 135 us -> 121 us
  blocking collectives: 33.4 us -> 0 us
  starting transfers between devices: 28.6 us -> 48.8 us
  other arithmetic: 7.72 us -> 2.51 us
  Pallas kernels: 5.45 us -> 9.22 us
  matrix products: 6.65 us -> 8.42 us
    all_to_all x1 -> x0, blocking collectives: 33.4 us -> none  [per_device_body(): parts = lax.all_to_all(padded.reshape(workers, share, length), DP, 0, 0)]
    all_to_all x3 -> x2, waiting for transfers between devices: 23.2 us -> 3.02 us  [gathered(): return lax.all_to_all(copies, axis, 0, 0)]
    all_to_all x0 -> x1, waiting for transfers between devices: none -> 17.2 us  [per_device_body(): parts = lax.all_to_all(sent.reshape(workers, share, length), DP, 0, 0)]
    all_to_all x0 -> x1, starting transfers between devices: none -> 13.4 us  [per_device_body(): parts = lax.all_to_all(sent.reshape(workers, share, length), DP, 0, 0)]
    ppermute x0 -> x3, starting transfers between devices: none -> 13.4 us  [the longest x1 4.94 us: gathered_over_y(): got_four = lax.ppermute(jnp.stack([pair, got_pair]), 'y', links)]
    all_to_all x3 -> x2, starting transfers between devices: 18.7 us -> 12.2 us  [gathered(): return lax.all_to_all(copies, axis, 0, 0)]
    reduce_or x1 -> x0, other arithmetic: 6.23 us -> none  [per_device_body(): mask = jnp.any(used[:, :, None] == frequency[None, None, :], axis=1)]
    pallas_call x0 -> x1, Pallas kernels: none -> 3.78 us  [band_mask(): pl.pallas_call(mask_kernel, out_shape=jax.ShapeDtypeStruct((rows, length)...]
  transfers between devices with their start and end apart: 7 -> 10, of which waited for: 4 -> 5; matrix products, arithmetic and copies ran while one was open for 14% -> 12% of each run, Pallas kernels for 0% -> 3%
where the time goes in v1:
time: 122 us; the launch traced here: 121 us
  starting transfers between devices  48.8 us (40%)
  waiting for transfers between devices  34.1 us (28%)
  between operations  14.2 us (12%)
  Pallas kernels  9.22 us (8%)
  matrix products  8.42 us (7%)
  local copies, waits for them, and re-layouts  3.91 us (3%)
  other arithmetic  2.51 us (2%)
    all_to_all x1, waiting for transfers between devices, per_device_body(): parts = lax.all_to_all(sent.reshape(workers, share, length), DP, 0, 0)  17.2 us
    all_to_all x1, starting transfers between devices, per_device_body(): parts = lax.all_to_all(sent.reshape(workers, share, length), DP, 0, 0)  13.4 us
    all_to_all x2, starting transfers between devices, gathered(): return lax.all_to_all(copies, axis, 0, 0)  12.2 us
    ppermute x3, waiting for transfers between devices, per_device_body(): lax.ppermute(own_piece, 'x', [(i, (i + s) % 4) for i in range(4)])  11.7 us
    ppermute x3, starting transfers between devices, per_device_body(): lax.ppermute(own_piece, 'x', [(i, (i + s) % 4) for i in range(4)])  9.71 us
    pallas_call x1, Pallas kernels, product(): pl.pallas_call(product_kernel, grid_spec=pltpu.PrefetchScalarGridSpec(num...  5.44 us
    ppermute x1, starting transfers between devices, gathered_over_y(): got_four = lax.ppermute(jnp.stack([pair, got_pair]), 'y', links)  4.94 us
    ppermute x1, starting transfers between devices, gathered_over_y(): got_pair = lax.ppermute(pair, 'y', links)  4.42 us
  transfers between devices with their start and end apart: 10, of which 5 were waited for; matrix products, arithmetic and copies ran while one was open for 12% of the time, Pallas kernels for 3%

profile of v1, /device:TPU:1, one launch (start us, length us, event | category | flops | bytes accessed | tf_op | source)
XLA Modules:
  0.0 121.2 jit_solution(4616764131164072098)
XLA Ops:
  7.9 4.0 %collective-permute-start = (bf16[8,4096]{1,0:T(8,128)(2,1)}, bf16[8,4096]{1,0:T(8,128)(2,1)S(1)}, u32[]{:S(2)}, u32[]{:S(2)}) collective-permute-start(bf16[8,4096]{1,0:T(8,128)(2,1)} %param.8), channel_id=1, source_target_pairs={{0,4},{4,0},{8,12},{12,8},{16,20},{20,16},{24,28},{28,24},{1,5},{5... | collective-permute-start | bytes 196616 | tf_op jit(solution)/shard_map/ppermute | solution.py:39
  13.3 8.8 %all-to-all-start = ((bf16[32,8,256]{2,1,0:T(8,128)(2,1)}), bf16[32,8,256]{2,1,0:T(8,128)(2,1)S(1)}, u32[]{:S(2)}, u32[]{:S(2)}) async-start(bf16[32,8,256]{2,1,0:T(8,128)(2,1)} %broadcast_in_dim.36), calls=%async_computation | async-start | bytes 262144 | tf_op jit(solution)/shard_map/all_to_all | solution.py:28
  22.1 3.8 %shard_map.112 = f32[512,256]{1,0:T(8,128)} custom-call(s32[32,464]{1,0:T(8,128)} %bitcast.37, s32[1,464]{1,0:T(1,128)} %count_ref.1), custom_call_target="tpu_custom_call" | custom-call | flops 7602176 | bytes 524288 | tf_op jit(solution)/shard_map/pallas_call | solution.py:69
  25.9 0.9 maximum_select_fusion.1
  26.9 4.4 %collective-permute-start.1 = (bf16[2,8,4096]{2,1,0:T(8,128)(2,1)S(1)}, bf16[2,8,4096]{2,1,0:T(8,128)(2,1)S(1)}, u32[]{:S(2)}, u32[]{:S(2)}) collective-permute-start(bf16[2,8,4096]{2,1,0:T(8,128)(2,1)S(1)} %maximum_select_fusion.1), channel_id=1, source_target_pairs={{0,28},{4,8},{8,4},{12,16},{16,12},{20,24},{24,20},{28,0},{1,29},{... | collective-permute-start | bytes 393224 | tf_op jit(solution)/shard_map/ppermute | solution.py:44
  31.3 1.0 constant_dynamic-update-slice_fusion.1
  32.3 1.5 %collective-permute-done.1 = bf16[2,8,4096]{2,1,0:T(8,128)(2,1)S(1)} collective-permute-done((bf16[2,8,4096]{2,1,0:T(8,128)(2,1)S(1)}, bf16[2,8,4096]{2,1,0:T(8,128)(2,1)S(1)}, u32[]{:S(2)}, u32[]{:S(2)}) %collective-permute-start.1) | collective-permute-done | bytes 131104 | tf_op jit(solution)/shard_map/ppermute | solution.py:44
  33.8 4.9 %collective-permute-start.2 = (bf16[2,2,8,4096]{3,2,1,0:T(8,128)(2,1)S(1)}, bf16[2,2,8,4096]{3,2,1,0:T(8,128)(2,1)S(1)}, u32[]{:S(2)}, u32[]{:S(2)}) collective-permute-start(bf16[2,2,8,4096]{3,2,1,0:T(8,128)(2,1)S(1)} %pad_maximum_fusion), channel_id=1, source_target_pairs={{0,12},{4,24},{8,20},{12,0},{16,28},{20,8},{24,4},{28,16},{1,13},{... | collective-permute-start | bytes 786440 | tf_op jit(solution)/shard_map/ppermute | solution.py:47
  38.8 1.5 %fusion = f32[464,256]{1,0:T(8,128)S(1)} fusion(f32[1,464,256]{2,1,0:T(8,128)} %param.12, bf16[256,464]{0,1:T(8,128)(2,1)} %param.10, bf16[256,464]{0,1:T(8,128)(2,1)} %param.9, bf16[32,8,256]{2,1,0:T(8,128)(2,1)S(1)} %all-to-all-done), kind=kOutput, calls=%fused_computation.2 | convolution fusion | flops 62124032 | bytes 1556480 | tf_op jit(solution)/shard_map/dot_general | solution.py:170
  40.3 2.4 %convolution_select_fusion = f32[512,256]{1,0:T(8,128)} fusion(f32[464,256]{1,0:T(8,128)S(1)} %fusion, f32[512,256]{1,0:T(8,128)S(1)} %copy-done.1, f32[256]{0:T(256)S(1)} %get-tuple-element.10, f32[256]{0:T(256)S(1)} %iota_convert_fusion, f32[256]{0:T(256)S(1)} %get-tuple-element.11), kind=kOutput, calls=%fused_computation | convolution fusion | flops 403111936 | bytes 1526784 | tf_op jit(solution)/shard_map/dot_general | solution.py:181
  42.7 13.4 %all-to-all-start.1 = ((f32[16,32,256]{2,1,0:T(8,128)}), f32[16,32,256]{2,1,0:T(8,128)S(1)}, u32[]{:S(2)}, u32[]{:S(2)}) async-start(f32[16,32,256]{2,1,0:T(8,128)} %bitcast.16), calls=%async_computation.1 | async-start | bytes 1048576 | tf_op jit(solution)/shard_map/all_to_all | solution.py:187
  56.2 17.2 %all-to-all-done.1 = f32[16,32,256]{2,1,0:T(8,128)S(1)} async-done(((f32[16,32,256]{2,1,0:T(8,128)}), f32[16,32,256]{2,1,0:T(8,128)S(1)}, u32[]{:S(2)}, u32[]{:S(2)}) %all-to-all-start.1) | async-done | bytes 524320 | tf_op jit(solution)/shard_map/all_to_all | solution.py:187
  73.4 1.2 fusion.9
  74.6 0.9 broadcast_in_dim.40
  75.5 3.5 %all-to-all-start.2 = ((f32[16,32,256]{2,1,0:T(8,128)}), f32[16,32,256]{2,1,0:T(8,128)S(1)}, u32[]{:S(2)}, u32[]{:S(2)}) async-start(f32[16,32,256]{2,1,0:T(8,128)} %broadcast_in_dim.40), calls=%async_computation.2 | async-start | bytes 1048576 | tf_op jit(solution)/shard_map/all_to_all | solution.py:28
  79.0 2.9 %collective-permute-start.3 = (bf16[8,8,4096]{2,1,0:T(8,128)(2,1)S(1)}, bf16[8,8,4096]{2,1,0:T(8,128)(2,1)S(1)}, u32[]{:S(2)}, u32[]{:S(2)}) collective-permute-start(bf16[8,8,4096]{2,1,0:T(8,128)(2,1)S(1)} %bitcast.25), channel_id=1, source_target_pairs={{0,1},{1,2},{2,3},{3,0},{4,5},{5,6},{6,7},{7,4},{8,9},{9,10},{10,1... | collective-permute-start | bytes 1572872 | tf_op jit(solution)/shard_map/ppermute | solution.py:163
  81.9 3.6 %collective-permute-start.4 = (bf16[8,8,4096]{2,1,0:T(8,128)(2,1)S(1)}, bf16[8,8,4096]{2,1,0:T(8,128)(2,1)S(1)}, u32[]{:S(2)}, u32[]{:S(2)}) collective-permute-start(bf16[8,8,4096]{2,1,0:T(8,128)(2,1)S(1)} %bitcast.26), channel_id=1, source_target_pairs={{0,3},{1,0},{2,1},{3,2},{4,7},{5,4},{6,5},{7,6},{8,11},{9,8},{10,9... | collective-permute-start | bytes 1572872 | tf_op jit(solution)/shard_map/ppermute | solution.py:163
  85.5 3.2 %collective-permute-start.5 = (bf16[8,8,4096]{2,1,0:T(8,128)(2,1)S(1)}, bf16[8,8,4096]{2,1,0:T(8,128)(2,1)S(1)}, u32[]{:S(2)}, u32[]{:S(2)}) collective-permute-start(bf16[8,8,4096]{2,1,0:T(8,128)(2,1)S(1)} %bitcast.27), channel_id=1, source_target_pairs={{0,2},{1,3},{2,0},{3,1},{4,6},{5,7},{6,4},{7,5},{8,10},{9,11},{10,... | collective-permute-start | bytes 1572872 | tf_op jit(solution)/shard_map/ppermute | solution.py:163
  89.3 3.3 %fusion.1 = f32[1,464,256]{2,1,0:T(8,128)} fusion(f32[464,256]{1,0:T(8,128)S(1)} %fusion, f32[512,256]{1,0:T(8,128)} %convolution_select_fusion, f32[256]{0:T(256)S(1)} %get-tuple-element.10, f32[256]{0:T(256)S(1)} %iota_convert_fusion, f32[256]{0:T(256)S(1)} %get-tuple-element.11), kind=kOutput, calls=%fused_computation.4 | convolution fusion | flops 365219840 | bytes 1428480 | tf_op jit(solution)/shard_map/dot_general | solution.py:183
  92.6 3.0 %all-to-all-done.2 = f32[16,32,256]{2,1,0:T(8,128)S(1)} async-done(((f32[16,32,256]{2,1,0:T(8,128)}), f32[16,32,256]{2,1,0:T(8,128)S(1)}, u32[]{:S(2)}, u32[]{:S(2)}) %all-to-all-start.2) | async-done | bytes 524320 | tf_op jit(solution)/shard_map/all_to_all | solution.py:28
  95.6 0.8 slice.23
  96.4 1.0 collective-permute-done.4.refs_2_
  97.4 10.7 %collective-permute-done.5.refs_3_ = bf16[8,8,4096]{2,1,0:T(8,128)(2,1)S(1)} collective-permute-done((bf16[8,8,4096]{2,1,0:T(8,128)(2,1)S(1)}, bf16[8,8,4096]{2,1,0:T(8,128)(2,1)S(1)}, u32[]{:S(2)}, u32[]{:S(2)}) %collective-permute-start.5) | collective-permute-done | bytes 524320 | tf_op jit(solution)/shard_map/ppermute | solution.py:163
  108.9 5.4 %shard_map.111 = (bf16[464,256]{1,0:T(8,128)(2,1)}, bf16[464,256]{1,0:T(8,128)(2,1)}) custom-call(s32[4]{0:T(128)} %add_and_fusion.order_ref, bf16[8,8,4096]{2,1,0:T(8,128)(2,1)} %bitcast.28, bf16[8,8,4096]{2,1,0:T(8,128)(2,1)} %copy-done.2, bf16[8,8,4096]{2,1,0:T(8,128)(2,1)} %copy-done.3, bf16[8,8,4096]{2,1,0:T(8,128)(2,1)} %copy-done.4, ...), custom_call_target="tpu_custom_call" | custom-call | flops 973078528 | bytes 6848512 | tf_op jit(solution)/shard_map/pallas_call | solution.py:127
  (30 shorter events, 3.6 us)
Async XLA Ops:
  7.2 101.0 %all-gather.3.cloned.1.call-start = ((), (), s32[]{:S(2)}) async-start(), calls=%async_computation.3 | async-start | bytes 4038656 | tf_op jit(solution)/shard_map/all_gather | solution.py:157
  7.9 18.0 %collective-permute-start = (bf16[8,4096]{1,0:T(8,128)(2,1)}, bf16[8,4096]{1,0:T(8,128)(2,1)S(1)}, u32[]{:S(2)}, u32[]{:S(2)}) collective-permute-start(bf16[8,4096]{1,0:T(8,128)(2,1)} %param.8), channel_id=1, source_target_pairs={{0,4},{4,0},{8,12},{12,8},{16,20},{20,16},{24,28},{28,24},{1,5},{5... | collective-permute-start | bytes 196616 | tf_op jit(solution)/shard_map/ppermute | solution.py:39
  13.3 25.5 %all-to-all-start = ((bf16[32,8,256]{2,1,0:T(8,128)(2,1)}), bf16[32,8,256]{2,1,0:T(8,128)(2,1)S(1)}, u32[]{:S(2)}, u32[]{:S(2)}) async-start(bf16[32,8,256]{2,1,0:T(8,128)(2,1)} %broadcast_in_dim.36), calls=%async_computation | async-start | bytes 262144 | tf_op jit(solution)/shard_map/all_to_all | solution.py:28
  25.9 14.4 %copy-start.1 = (f32[512,256]{1,0:T(8,128)S(1)}, f32[512,256]{1,0:T(8,128)}, u32[]{:S(2)}) copy-start(f32[512,256]{1,0:T(8,128)} %shard_map.112) | copy-start | bytes 1572868
  26.9 6.9 %collective-permute-start.1 = (bf16[2,8,4096]{2,1,0:T(8,128)(2,1)S(1)}, bf16[2,8,4096]{2,1,0:T(8,128)(2,1)S(1)}, u32[]{:S(2)}, u32[]{:S(2)}) collective-permute-start(bf16[2,8,4096]{2,1,0:T(8,128)(2,1)S(1)} %maximum_select_fusion.1), channel_id=1, source_target_pairs={{0,28},{4,8},{8,4},{12,16},{16,12},{20,24},{24,20},{28,0},{1,29},{... | collective-permute-start | bytes 393224 | tf_op jit(solution)/shard_map/ppermute | solution.py:44
  33.8 54.9 %copy-start.5 = (s32[4]{0:T(128)S(1)}, s32[4]{0:T(128)}, u32[]{:S(2)}) copy-start(s32[4]{0:T(128)} %constant.59) | copy-start | bytes 52
  33.8 22.3 %collective-permute-start.2 = (bf16[2,2,8,4096]{3,2,1,0:T(8,128)(2,1)S(1)}, bf16[2,2,8,4096]{3,2,1,0:T(8,128)(2,1)S(1)}, u32[]{:S(2)}, u32[]{:S(2)}) collective-permute-start(bf16[2,2,8,4096]{3,2,1,0:T(8,128)(2,1)S(1)} %pad_maximum_fusion), channel_id=1, source_target_pairs={{0,12},{4,24},{8,20},{12,0},{16,28},{20,8},{24,4},{28,16},{1,13},{... | collective-permute-start | bytes 786440 | tf_op jit(solution)/shard_map/ppermute | solution.py:47
  42.7 30.7 %all-to-all-start.1 = ((f32[16,32,256]{2,1,0:T(8,128)}), f32[16,32,256]{2,1,0:T(8,128)S(1)}, u32[]{:S(2)}, u32[]{:S(2)}) async-start(f32[16,32,256]{2,1,0:T(8,128)} %bitcast.16), calls=%async_computation.1 | async-start | bytes 1048576 | tf_op jit(solution)/shard_map/all_to_all | solution.py:187
  75.5 20.1 %all-to-all-start.2 = ((f32[16,32,256]{2,1,0:T(8,128)}), f32[16,32,256]{2,1,0:T(8,128)S(1)}, u32[]{:S(2)}, u32[]{:S(2)}) async-start(f32[16,32,256]{2,1,0:T(8,128)} %broadcast_in_dim.40), calls=%async_computation.2 | async-start | bytes 1048576 | tf_op jit(solution)/shard_map/all_to_all | solution.py:28
  79.0 29.1 %copy-start = (bf16[4,2,8,4096]{3,2,1,0:T(8,128)(2,1)}, bf16[4,2,8,4096]{3,2,1,0:T(8,128)(2,1)S(1)}, u32[]{:S(2)}) copy-start(bf16[4,2,8,4096]{3,2,1,0:T(8,128)(2,1)S(1)} %slice_dynamic-update-slice_fusion) | copy-start | bytes 1572868
  79.0 17.4 %collective-permute-start.3 = (bf16[8,8,4096]{2,1,0:T(8,128)(2,1)S(1)}, bf16[8,8,4096]{2,1,0:T(8,128)(2,1)S(1)}, u32[]{:S(2)}, u32[]{:S(2)}) collective-permute-start(bf16[8,8,4096]{2,1,0:T(8,128)(2,1)S(1)} %bitcast.25), channel_id=1, source_target_pairs={{0,1},{1,2},{2,3},{3,0},{4,5},{5,6},{6,7},{7,4},{8,9},{9,10},{10,1... | collective-permute-start | bytes 1572872 | tf_op jit(solution)/shard_map/ppermute | solution.py:163
  81.9 15.5 %collective-permute-start.4 = (bf16[8,8,4096]{2,1,0:T(8,128)(2,1)S(1)}, bf16[8,8,4096]{2,1,0:T(8,128)(2,1)S(1)}, u32[]{:S(2)}, u32[]{:S(2)}) collective-permute-start(bf16[8,8,4096]{2,1,0:T(8,128)(2,1)S(1)} %bitcast.26), channel_id=1, source_target_pairs={{0,3},{1,0},{2,1},{3,2},{4,7},{5,4},{6,5},{7,6},{8,11},{9,8},{10,9... | collective-permute-start | bytes 1572872 | tf_op jit(solution)/shard_map/ppermute | solution.py:163
  85.5 22.6 %collective-permute-start.5 = (bf16[8,8,4096]{2,1,0:T(8,128)(2,1)S(1)}, bf16[8,8,4096]{2,1,0:T(8,128)(2,1)S(1)}, u32[]{:S(2)}, u32[]{:S(2)}) collective-permute-start(bf16[8,8,4096]{2,1,0:T(8,128)(2,1)S(1)} %bitcast.27), channel_id=1, source_target_pairs={{0,2},{1,3},{2,0},{3,1},{4,6},{5,7},{6,4},{7,5},{8,10},{9,11},{10,... | collective-permute-start | bytes 1572872 | tf_op jit(solution)/shard_map/ppermute | solution.py:163
  96.4 11.7 %copy-start.2 = (bf16[8,8,4096]{2,1,0:T(8,128)(2,1)}, bf16[8,8,4096]{2,1,0:T(8,128)(2,1)S(1)}, u32[]{:S(2)}) copy-start(bf16[8,8,4096]{2,1,0:T(8,128)(2,1)S(1)} %collective-permute-done.3.refs_1_) | copy-start | bytes 1572868
  97.4 10.7 %copy-start.3 = (bf16[8,8,4096]{2,1,0:T(8,128)(2,1)}, bf16[8,8,4096]{2,1,0:T(8,128)(2,1)S(1)}, u32[]{:S(2)}) copy-start(bf16[8,8,4096]{2,1,0:T(8,128)(2,1)S(1)} %collective-permute-done.4.refs_2_) | copy-start | bytes 1572868
  108.1 0.8 copy-start.4
Sparse Core Ops, SparseCore 0:
  10.1 50.7 all-gather.2

commit v2 on v1

--- a/solution.py
+++ b/solution.py
@@ -54,14 +54,18 @@
 def mask_kernel(index_ref, count_ref, mask_ref):
     slots, blocks = index_ref.shape
     length = mask_ref.shape[1]
+    index = index_ref[...]
     slot = lax.broadcasted_iota(jnp.int32, (slots, blocks), 0)
-    used = jnp.where(slot < count_ref[...], index_ref[...], -1)
-    frequency = lax.broadcasted_iota(jnp.int32, (length, blocks), 0)
-    found = used[0:1] == frequency
-    for j in range(1, slots):
-        found = found | (used[j : j + 1] == frequency)
+    bit = jnp.where(slot < count_ref[...], lax.shift_left(jnp.ones_like(index), index & 31), 0)
+    word = lax.shift_right_logical(index, 5)
+    place = lax.broadcasted_iota(jnp.int32, (32, blocks), 0)
+    parts = []
+    for w in range(length // 32):
+        value = jnp.sum(jnp.where(word == w, bit, 0), axis=0, keepdims=True)
+        ones = lax.shift_right_logical(jnp.broadcast_to(value, place.shape), place) & 1
+        parts.append(ones.astype(jnp.float32))
     mask_ref[...] = jnp.zeros_like(mask_ref)
-    mask_ref[:blocks] = jnp.where(found, 1.0, 0.0).astype(jnp.float32).T
+    mask_ref[:blocks] = jnp.concatenate(parts, axis=0).T
 
 
 def band_mask(index, count, rows, length):

time: 122 us -> 120 us (0.984)
  Pallas kernels: 9.22 us -> 7.29 us
    pallas_call x1, Pallas kernels: 3.78 us -> 1.85 us  [band_mask(): pl.pallas_call(mask_kernel, out_shape=jax.ShapeDtypeStruct((rows, length)...]
  transfers between devices with their start and end apart: 10 -> 10, of which waited for: 5 -> 5; matrix products, arithmetic and copies ran while one was open for 12% -> 12% of each run, Pallas kernels for 3% -> 2%
where the time goes in v2:
time: 120 us; the launch traced here: 118 us
  starting transfers between devices  49.1 us (41%)
  waiting for transfers between devices  33 us (28%)
  between operations  14.2 us (12%)
  matrix products  8.42 us (7%)
  Pallas kernels  7.29 us (6%)
  local copies, waits for them, and re-layouts  3.91 us (3%)
  other arithmetic  2.51 us (2%)
    all_to_all x1, waiting for transfers between devices, per_device_body(): parts = lax.all_to_all(sent.reshape(workers, share, length), DP, 0, 0)  16.3 us
    all_to_all x1, starting transfers between devices, per_device_body(): parts = lax.all_to_all(sent.reshape(workers, share, length), DP, 0, 0)  13.3 us
    all_to_all x2, starting transfers between devices, gathered(): return lax.all_to_all(copies, axis, 0, 0)  12.9 us
    ppermute x3, waiting for transfers between devices, per_device_body(): lax.ppermute(own_piece, 'x', [(i, (i + s) % 4) for i in range(4)])  10.6 us
    ppermute x3, starting transfers between devices, per_device_body(): lax.ppermute(own_piece, 'x', [(i, (i + s) % 4) for i in range(4)])  9.9 us
    pallas_call x1, Pallas kernels, product(): pl.pallas_call(product_kernel, grid_spec=pltpu.PrefetchScalarGridSpec(num...  5.44 us
    ppermute x1, starting transfers between devices, gathered_over_y(): got_four = lax.ppermute(jnp.stack([pair, got_pair]), 'y', links)  4.52 us
    ppermute x1, starting transfers between devices, gathered_over_y(): got_pair = lax.ppermute(pair, 'y', links)  4.42 us
  transfers between devices with their start and end apart: 10, of which 5 were waited for; matrix products, arithmetic and copies ran while one was open for 12% of the time, Pallas kernels for 2%

profile of v2, /device:TPU:1, one launch (start us, length us, event | category | flops | bytes accessed | tf_op | source)
XLA Modules:
  0.0 118.4 jit_solution(6183114821693400475)
XLA Ops:
  7.9 4.0 %collective-permute-start = (bf16[8,4096]{1,0:T(8,128)(2,1)}, bf16[8,4096]{1,0:T(8,128)(2,1)S(1)}, u32[]{:S(2)}, u32[]{:S(2)}) collective-permute-start(bf16[8,4096]{1,0:T(8,128)(2,1)} %param.8), channel_id=1, source_target_pairs={{0,4},{4,0},{8,12},{12,8},{16,20},{20,16},{24,28},{28,24},{1,5},{5... | collective-permute-start | bytes 196616 | tf_op jit(solution)/shard_map/ppermute | solution.py:39
  13.3 8.8 %all-to-all-start = ((bf16[32,8,256]{2,1,0:T(8,128)(2,1)}), bf16[32,8,256]{2,1,0:T(8,128)(2,1)S(1)}, u32[]{:S(2)}, u32[]{:S(2)}) async-start(bf16[32,8,256]{2,1,0:T(8,128)(2,1)} %broadcast_in_dim.36), calls=%async_computation | async-start | bytes 262144 | tf_op jit(solution)/shard_map/all_to_all | solution.py:28
  22.1 1.8 %shard_map.112 = f32[512,256]{1,0:T(8,128)} custom-call(s32[32,464]{1,0:T(8,128)} %bitcast.37, s32[1,464]{1,0:T(1,128)} %count_ref.1), custom_call_target="tpu_custom_call" | custom-call | flops 7602176 | bytes 524288 | tf_op jit(solution)/shard_map/pallas_call | solution.py:73
  24.0 0.9 maximum_select_fusion.1
  24.9 4.4 %collective-permute-start.1 = (bf16[2,8,4096]{2,1,0:T(8,128)(2,1)S(1)}, bf16[2,8,4096]{2,1,0:T(8,128)(2,1)S(1)}, u32[]{:S(2)}, u32[]{:S(2)}) collective-permute-start(bf16[2,8,4096]{2,1,0:T(8,128)(2,1)S(1)} %maximum_select_fusion.1), channel_id=1, source_target_pairs={{0,28},{4,8},{8,4},{12,16},{16,12},{20,24},{24,20},{28,0},{1,29},{... | collective-permute-start | bytes 393224 | tf_op jit(solution)/shard_map/ppermute | solution.py:44
  29.4 1.0 constant_dynamic-update-slice_fusion.1
  30.3 1.9 %collective-permute-done.1 = bf16[2,8,4096]{2,1,0:T(8,128)(2,1)S(1)} collective-permute-done((bf16[2,8,4096]{2,1,0:T(8,128)(2,1)S(1)}, bf16[2,8,4096]{2,1,0:T(8,128)(2,1)S(1)}, u32[]{:S(2)}, u32[]{:S(2)}) %collective-permute-start.1) | collective-permute-done | bytes 131104 | tf_op jit(solution)/shard_map/ppermute | solution.py:44
  32.3 4.5 %collective-permute-start.2 = (bf16[2,2,8,4096]{3,2,1,0:T(8,128)(2,1)S(1)}, bf16[2,2,8,4096]{3,2,1,0:T(8,128)(2,1)S(1)}, u32[]{:S(2)}, u32[]{:S(2)}) collective-permute-start(bf16[2,2,8,4096]{3,2,1,0:T(8,128)(2,1)S(1)} %pad_maximum_fusion), channel_id=1, source_target_pairs={{0,12},{4,24},{8,20},{12,0},{16,28},{20,8},{24,4},{28,16},{1,13},{... | collective-permute-start | bytes 786440 | tf_op jit(solution)/shard_map/ppermute | solution.py:47
  36.8 1.6 %fusion = f32[464,256]{1,0:T(8,128)S(1)} fusion(f32[1,464,256]{2,1,0:T(8,128)} %param.12, bf16[256,464]{0,1:T(8,128)(2,1)} %param.10, bf16[256,464]{0,1:T(8,128)(2,1)} %param.9, bf16[32,8,256]{2,1,0:T(8,128)(2,1)S(1)} %all-to-all-done), kind=kOutput, calls=%fused_computation.2 | convolution fusion | flops 62124032 | bytes 1556480 | tf_op jit(solution)/shard_map/dot_general | solution.py:174
  38.4 2.3 %convolution_select_fusion = f32[512,256]{1,0:T(8,128)} fusion(f32[464,256]{1,0:T(8,128)S(1)} %fusion, f32[512,256]{1,0:T(8,128)S(1)} %copy-done.1, f32[256]{0:T(256)S(1)} %get-tuple-element.10, f32[256]{0:T(256)S(1)} %iota_convert_fusion, f32[256]{0:T(256)S(1)} %get-tuple-element.11), kind=kOutput, calls=%fused_computation | convolution fusion | flops 403111936 | bytes 1526784 | tf_op jit(solution)/shard_map/dot_general | solution.py:185
  40.8 13.3 %all-to-all-start.1 = ((f32[16,32,256]{2,1,0:T(8,128)}), f32[16,32,256]{2,1,0:T(8,128)S(1)}, u32[]{:S(2)}, u32[]{:S(2)}) async-start(f32[16,32,256]{2,1,0:T(8,128)} %bitcast.16), calls=%async_computation.1 | async-start | bytes 1048576 | tf_op jit(solution)/shard_map/all_to_all | solution.py:191
  54.1 16.3 %all-to-all-done.1 = f32[16,32,256]{2,1,0:T(8,128)S(1)} async-done(((f32[16,32,256]{2,1,0:T(8,128)}), f32[16,32,256]{2,1,0:T(8,128)S(1)}, u32[]{:S(2)}, u32[]{:S(2)}) %all-to-all-start.1) | async-done | bytes 524320 | tf_op jit(solution)/shard_map/all_to_all | solution.py:191
  70.5 1.2 %fusion.9 = f32[32,256]{1,0:T(8,128)S(1)} fusion(f32[256]{0:T(256)S(1)} %get-tuple-element.10, f32[256]{0:T(256)S(1)} %iota_convert_fusion, f32[256]{0:T(256)S(1)} %get-tuple-element.11, f32[32,256]{1,0:T(8,128)S(1)} %reduce_sum.9), kind=kOutput, calls=%fused_computation.16 | convolution fusion | flops 25370624 | bytes 68608 | tf_op jit(solution)/shard_map/dot_general | solution.py:193
  71.7 0.9 broadcast_in_dim.40
  72.5 4.1 %all-to-all-start.2 = ((f32[16,32,256]{2,1,0:T(8,128)}), f32[16,32,256]{2,1,0:T(8,128)S(1)}, u32[]{:S(2)}, u32[]{:S(2)}) async-start(f32[16,32,256]{2,1,0:T(8,128)} %broadcast_in_dim.40), calls=%async_computation.2 | async-start | bytes 1048576 | tf_op jit(solution)/shard_map/all_to_all | solution.py:28
  76.7 3.1 %collective-permute-start.3 = (bf16[8,8,4096]{2,1,0:T(8,128)(2,1)S(1)}, bf16[8,8,4096]{2,1,0:T(8,128)(2,1)S(1)}, u32[]{:S(2)}, u32[]{:S(2)}) collective-permute-start(bf16[8,8,4096]{2,1,0:T(8,128)(2,1)S(1)} %bitcast.25), channel_id=1, source_target_pairs={{0,1},{1,2},{2,3},{3,0},{4,5},{5,6},{6,7},{7,4},{8,9},{9,10},{10,1... | collective-permute-start | bytes 1572872 | tf_op jit(solution)/shard_map/ppermute | solution.py:167
  79.8 3.4 %collective-permute-start.4 = (bf16[8,8,4096]{2,1,0:T(8,128)(2,1)S(1)}, bf16[8,8,4096]{2,1,0:T(8,128)(2,1)S(1)}, u32[]{:S(2)}, u32[]{:S(2)}) collective-permute-start(bf16[8,8,4096]{2,1,0:T(8,128)(2,1)S(1)} %bitcast.26), channel_id=1, source_target_pairs={{0,3},{1,0},{2,1},{3,2},{4,7},{5,4},{6,5},{7,6},{8,11},{9,8},{10,9... | collective-permute-start | bytes 1572872 | tf_op jit(solution)/shard_map/ppermute | solution.py:167
  83.2 3.4 %collective-permute-start.5 = (bf16[8,8,4096]{2,1,0:T(8,128)(2,1)S(1)}, bf16[8,8,4096]{2,1,0:T(8,128)(2,1)S(1)}, u32[]{:S(2)}, u32[]{:S(2)}) collective-permute-start(bf16[8,8,4096]{2,1,0:T(8,128)(2,1)S(1)} %bitcast.27), channel_id=1, source_target_pairs={{0,2},{1,3},{2,0},{3,1},{4,6},{5,7},{6,4},{7,5},{8,10},{9,11},{10,... | collective-permute-start | bytes 1572872 | tf_op jit(solution)/shard_map/ppermute | solution.py:167
  87.2 3.3 %fusion.1 = f32[1,464,256]{2,1,0:T(8,128)} fusion(f32[464,256]{1,0:T(8,128)S(1)} %fusion, f32[512,256]{1,0:T(8,128)} %convolution_select_fusion, f32[256]{0:T(256)S(1)} %get-tuple-element.10, f32[256]{0:T(256)S(1)} %iota_convert_fusion, f32[256]{0:T(256)S(1)} %get-tuple-element.11), kind=kOutput, calls=%fused_computation.4 | convolution fusion | flops 365219840 | bytes 1428480 | tf_op jit(solution)/shard_map/dot_general | solution.py:187
  90.5 3.4 %all-to-all-done.2 = f32[16,32,256]{2,1,0:T(8,128)S(1)} async-done(((f32[16,32,256]{2,1,0:T(8,128)}), f32[16,32,256]{2,1,0:T(8,128)S(1)}, u32[]{:S(2)}, u32[]{:S(2)}) %all-to-all-start.2) | async-done | bytes 524320 | tf_op jit(solution)/shard_map/all_to_all | solution.py:28
  93.9 0.8 slice.23
  94.8 10.5 %collective-permute-done.5.refs_3_ = bf16[8,8,4096]{2,1,0:T(8,128)(2,1)S(1)} collective-permute-done((bf16[8,8,4096]{2,1,0:T(8,128)(2,1)S(1)}, bf16[8,8,4096]{2,1,0:T(8,128)(2,1)S(1)}, u32[]{:S(2)}, u32[]{:S(2)}) %collective-permute-start.5) | collective-permute-done | bytes 524320 | tf_op jit(solution)/shard_map/ppermute | solution.py:167
  105.3 0.8 copy-done.4
  106.1 5.4 %shard_map.111 = (bf16[464,256]{1,0:T(8,128)(2,1)}, bf16[464,256]{1,0:T(8,128)(2,1)}) custom-call(s32[4]{0:T(128)} %add_and_fusion.order_ref, bf16[8,8,4096]{2,1,0:T(8,128)(2,1)} %bitcast.28, bf16[8,8,4096]{2,1,0:T(8,128)(2,1)} %copy-done.2, bf16[8,8,4096]{2,1,0:T(8,128)(2,1)} %copy-done.3, bf16[8,8,4096]{2,1,0:T(8,128)(2,1)} %copy-done.4, ...), custom_call_target="tpu_custom_call" | custom-call | flops 973078528 | bytes 6848512 | tf_op jit(solution)/shard_map/pallas_call | solution.py:131
  (30 shorter events, 2.9 us)
Async XLA Ops:
  7.2 98.2 %all-gather.3.cloned.1.call-start = ((), (), s32[]{:S(2)}) async-start(), calls=%async_computation.3 | async-start | bytes 4038656 | tf_op jit(solution)/shard_map/all_gather | solution.py:161
  7.9 16.1 %collective-permute-start = (bf16[8,4096]{1,0:T(8,128)(2,1)}, bf16[8,4096]{1,0:T(8,128)(2,1)S(1)}, u32[]{:S(2)}, u32[]{:S(2)}) collective-permute-start(bf16[8,4096]{1,0:T(8,128)(2,1)} %param.8), channel_id=1, source_target_pairs={{0,4},{4,0},{8,12},{12,8},{16,20},{20,16},{24,28},{28,24},{1,5},{5... | collective-permute-start | bytes 196616 | tf_op jit(solution)/shard_map/ppermute | solution.py:39
  13.3 23.5 %all-to-all-start = ((bf16[32,8,256]{2,1,0:T(8,128)(2,1)}), bf16[32,8,256]{2,1,0:T(8,128)(2,1)S(1)}, u32[]{:S(2)}, u32[]{:S(2)}) async-start(bf16[32,8,256]{2,1,0:T(8,128)(2,1)} %broadcast_in_dim.36), calls=%async_computation | async-start | bytes 262144 | tf_op jit(solution)/shard_map/all_to_all | solution.py:28
  23.9 14.5 %copy-start.1 = (f32[512,256]{1,0:T(8,128)S(1)}, f32[512,256]{1,0:T(8,128)}, u32[]{:S(2)}) copy-start(f32[512,256]{1,0:T(8,128)} %shard_map.112) | copy-start | bytes 1572868
  24.9 7.3 %collective-permute-start.1 = (bf16[2,8,4096]{2,1,0:T(8,128)(2,1)S(1)}, bf16[2,8,4096]{2,1,0:T(8,128)(2,1)S(1)}, u32[]{:S(2)}, u32[]{:S(2)}) collective-permute-start(bf16[2,8,4096]{2,1,0:T(8,128)(2,1)S(1)} %maximum_select_fusion.1), channel_id=1, source_target_pairs={{0,28},{4,8},{8,4},{12,16},{16,12},{20,24},{24,20},{28,0},{1,29},{... | collective-permute-start | bytes 393224 | tf_op jit(solution)/shard_map/ppermute | solution.py:44
  32.3 54.3 %copy-start.5 = (s32[4]{0:T(128)S(1)}, s32[4]{0:T(128)}, u32[]{:S(2)}) copy-start(s32[4]{0:T(128)} %constant.59) | copy-start | bytes 52
  32.3 21.8 %collective-permute-start.2 = (bf16[2,2,8,4096]{3,2,1,0:T(8,128)(2,1)S(1)}, bf16[2,2,8,4096]{3,2,1,0:T(8,128)(2,1)S(1)}, u32[]{:S(2)}, u32[]{:S(2)}) collective-permute-start(bf16[2,2,8,4096]{3,2,1,0:T(8,128)(2,1)S(1)} %pad_maximum_fusion), channel_id=1, source_target_pairs={{0,12},{4,24},{8,20},{12,0},{16,28},{20,8},{24,4},{28,16},{1,13},{... | collective-permute-start | bytes 786440 | tf_op jit(solution)/shard_map/ppermute | solution.py:47
  40.8 29.7 %all-to-all-start.1 = ((f32[16,32,256]{2,1,0:T(8,128)}), f32[16,32,256]{2,1,0:T(8,128)S(1)}, u32[]{:S(2)}, u32[]{:S(2)}) async-start(f32[16,32,256]{2,1,0:T(8,128)} %bitcast.16), calls=%async_computation.1 | async-start | bytes 1048576 | tf_op jit(solution)/shard_map/all_to_all | solution.py:191
  72.5 21.3 %all-to-all-start.2 = ((f32[16,32,256]{2,1,0:T(8,128)}), f32[16,32,256]{2,1,0:T(8,128)S(1)}, u32[]{:S(2)}, u32[]{:S(2)}) async-start(f32[16,32,256]{2,1,0:T(8,128)} %broadcast_in_dim.40), calls=%async_computation.2 | async-start | bytes 1048576 | tf_op jit(solution)/shard_map/all_to_all | solution.py:28
  76.7 28.6 %copy-start = (bf16[4,2,8,4096]{3,2,1,0:T(8,128)(2,1)}, bf16[4,2,8,4096]{3,2,1,0:T(8,128)(2,1)S(1)}, u32[]{:S(2)}) copy-start(bf16[4,2,8,4096]{3,2,1,0:T(8,128)(2,1)S(1)} %slice_dynamic-update-slice_fusion) | copy-start | bytes 1572868
  76.7 18.0 %collective-permute-start.3 = (bf16[8,8,4096]{2,1,0:T(8,128)(2,1)S(1)}, bf16[8,8,4096]{2,1,0:T(8,128)(2,1)S(1)}, u32[]{:S(2)}, u32[]{:S(2)}) collective-permute-start(bf16[8,8,4096]{2,1,0:T(8,128)(2,1)S(1)} %bitcast.25), channel_id=1, source_target_pairs={{0,1},{1,2},{2,3},{3,0},{4,5},{5,6},{6,7},{7,4},{8,9},{9,10},{10,1... | collective-permute-start | bytes 1572872 | tf_op jit(solution)/shard_map/ppermute | solution.py:167
  79.8 15.0 %collective-permute-start.4 = (bf16[8,8,4096]{2,1,0:T(8,128)(2,1)S(1)}, bf16[8,8,4096]{2,1,0:T(8,128)(2,1)S(1)}, u32[]{:S(2)}, u32[]{:S(2)}) collective-permute-start(bf16[8,8,4096]{2,1,0:T(8,128)(2,1)S(1)} %bitcast.26), channel_id=1, source_target_pairs={{0,3},{1,0},{2,1},{3,2},{4,7},{5,4},{6,5},{7,6},{8,11},{9,8},{10,9... | collective-permute-start | bytes 1572872 | tf_op jit(solution)/shard_map/ppermute | solution.py:167
  83.2 22.1 %collective-permute-start.5 = (bf16[8,8,4096]{2,1,0:T(8,128)(2,1)S(1)}, bf16[8,8,4096]{2,1,0:T(8,128)(2,1)S(1)}, u32[]{:S(2)}, u32[]{:S(2)}) collective-permute-start(bf16[8,8,4096]{2,1,0:T(8,128)(2,1)S(1)} %bitcast.27), channel_id=1, source_target_pairs={{0,2},{1,3},{2,0},{3,1},{4,6},{5,7},{6,4},{7,5},{8,10},{9,11},{10,... | collective-permute-start | bytes 1572872 | tf_op jit(solution)/shard_map/ppermute | solution.py:167
  94.7 10.7 %copy-start.2 = (bf16[8,8,4096]{2,1,0:T(8,128)(2,1)}, bf16[8,8,4096]{2,1,0:T(8,128)(2,1)S(1)}, u32[]{:S(2)}) copy-start(bf16[8,8,4096]{2,1,0:T(8,128)(2,1)S(1)} %collective-permute-done.3.refs_1_) | copy-start | bytes 1572868
  94.8 10.5 %copy-start.3 = (bf16[8,8,4096]{2,1,0:T(8,128)(2,1)}, bf16[8,8,4096]{2,1,0:T(8,128)(2,1)S(1)}, u32[]{:S(2)}) copy-start(bf16[8,8,4096]{2,1,0:T(8,128)(2,1)S(1)} %collective-permute-done.4.refs_2_) | copy-start | bytes 1572868
  105.3 0.8 copy-start.4
Sparse Core Ops, SparseCore 0:
  10.1 53.7 all-gather.2

commit v3 on v2

--- a/solution.py
+++ b/solution.py
@@ -2,6 +2,7 @@
 
 import jax
 import jax.numpy as jnp
+import numpy as np
 from jax import lax
 from jax.experimental import pallas as pl
 from jax.experimental.pallas import tpu as pltpu
@@ -12,14 +13,14 @@
 DP = ("z", "core")
 FSDP = ("y", "x")
 momentum_decay = 0.9
+SHIFTS = (0, 1, 3, 2)
 
 
 def cosine_matrix(length):
-    frequency = jnp.arange(length, dtype=jnp.int32).astype(jnp.float32)[:, None]
-    position = jnp.arange(length, dtype=jnp.int32).astype(jnp.float32)[None, :]
-    angles = math.pi * (position + 0.5) * frequency / length
-    row_weight = jnp.where(frequency == 0.0, math.sqrt(1.0 / length), math.sqrt(2.0 / length))
-    return jnp.cos(angles) * row_weight
+    frequency = np.arange(length, dtype=np.float64)[:, None]
+    position = np.arange(length, dtype=np.float64)[None, :]
+    row_weight = np.where(frequency == 0.0, math.sqrt(1.0 / length), math.sqrt(2.0 / length))
+    return (np.cos(math.pi * (position + 0.5) * frequency / length) * row_weight).astype(np.float32)
 
 
 def gathered(value, axis):
@@ -29,26 +30,31 @@
 
 
 def gathered_over_y(value):
-    me = lax.axis_index("y")
-    even = (me & 1) == 0
-    blocks = jnp.zeros((4, 2, *value.shape), value.dtype)
-
-    def put(blocks, pair, at):
-        return lax.dynamic_update_slice(blocks, pair[None], (at, 0, 0, 0))
-
-    got = lax.ppermute(value, "y", [(i, i ^ 1) for i in range(8)])
-    pair = jnp.where(even, jnp.stack([value, got]), jnp.stack([got, value]))
-    own = me >> 1
-    blocks = put(blocks, pair, own)
+    near = lax.ppermute(value, "y", [(i, i ^ 1) for i in range(8)])
+    pair = jnp.stack([value, near])
     links = [(i, (i - 1) % 8 if i % 2 == 0 else (i + 1) % 8) for i in range(8)]
-    got_pair = lax.ppermute(pair, "y", links)
-    blocks = put(blocks, got_pair, (own + jnp.where(even, 3, 1)) & 3)
+    second = lax.ppermute(pair, "y", links)
+    four = jnp.concatenate([pair, second])
     links = [(i, (i + 3) % 8 if i % 2 == 0 else (i - 3) % 8) for i in range(8)]
-    got_four = lax.ppermute(jnp.stack([pair, got_pair]), "y", links)
-    far = ((me + jnp.where(even, 3, 5)) & 7) >> 1
-    blocks = put(blocks, got_four[0], far)
-    blocks = put(blocks, got_four[1], (far + jnp.where(even, 1, 3)) & 3)
-    return blocks.reshape(8, *value.shape)
+    third = lax.ppermute(four, "y", links)
+    return jnp.concatenate([four, third])
+
+
+def arrival_order():
+    def second(y):
+        return (y - 1) % 8 if y % 2 == 0 else (y + 1) % 8
+
+    def third(y):
+        return (y + 3) % 8 if y % 2 == 0 else (y - 3) % 8
+
+    table = []
+    for y in range(8):
+        pairs = [y, second(y), third(y), second(third(y))]
+        blocks = [b for p in pairs for b in (p, p ^ 1)]
+        table += [[(x - s) % 4 for s in SHIFTS] + blocks for x in range(4)]
+    row = lax.axis_index("y") * 4 + lax.axis_index("x")
+    table = jnp.asarray(np.array(table, np.int32))
+    return lax.dynamic_slice(table, (row, 0), (1, table.shape[1]))[0]
 
 
 def mask_kernel(index_ref, count_ref, mask_ref):
@@ -93,7 +99,8 @@
         slope_ref[...] = up_ref[...].astype(jnp.float32) * sigmoid * (1.0 + gate * (1.0 - sigmoid))
 
     for i, piece in enumerate(pieces):
-        rows_ref[:, order_ref[i]] = piece[...]
+        for j in range(piece.shape[0]):
+            rows_ref[order_ref[4 + j], order_ref[i]] = piece[j]
     width = weight_ref.shape[2]
     rows = rows_ref[...].reshape(-1, rows_ref.shape[3])
     total = None
@@ -160,10 +167,9 @@
     window_grad = gathered(out_grad[:, :window], FSDP).reshape(worker_rows, window)
     weight = lax.all_gather(down_weight, DP)
     own_piece = gathered_over_y(out_grad)
-    shifts = (0, 1, 3, 2)
-    order = (lax.axis_index("x") + 4 - jnp.array(shifts, jnp.int32)) & 3
+    order = arrival_order()
     pieces = [own_piece]
-    for s in shifts[1:]:
+    for s in SHIFTS[1:]:
         pieces.append(lax.ppermute(own_piece, "x", [(i, (i + s) % 4) for i in range(4)]))
 
     gate_float = gate_pre.astype(jnp.float32)
@@ -179,18 +185,16 @@
     rows = share * workers
     mask = band_mask(band_index[0].T, band_count, rows, length)
 
-    cosine_table = cosine_matrix(length)
+    cosine_table = jnp.asarray(cosine_matrix(length))
     mixed = momentum_decay * momentum[0] + worker_grad
     spread = jnp.pad(mixed, ((0, rows - block_count), (0, 0)))
-    spectrum = jnp.dot(spread, cosine_table.T, precision=lax.Precision.HIGHEST)
+    spectrum = jnp.dot(spread, cosine_table.T, precision=lax.Precision.HIGH)
     sent = jnp.where(mask > 0.0, spectrum, 0.0)
-    new_momentum = mixed - jnp.dot(
-        sent[:block_count], cosine_table, precision=lax.Precision.HIGHEST
-    )
+    new_momentum = mixed - jnp.dot(sent[:block_count], cosine_table, precision=lax.Precision.HIGH)
 
     parts = lax.all_to_all(sent.reshape(workers, share, length), DP, 0, 0)
     averaged = parts.sum(0) / workers
-    own_update = jnp.dot(averaged, cosine_table, precision=lax.Precision.HIGHEST)
+    own_update = jnp.dot(averaged, cosine_table, precision=lax.Precision.HIGH)
     update = gathered(own_update, DP).reshape(rows, length)[:block_count]
 
     gate_grad, up_grad = product(order, pieces, weight, gate_pre.T, up_pre.T)

time: 120 us -> 115 us (0.958)
  the two profiles are of different devices: /device:TPU:1 before, /device:TPU:6 now
where the time goes in v3:
time: 115 us; the launch traced here: 114 us
  starting transfers between devices  42.8 us (37%)
  waiting for transfers between devices  38.4 us (33%)
  between operations  14.2 us (12%)
  Pallas kernels  7.32 us (6%)
  matrix products  6.17 us (5%)
  local copies, waits for them, and re-layouts  5.22 us (5%)
    all_to_all x2, starting transfers between devices, gathered(): return lax.all_to_all(copies, axis, 0, 0)  15.1 us
    ppermute x3, waiting for transfers between devices, per_device_body(): lax.ppermute(own_piece, 'x', [(i, (i + s) % 4) for i in range(4)])  15 us
    all_to_all x1, starting transfers between devices, per_device_body(): parts = lax.all_to_all(sent.reshape(workers, share, length), DP, 0, 0)  10.4 us
    ppermute x3, starting transfers between devices, per_device_body(): lax.ppermute(own_piece, 'x', [(i, (i + s) % 4) for i in range(4)])  9.07 us
    all_to_all x1, waiting for transfers between devices, per_device_body(): parts = lax.all_to_all(sent.reshape(workers, share, length), DP, 0, 0)  8.84 us
    all_to_all x2, waiting for transfers between devices, gathered(): return lax.all_to_all(copies, axis, 0, 0)  7.08 us
    ppermute x1, waiting for transfers between devices, gathered_over_y(): second = lax.ppermute(pair, 'y', links)  6.79 us
    pallas_call x1, Pallas kernels, product(): pl.pallas_call(product_kernel, grid_spec=pltpu.PrefetchScalarGridSpec(num...  5.46 us
  transfers between devices with their start and end apart: 10, of which 5 were waited for; matrix products, arithmetic and copies ran while one was open for 9% of the time, Pallas kernels for 2%

profile of v3, /device:TPU:6, one launch (start us, length us, event | category | flops | bytes accessed | tf_op | source)
XLA Modules:
  0.0 114.3 jit_solution(1049253856066356092)
XLA Ops:
  7.9 0.7 slice.9
  9.3 10.2 %all-to-all-start = ((bf16[32,8,256]{2,1,0:T(8,128)(2,1)}), bf16[32,8,256]{2,1,0:T(8,128)(2,1)S(1)}, u32[]{:S(2)}, u32[]{:S(2)}) async-start(bf16[32,8,256]{2,1,0:T(8,128)(2,1)} %broadcast_in_dim.8), calls=%async_computation | async-start | bytes 262144 | tf_op jit(solution)/shard_map/all_to_all | solution.py:29
  19.5 3.4 %collective-permute-start = (bf16[8,4096]{1,0:T(8,128)(2,1)}, bf16[8,4096]{1,0:T(8,128)(2,1)S(1)}, u32[]{:S(2)}, u32[]{:S(2)}) collective-permute-start(bf16[8,4096]{1,0:T(8,128)(2,1)} %param.9), channel_id=1, source_target_pairs={{0,4},{4,0},{8,12},{12,8},{16,20},{20,16},{24,28},{28,24},{1,5},{5... | collective-permute-start | bytes 196616 | tf_op jit(solution)/shard_map/ppermute | solution.py:33
  22.9 1.9 %shard_map.121 = f32[512,256]{1,0:T(8,128)} custom-call(s32[32,464]{1,0:T(8,128)} %bitcast.34, s32[1,464]{1,0:T(1,128)} %count_ref.1), custom_call_target="tpu_custom_call" | custom-call | flops 7602176 | bytes 524288 | tf_op jit(solution)/shard_map/pallas_call | solution.py:79
  24.7 3.7 %all-to-all-done = bf16[32,8,256]{2,1,0:T(8,128)(2,1)S(1)} async-done(((bf16[32,8,256]{2,1,0:T(8,128)(2,1)}), bf16[32,8,256]{2,1,0:T(8,128)(2,1)S(1)}, u32[]{:S(2)}, u32[]{:S(2)}) %all-to-all-start) | async-done | bytes 131104 | tf_op jit(solution)/shard_map/all_to_all | solution.py:29
  28.5 1.5 %fusion = f32[464,256]{1,0:T(8,128)S(1)} fusion(f32[1,464,256]{2,1,0:T(8,128)} %param.13, bf16[256,464]{0,1:T(8,128)(2,1)} %param.11, bf16[256,464]{0,1:T(8,128)(2,1)} %param.10, bf16[32,8,256]{2,1,0:T(8,128)(2,1)S(1)} %all-to-all-done), kind=kOutput, calls=%fused_computation.2 | convolution fusion | flops 62124032 | bytes 1556480 | tf_op jit(solution)/shard_map/dot_general | solution.py:180
  30.0 2.3 %convolution_select_fusion = f32[512,256]{1,0:T(8,128)} fusion(f32[256,256]{1,0:T(8,128)S(1)} %copy-done, f32[464,256]{1,0:T(8,128)S(1)} %fusion, f32[512,256]{1,0:T(8,128)} %shard_map.121), kind=kOutput, calls=%fused_computation | convolution fusion | flops 201588736 | bytes 1785856 | tf_op jit(solution)/shard_map/dot_general | solution.py:191
  32.3 10.4 %all-to-all-start.1 = ((f32[16,32,256]{2,1,0:T(8,128)}), f32[16,32,256]{2,1,0:T(8,128)S(1)}, u32[]{:S(2)}, u32[]{:S(2)}) async-start(f32[16,32,256]{2,1,0:T(8,128)} %bitcast.13), calls=%async_computation.1 | async-start | bytes 1048576 | tf_op jit(solution)/shard_map/all_to_all | solution.py:195
  42.8 2.1 %collective-permute-start.1 = (bf16[2,8,4096]{2,1,0:T(8,128)(2,1)S(1)}, bf16[2,8,4096]{2,1,0:T(8,128)(2,1)S(1)}, u32[]{:S(2)}, u32[]{:S(2)}) collective-permute-start(bf16[2,8,4096]{2,1,0:T(8,128)(2,1)S(1)} %pad_maximum_fusion.2), channel_id=1, source_target_pairs={{0,28},{4,8},{8,4},{12,16},{16,12},{20,24},{24,20},{28,0},{1,29},{... | collective-permute-start | bytes 393224 | tf_op jit(solution)/shard_map/ppermute | solution.py:36
  44.9 6.8 %collective-permute-done.1 = bf16[2,8,4096]{2,1,0:T(8,128)(2,1)S(1)} collective-permute-done((bf16[2,8,4096]{2,1,0:T(8,128)(2,1)S(1)}, bf16[2,8,4096]{2,1,0:T(8,128)(2,1)S(1)}, u32[]{:S(2)}, u32[]{:S(2)}) %collective-permute-start.1) | collective-permute-done | bytes 131104 | tf_op jit(solution)/shard_map/ppermute | solution.py:36
  51.7 2.6 %collective-permute-start.2 = (bf16[4,8,4096]{2,1,0:T(8,128)(2,1)S(1)}, bf16[4,8,4096]{2,1,0:T(8,128)(2,1)S(1)}, u32[]{:S(2)}, u32[]{:S(2)}) collective-permute-start(bf16[4,8,4096]{2,1,0:T(8,128)(2,1)S(1)} %pad_maximum_fusion.1), channel_id=1, source_target_pairs={{0,12},{4,24},{8,20},{12,0},{16,28},{20,8},{24,4},{28,16},{1,13},{... | collective-permute-start | bytes 786440 | tf_op jit(solution)/shard_map/ppermute | solution.py:39
  54.3 8.8 %all-to-all-done.1 = f32[16,32,256]{2,1,0:T(8,128)S(1)} async-done(((f32[16,32,256]{2,1,0:T(8,128)}), f32[16,32,256]{2,1,0:T(8,128)S(1)}, u32[]{:S(2)}, u32[]{:S(2)}) %all-to-all-start.1) | async-done | bytes 524320 | tf_op jit(solution)/shard_map/all_to_all | solution.py:195
  63.4 0.9 broadcast_in_dim.10
  64.3 4.9 %all-to-all-start.2 = ((f32[16,32,256]{2,1,0:T(8,128)}), f32[16,32,256]{2,1,0:T(8,128)S(1)}, u32[]{:S(2)}, u32[]{:S(2)}) async-start(f32[16,32,256]{2,1,0:T(8,128)} %broadcast_in_dim.10), calls=%async_computation.2 | async-start | bytes 1048576 | tf_op jit(solution)/shard_map/all_to_all | solution.py:29
  69.3 3.6 %collective-permute-start.3 = (bf16[8,8,4096]{2,1,0:T(8,128)(2,1)S(1)}, bf16[8,8,4096]{2,1,0:T(8,128)(2,1)S(1)}, u32[]{:S(2)}, u32[]{:S(2)}) collective-permute-start(bf16[8,8,4096]{2,1,0:T(8,128)(2,1)S(1)} %pad_maximum_fusion.refs_0_), channel_id=1, source_target_pairs={{0,1},{1,2},{2,3},{3,0},{4,5},{5,6},{6,7},{7,4},{8,9},{9,10},{10,1... | collective-permute-start | bytes 1572872 | tf_op jit(solution)/shard_map/ppermute | solution.py:173
  72.9 2.3 %collective-permute-start.4 = (bf16[8,8,4096]{2,1,0:T(8,128)(2,1)S(1)}, bf16[8,8,4096]{2,1,0:T(8,128)(2,1)S(1)}, u32[]{:S(2)}, u32[]{:S(2)}) collective-permute-start(bf16[8,8,4096]{2,1,0:T(8,128)(2,1)S(1)} %pad_maximum_fusion.refs_0_), channel_id=1, source_target_pairs={{0,3},{1,0},{2,1},{3,2},{4,7},{5,4},{6,5},{7,6},{8,11},{9,8},{10,9... | collective-permute-start | bytes 1572872 | tf_op jit(solution)/shard_map/ppermute | solution.py:173
  75.1 3.2 %collective-permute-start.5 = (bf16[8,8,4096]{2,1,0:T(8,128)(2,1)S(1)}, bf16[8,8,4096]{2,1,0:T(8,128)(2,1)S(1)}, u32[]{:S(2)}, u32[]{:S(2)}) collective-permute-start(bf16[8,8,4096]{2,1,0:T(8,128)(2,1)S(1)} %pad_maximum_fusion.refs_0_), channel_id=1, source_target_pairs={{0,2},{1,3},{2,0},{3,1},{4,6},{5,7},{6,4},{7,5},{8,10},{9,11},{10,... | collective-permute-start | bytes 1572872 | tf_op jit(solution)/shard_map/ppermute | solution.py:173
  78.4 1.2 %dynamic-slice_bitcast_fusion.order_ref = s32[12]{0:T(128)} fusion(s32[32,12]{1,0:T(8,128)} %constant.31.clone, s32[]{:T(128)S(6)} %select_n.7), kind=kLoop, calls=%fused_computation.22 | loop fusion | bytes 100 | tf_op jit(solution)/shard_map/squeeze | solution.py:57
  79.6 2.2 %fusion.1 = f32[1,464,256]{2,1,0:T(8,128)} fusion(f32[464,256]{1,0:T(8,128)S(1)} %fusion, f32[256,256]{1,0:T(8,128)S(1)} %copy-done, f32[512,256]{1,0:T(8,128)} %convolution_select_fusion), kind=kOutput, calls=%fused_computation.4 | convolution fusion | flops 182571008 | bytes 1687552 | tf_op jit(solution)/shard_map/dot_general | solution.py:193
  81.8 3.4 %all-to-all-done.2 = f32[16,32,256]{2,1,0:T(8,128)S(1)} async-done(((f32[16,32,256]{2,1,0:T(8,128)}), f32[16,32,256]{2,1,0:T(8,128)S(1)}, u32[]{:S(2)}, u32[]{:S(2)}) %all-to-all-start.2) | async-done | bytes 524320 | tf_op jit(solution)/shard_map/all_to_all | solution.py:29
  85.1 0.8 slice.13
  86.0 15.0 %collective-permute-done.4.refs_2_ = bf16[8,8,4096]{2,1,0:T(8,128)(2,1)S(1)} collective-permute-done((bf16[8,8,4096]{2,1,0:T(8,128)(2,1)S(1)}, bf16[8,8,4096]{2,1,0:T(8,128)(2,1)S(1)}, u32[]{:S(2)}, u32[]{:S(2)}) %collective-permute-start.4) | collective-permute-done | bytes 524320 | tf_op jit(solution)/shard_map/ppermute | solution.py:173
  101.0 0.7 copy-done.4
  102.0 5.5 %shard_map.120 = (bf16[464,256]{1,0:T(8,128)(2,1)}, bf16[464,256]{1,0:T(8,128)(2,1)}) custom-call(s32[12]{0:T(128)} %dynamic-slice_bitcast_fusion.order_ref, bf16[8,8,4096]{2,1,0:T(8,128)(2,1)} %copy-done.1, bf16[8,8,4096]{2,1,0:T(8,128)(2,1)} %copy-done.3, bf16[8,8,4096]{2,1,0:T(8,128)(2,1)} %copy-done.4, bf16[8,8,4096]{2,1,0:T(8,128)(2,1)} %copy-done.5, ...), custom_call_target="tpu_custom_call" | custom-call | flops 973078528 | bytes 6848512 | tf_op jit(solution)/shard_map/pallas_call | solution.py:138
  (24 shorter events, 2.0 us)
Async XLA Ops:
  7.2 22.8 %copy-start = (f32[256,256]{1,0:T(8,128)S(1)}, f32[256,256]{1,0:T(8,128)}, u32[]{:S(2)}) copy-start(f32[256,256]{1,0:T(8,128)} %constant.32.clone) | copy-start | bytes 786436
  7.2 35.6 %copy-start.2 = (bf16[8,4096]{1,0:T(8,128)(2,1)S(1)}, bf16[8,4096]{1,0:T(8,128)(2,1)}, u32[]{:S(2)}) copy-start(bf16[8,4096]{1,0:T(8,128)(2,1)} %param.9) | copy-start | bytes 196612
  7.2 93.8 %all-gather.3.cloned.1.call-start = ((), (), s32[]{:S(2)}) async-start(), calls=%async_computation.3 | async-start | bytes 4038656 | tf_op jit(solution)/shard_map/all_gather | solution.py:168
  9.3 19.2 %all-to-all-start = ((bf16[32,8,256]{2,1,0:T(8,128)(2,1)}), bf16[32,8,256]{2,1,0:T(8,128)(2,1)S(1)}, u32[]{:S(2)}, u32[]{:S(2)}) async-start(bf16[32,8,256]{2,1,0:T(8,128)(2,1)} %broadcast_in_dim.8), calls=%async_computation | async-start | bytes 262144 | tf_op jit(solution)/shard_map/all_to_all | solution.py:29
  19.5 23.2 %collective-permute-start = (bf16[8,4096]{1,0:T(8,128)(2,1)}, bf16[8,4096]{1,0:T(8,128)(2,1)S(1)}, u32[]{:S(2)}, u32[]{:S(2)}) collective-permute-start(bf16[8,4096]{1,0:T(8,128)(2,1)} %param.9), channel_id=1, source_target_pairs={{0,4},{4,0},{8,12},{12,8},{16,20},{20,16},{24,28},{28,24},{1,5},{5... | collective-permute-start | bytes 196616 | tf_op jit(solution)/shard_map/ppermute | solution.py:33
  32.3 30.9 %all-to-all-start.1 = ((f32[16,32,256]{2,1,0:T(8,128)}), f32[16,32,256]{2,1,0:T(8,128)S(1)}, u32[]{:S(2)}, u32[]{:S(2)}) async-start(f32[16,32,256]{2,1,0:T(8,128)} %bitcast.13), calls=%async_computation.1 | async-start | bytes 1048576 | tf_op jit(solution)/shard_map/all_to_all | solution.py:195
  42.8 8.9 %collective-permute-start.1 = (bf16[2,8,4096]{2,1,0:T(8,128)(2,1)S(1)}, bf16[2,8,4096]{2,1,0:T(8,128)(2,1)S(1)}, u32[]{:S(2)}, u32[]{:S(2)}) collective-permute-start(bf16[2,8,4096]{2,1,0:T(8,128)(2,1)S(1)} %pad_maximum_fusion.2), channel_id=1, source_target_pairs={{0,28},{4,8},{8,4},{12,16},{16,12},{20,24},{24,20},{28,0},{1,29},{... | collective-permute-start | bytes 393224 | tf_op jit(solution)/shard_map/ppermute | solution.py:36
  51.7 17.5 %collective-permute-start.2 = (bf16[4,8,4096]{2,1,0:T(8,128)(2,1)S(1)}, bf16[4,8,4096]{2,1,0:T(8,128)(2,1)S(1)}, u32[]{:S(2)}, u32[]{:S(2)}) collective-permute-start(bf16[4,8,4096]{2,1,0:T(8,128)(2,1)S(1)} %pad_maximum_fusion.1), channel_id=1, source_target_pairs={{0,12},{4,24},{8,20},{12,0},{16,28},{20,8},{24,4},{28,16},{1,13},{... | collective-permute-start | bytes 786440 | tf_op jit(solution)/shard_map/ppermute | solution.py:39
  64.3 20.9 %all-to-all-start.2 = ((f32[16,32,256]{2,1,0:T(8,128)}), f32[16,32,256]{2,1,0:T(8,128)S(1)}, u32[]{:S(2)}, u32[]{:S(2)}) async-start(f32[16,32,256]{2,1,0:T(8,128)} %broadcast_in_dim.10), calls=%async_computation.2 | async-start | bytes 1048576 | tf_op jit(solution)/shard_map/all_to_all | solution.py:29
  69.3 31.7 %copy-start.1 = (bf16[8,8,4096]{2,1,0:T(8,128)(2,1)}, bf16[8,8,4096]{2,1,0:T(8,128)(2,1)S(1)}, u32[]{:S(2)}) copy-start(bf16[8,8,4096]{2,1,0:T(8,128)(2,1)S(1)} %pad_maximum_fusion.refs_0_) | copy-start | bytes 1572868
  69.3 16.7 %collective-permute-start.3 = (bf16[8,8,4096]{2,1,0:T(8,128)(2,1)S(1)}, bf16[8,8,4096]{2,1,0:T(8,128)(2,1)S(1)}, u32[]{:S(2)}, u32[]{:S(2)}) collective-permute-start(bf16[8,8,4096]{2,1,0:T(8,128)(2,1)S(1)} %pad_maximum_fusion.refs_0_), channel_id=1, source_target_pairs={{0,1},{1,2},{2,3},{3,0},{4,5},{5,6},{6,7},{7,4},{8,9},{9,10},{10,1... | collective-permute-start | bytes 1572872 | tf_op jit(solution)/shard_map/ppermute | solution.py:173
  72.9 28.1 %collective-permute-start.4 = (bf16[8,8,4096]{2,1,0:T(8,128)(2,1)S(1)}, bf16[8,8,4096]{2,1,0:T(8,128)(2,1)S(1)}, u32[]{:S(2)}, u32[]{:S(2)}) collective-permute-start(bf16[8,8,4096]{2,1,0:T(8,128)(2,1)S(1)} %pad_maximum_fusion.refs_0_), channel_id=1, source_target_pairs={{0,3},{1,0},{2,1},{3,2},{4,7},{5,4},{6,5},{7,6},{8,11},{9,8},{10,9... | collective-permute-start | bytes 1572872 | tf_op jit(solution)/shard_map/ppermute | solution.py:173
  75.1 25.8 %collective-permute-start.5 = (bf16[8,8,4096]{2,1,0:T(8,128)(2,1)S(1)}, bf16[8,8,4096]{2,1,0:T(8,128)(2,1)S(1)}, u32[]{:S(2)}, u32[]{:S(2)}) collective-permute-start(bf16[8,8,4096]{2,1,0:T(8,128)(2,1)S(1)} %pad_maximum_fusion.refs_0_), channel_id=1, source_target_pairs={{0,2},{1,3},{2,0},{3,1},{4,6},{5,7},{6,4},{7,5},{8,10},{9,11},{10,... | collective-permute-start | bytes 1572872 | tf_op jit(solution)/shard_map/ppermute | solution.py:173
  86.0 15.0 %copy-start.3 = (bf16[8,8,4096]{2,1,0:T(8,128)(2,1)}, bf16[8,8,4096]{2,1,0:T(8,128)(2,1)S(1)}, u32[]{:S(2)}) copy-start(bf16[8,8,4096]{2,1,0:T(8,128)(2,1)S(1)} %collective-permute-done.3.refs_1_) | copy-start | bytes 1572868
  101.0 0.8 copy-start.4
  101.0 1.0 copy-start.5
Sparse Core Ops, SparseCore 0:
  10.1 58.5 all-gather.2

commit v4 on v3

--- a/solution.py
+++ b/solution.py
@@ -83,6 +83,35 @@
             flops=2 * slots * blocks * length, bytes_accessed=4 * rows * length, transcendentals=0
         ),
     )(index, count)
+
+
+def interleave_kernel(core_ref, own_ref, other_ref, out_ref):
+    core = core_ref[0]
+    count, share, _ = own_ref.shape
+    for z in range(count):
+        first = 2 * z * share
+        if first + 2 * share <= out_ref.shape[0]:
+            out_ref[pl.ds(pl.multiple_of(first + core * share, share), share)] = own_ref[z]
+            out_ref[pl.ds(pl.multiple_of(first + (1 - core) * share, share), share)] = other_ref[z]
+        else:
+            left = out_ref.shape[0] - first
+            even = jnp.where(core == 0, own_ref[z], other_ref[z])
+            odd = jnp.where(core == 0, other_ref[z], own_ref[z])
+            out_ref[first:] = jnp.concatenate([even, odd], axis=0)[:left]
+
+
+def interleaved(core, own, other, rows):
+    whole = pl.BlockSpec(own.shape, lambda i, core: (0, 0, 0))
+    return pl.pallas_call(
+        interleave_kernel,
+        grid_spec=pltpu.PrefetchScalarGridSpec(
+            num_scalar_prefetch=1,
+            grid=(1,),
+            in_specs=[whole, whole],
+            out_specs=pl.BlockSpec((rows, own.shape[2]), lambda i, core: (0, 0)),
+        ),
+        out_shape=jax.ShapeDtypeStruct((rows, own.shape[2]), own.dtype),
+    )(core.reshape(1), own, other)
 
 
 def product_kernel(order_ref, *refs):
@@ -195,7 +224,9 @@
     parts = lax.all_to_all(sent.reshape(workers, share, length), DP, 0, 0)
     averaged = parts.sum(0) / workers
     own_update = jnp.dot(averaged, cosine_table, precision=lax.Precision.HIGH)
-    update = gathered(own_update, DP).reshape(rows, length)[:block_count]
+    along_z = gathered(own_update, "z")
+    swapped = lax.ppermute(along_z, "core", [(0, 1), (1, 0)])
+    update = interleaved(lax.axis_index("core"), along_z, swapped, block_count)
 
     gate_grad, up_grad = product(order, pieces, weight, gate_pre.T, up_pre.T)
     return (gate_grad.T, up_grad.T, new_momentum[None], update)

time: 115 us -> 115 us (level)
  waiting for transfers between devices: 38.4 us -> 34.7 us
  Pallas kernels: 7.32 us -> 9.16 us
  starting transfers between devices: 42.8 us -> 44.5 us
    ppermute x3, waiting for transfers between devices: 15 us -> 11.3 us  [per_device_body(): lax.ppermute(own_piece, 'x', [(i, (i + s) % 4) for i in range(4)])]
    ppermute x0 -> x1, starting transfers between devices: none -> 1.94 us  [per_device_body(): swapped = lax.ppermute(along_z, 'core', [(0, 1), (1, 0)])]
    pallas_call x0 -> x1, Pallas kernels: none -> 1.83 us  [interleaved(): pl.pallas_call(interleave_kernel, grid_spec=pltpu.PrefetchScalarGridSpec(...]
  transfers between devices with their start and end apart: 10 -> 11, of which waited for: 5 -> 5; matrix products, arithmetic and copies ran while one was open for 9% -> 8% of each run, Pallas kernels for 2% -> 3%
where the time goes in v4:
time: 115 us; the launch traced here: 114 us
  starting transfers between devices  44.5 us (39%)
  waiting for transfers between devices  34.7 us (30%)
  between operations  14.2 us (12%)
  Pallas kernels  9.16 us (8%)
  matrix products  6.19 us (5%)
  local copies, waits for them, and re-layouts  5.04 us (4%)
    all_to_all x2, starting transfers between devices, gathered(): return lax.all_to_all(copies, axis, 0, 0)  14.8 us
    ppermute x3, waiting for transfers between devices, per_device_body(): lax.ppermute(own_piece, 'x', [(i, (i + s) % 4) for i in range(4)])  11.3 us
    all_to_all x1, starting transfers between devices, per_device_body(): parts = lax.all_to_all(sent.reshape(workers, share, length), DP, 0, 0)  10.5 us
    ppermute x3, starting transfers between devices, per_device_body(): lax.ppermute(own_piece, 'x', [(i, (i + s) % 4) for i in range(4)])  9.19 us
    all_to_all x1, waiting for transfers between devices, per_device_body(): parts = lax.all_to_all(sent.reshape(workers, share, length), DP, 0, 0)  8.96 us
    all_to_all x2, waiting for transfers between devices, gathered(): return lax.all_to_all(copies, axis, 0, 0)  6.91 us
    ppermute x1, waiting for transfers between devices, gathered_over_y(): second = lax.ppermute(pair, 'y', links)  6.79 us
    pallas_call x1, Pallas kernels, product(): pl.pallas_call(product_kernel, grid_spec=pltpu.PrefetchScalarGridSpec(num...  5.44 us
  transfers between devices with their start and end apart: 11, of which 5 were waited for; matrix products, arithmetic and copies ran while one was open for 8% of the time, Pallas kernels for 3%

profile of v4, /device:TPU:6, one launch (start us, length us, event | category | flops | bytes accessed | tf_op | source)
XLA Modules:
  0.0 114.0 jit_solution(16725015563984447644)
XLA Ops:
  9.3 10.2 %all-to-all-start = ((bf16[32,8,256]{2,1,0:T(8,128)(2,1)}), bf16[32,8,256]{2,1,0:T(8,128)(2,1)S(1)}, u32[]{:S(2)}, u32[]{:S(2)}) async-start(bf16[32,8,256]{2,1,0:T(8,128)(2,1)} %broadcast_in_dim.8), calls=%async_computation | async-start | bytes 262144 | tf_op jit(solution)/shard_map/all_to_all | solution.py:29
  19.5 3.4 %collective-permute-start = (bf16[8,4096]{1,0:T(8,128)(2,1)}, bf16[8,4096]{1,0:T(8,128)(2,1)S(1)}, u32[]{:S(2)}, u32[]{:S(2)}) collective-permute-start(bf16[8,4096]{1,0:T(8,128)(2,1)} %param.9), channel_id=1, source_target_pairs={{0,4},{4,0},{8,12},{12,8},{16,20},{20,16},{24,28},{28,24},{1,5},{5... | collective-permute-start | bytes 196616 | tf_op jit(solution)/shard_map/ppermute | solution.py:33
  22.9 1.9 %shard_map.121 = f32[512,256]{1,0:T(8,128)} custom-call(s32[32,464]{1,0:T(8,128)} %bitcast.33, s32[1,464]{1,0:T(1,128)} %count_ref.1), custom_call_target="tpu_custom_call" | custom-call | flops 7602176 | bytes 524288 | tf_op jit(solution)/shard_map/pallas_call | solution.py:79
  24.7 3.7 %all-to-all-done = bf16[32,8,256]{2,1,0:T(8,128)(2,1)S(1)} async-done(((bf16[32,8,256]{2,1,0:T(8,128)(2,1)}), bf16[32,8,256]{2,1,0:T(8,128)(2,1)S(1)}, u32[]{:S(2)}, u32[]{:S(2)}) %all-to-all-start) | async-done | bytes 131104 | tf_op jit(solution)/shard_map/all_to_all | solution.py:29
  28.5 1.5 %fusion = f32[464,256]{1,0:T(8,128)S(1)} fusion(f32[1,464,256]{2,1,0:T(8,128)} %param.13, bf16[256,464]{0,1:T(8,128)(2,1)} %param.11, bf16[256,464]{0,1:T(8,128)(2,1)} %param.10, bf16[32,8,256]{2,1,0:T(8,128)(2,1)S(1)} %all-to-all-done), kind=kOutput, calls=%fused_computation.2 | convolution fusion | flops 62124032 | bytes 1556480 | tf_op jit(solution)/shard_map/dot_general | solution.py:209
  30.0 2.3 %convolution_select_fusion = f32[512,256]{1,0:T(8,128)} fusion(f32[256,256]{1,0:T(8,128)S(1)} %copy-done, f32[464,256]{1,0:T(8,128)S(1)} %fusion, f32[512,256]{1,0:T(8,128)} %shard_map.121), kind=kOutput, calls=%fused_computation | convolution fusion | flops 201588736 | bytes 1785856 | tf_op jit(solution)/shard_map/dot_general | solution.py:220
  32.3 10.5 %all-to-all-start.1 = ((f32[16,32,256]{2,1,0:T(8,128)}), f32[16,32,256]{2,1,0:T(8,128)S(1)}, u32[]{:S(2)}, u32[]{:S(2)}) async-start(f32[16,32,256]{2,1,0:T(8,128)} %bitcast.14), calls=%async_computation.1 | async-start | bytes 1048576 | tf_op jit(solution)/shard_map/all_to_all | solution.py:224
  42.8 2.1 %collective-permute-start.1 = (bf16[2,8,4096]{2,1,0:T(8,128)(2,1)S(1)}, bf16[2,8,4096]{2,1,0:T(8,128)(2,1)S(1)}, u32[]{:S(2)}, u32[]{:S(2)}) collective-permute-start(bf16[2,8,4096]{2,1,0:T(8,128)(2,1)S(1)} %pad_maximum_fusion.2), channel_id=1, source_target_pairs={{0,28},{4,8},{8,4},{12,16},{16,12},{20,24},{24,20},{28,0},{1,29},{... | collective-permute-start | bytes 393224 | tf_op jit(solution)/shard_map/ppermute | solution.py:36
  44.9 6.8 %collective-permute-done.1 = bf16[2,8,4096]{2,1,0:T(8,128)(2,1)S(1)} collective-permute-done((bf16[2,8,4096]{2,1,0:T(8,128)(2,1)S(1)}, bf16[2,8,4096]{2,1,0:T(8,128)(2,1)S(1)}, u32[]{:S(2)}, u32[]{:S(2)}) %collective-permute-start.1) | collective-permute-done | bytes 131104 | tf_op jit(solution)/shard_map/ppermute | solution.py:36
  51.7 2.6 %collective-permute-start.2 = (bf16[4,8,4096]{2,1,0:T(8,128)(2,1)S(1)}, bf16[4,8,4096]{2,1,0:T(8,128)(2,1)S(1)}, u32[]{:S(2)}, u32[]{:S(2)}) collective-permute-start(bf16[4,8,4096]{2,1,0:T(8,128)(2,1)S(1)} %pad_maximum_fusion.1), channel_id=1, source_target_pairs={{0,12},{4,24},{8,20},{12,0},{16,28},{20,8},{24,4},{28,16},{1,13},{... | collective-permute-start | bytes 786440 | tf_op jit(solution)/shard_map/ppermute | solution.py:39
  54.4 9.0 %all-to-all-done.1 = f32[16,32,256]{2,1,0:T(8,128)S(1)} async-done(((f32[16,32,256]{2,1,0:T(8,128)}), f32[16,32,256]{2,1,0:T(8,128)S(1)}, u32[]{:S(2)}, u32[]{:S(2)}) %all-to-all-start.1) | async-done | bytes 524320 | tf_op jit(solution)/shard_map/all_to_all | solution.py:224
  63.6 0.7 broadcast_in_dim.10
  64.3 4.6 %all-to-all-start.2 = ((f32[8,32,256]{2,1,0:T(8,128)}), f32[8,32,256]{2,1,0:T(8,128)S(1)}, u32[]{:S(2)}, u32[]{:S(2)}) async-start(f32[8,32,256]{2,1,0:T(8,128)} %broadcast_in_dim.10), calls=%async_computation.2 | async-start | bytes 524288 | tf_op jit(solution)/shard_map/all_to_all | solution.py:29
  69.0 3.9 %collective-permute-start.3 = (bf16[8,8,4096]{2,1,0:T(8,128)(2,1)S(1)}, bf16[8,8,4096]{2,1,0:T(8,128)(2,1)S(1)}, u32[]{:S(2)}, u32[]{:S(2)}) collective-permute-start(bf16[8,8,4096]{2,1,0:T(8,128)(2,1)S(1)} %pad_maximum_fusion.refs_0_), channel_id=1, source_target_pairs={{0,1},{1,2},{2,3},{3,0},{4,5},{5,6},{6,7},{7,4},{8,9},{9,10},{10,1... | collective-permute-start | bytes 1572872 | tf_op jit(solution)/shard_map/ppermute | solution.py:202
  72.9 1.9 %collective-permute-start.4 = (bf16[8,8,4096]{2,1,0:T(8,128)(2,1)S(1)}, bf16[8,8,4096]{2,1,0:T(8,128)(2,1)S(1)}, u32[]{:S(2)}, u32[]{:S(2)}) collective-permute-start(bf16[8,8,4096]{2,1,0:T(8,128)(2,1)S(1)} %pad_maximum_fusion.refs_0_), channel_id=1, source_target_pairs={{0,3},{1,0},{2,1},{3,2},{4,7},{5,4},{6,5},{7,6},{8,11},{9,8},{10,9... | collective-permute-start | bytes 1572872 | tf_op jit(solution)/shard_map/ppermute | solution.py:202
  74.8 3.4 %collective-permute-start.5 = (bf16[8,8,4096]{2,1,0:T(8,128)(2,1)S(1)}, bf16[8,8,4096]{2,1,0:T(8,128)(2,1)S(1)}, u32[]{:S(2)}, u32[]{:S(2)}) collective-permute-start(bf16[8,8,4096]{2,1,0:T(8,128)(2,1)S(1)} %pad_maximum_fusion.refs_0_), channel_id=1, source_target_pairs={{0,2},{1,3},{2,0},{3,1},{4,6},{5,7},{6,4},{7,5},{8,10},{9,11},{10,... | collective-permute-start | bytes 1572872 | tf_op jit(solution)/shard_map/ppermute | solution.py:202
  78.2 3.2 %all-to-all-done.2.own_ref = f32[8,32,256]{2,1,0:T(8,128)S(1)} async-done(((f32[8,32,256]{2,1,0:T(8,128)}), f32[8,32,256]{2,1,0:T(8,128)S(1)}, u32[]{:S(2)}, u32[]{:S(2)}) %all-to-all-start.2) | async-done | bytes 262176 | tf_op jit(solution)/shard_map/all_to_all | solution.py:29
  81.4 1.9 %collective-permute-start.6 = (f32[8,32,256]{2,1,0:T(8,128)S(1)}, f32[8,32,256]{2,1,0:T(8,128)S(1)}, u32[]{:S(2)}, u32[]{:S(2)}) collective-permute-start(f32[8,32,256]{2,1,0:T(8,128)S(1)} %all-to-all-done.2.own_ref), channel_id=1, source_target_pairs={{0,32},{32,0},{1,33},{33,1},{2,34},{34,2},{3,35},{35,3},{4,36},{36... | collective-permute-start | bytes 786440 | tf_op jit(solution)/shard_map/ppermute | solution.py:228
  83.4 1.3 %dynamic-slice_bitcast_fusion.order_ref = s32[12]{0:T(128)} fusion(s32[32,12]{1,0:T(8,128)} %constant.37.clone, s32[]{:T(128)S(6)} %select_n.7), kind=kLoop, calls=%fused_computation.22 | loop fusion | bytes 100 | tf_op jit(solution)/shard_map/squeeze | solution.py:57
  84.6 2.2 %fusion.1 = f32[1,464,256]{2,1,0:T(8,128)} fusion(f32[464,256]{1,0:T(8,128)S(1)} %fusion, f32[256,256]{1,0:T(8,128)S(1)} %copy-done, f32[512,256]{1,0:T(8,128)} %convolution_select_fusion), kind=kOutput, calls=%fused_computation.4 | convolution fusion | flops 182571008 | bytes 1687552 | tf_op jit(solution)/shard_map/dot_general | solution.py:222
  87.5 1.8 %shard_map.122 = f32[464,256]{1,0:T(8,128)} custom-call(s32[1]{0:T(128)} %bitcast.13.core_ref, f32[8,32,256]{2,1,0:T(8,128)} %copy-done.2, f32[8,32,256]{2,1,0:T(8,128)} %copy-done.7), custom_call_target="tpu_custom_call" | custom-call | tf_op jit(solution)/shard_map/pallas_call | solution.py:105
  89.4 11.3 %collective-permute-done.4.refs_2_ = bf16[8,8,4096]{2,1,0:T(8,128)(2,1)S(1)} collective-permute-done((bf16[8,8,4096]{2,1,0:T(8,128)(2,1)S(1)}, bf16[8,8,4096]{2,1,0:T(8,128)(2,1)S(1)}, u32[]{:S(2)}, u32[]{:S(2)}) %collective-permute-start.4) | collective-permute-done | bytes 524320 | tf_op jit(solution)/shard_map/ppermute | solution.py:202
  100.7 0.8 copy-done.5
  101.7 5.4 %shard_map.120 = (bf16[464,256]{1,0:T(8,128)(2,1)}, bf16[464,256]{1,0:T(8,128)(2,1)}) custom-call(s32[12]{0:T(128)} %dynamic-slice_bitcast_fusion.order_ref, bf16[8,8,4096]{2,1,0:T(8,128)(2,1)} %copy-done.1, bf16[8,8,4096]{2,1,0:T(8,128)(2,1)} %copy-done.4, bf16[8,8,4096]{2,1,0:T(8,128)(2,1)} %copy-done.5, bf16[8,8,4096]{2,1,0:T(8,128)(2,1)} %copy-done.6, ...), custom_call_target="tpu_custom_call" | custom-call | flops 973078528 | bytes 6848512 | tf_op jit(solution)/shard_map/pallas_call | solution.py:167
  (30 shorter events, 3.4 us)
Async XLA Ops:
  7.2 22.8 %copy-start = (f32[256,256]{1,0:T(8,128)S(1)}, f32[256,256]{1,0:T(8,128)}, u32[]{:S(2)}) copy-start(f32[256,256]{1,0:T(8,128)} %constant.38.clone) | copy-start | bytes 786436
  7.2 35.6 %copy-start.3 = (bf16[8,4096]{1,0:T(8,128)(2,1)S(1)}, bf16[8,4096]{1,0:T(8,128)(2,1)}, u32[]{:S(2)}) copy-start(bf16[8,4096]{1,0:T(8,128)(2,1)} %param.9) | copy-start | bytes 196612
  7.2 93.5 %all-gather.3.cloned.1.call-start = ((), (), s32[]{:S(2)}) async-start(), calls=%async_computation.3 | async-start | bytes 4038656 | tf_op jit(solution)/shard_map/all_gather | solution.py:197
  9.3 19.2 %all-to-all-start = ((bf16[32,8,256]{2,1,0:T(8,128)(2,1)}), bf16[32,8,256]{2,1,0:T(8,128)(2,1)S(1)}, u32[]{:S(2)}, u32[]{:S(2)}) async-start(bf16[32,8,256]{2,1,0:T(8,128)(2,1)} %broadcast_in_dim.8), calls=%async_computation | async-start | bytes 262144 | tf_op jit(solution)/shard_map/all_to_all | solution.py:29
  19.5 23.3 %collective-permute-start = (bf16[8,4096]{1,0:T(8,128)(2,1)}, bf16[8,4096]{1,0:T(8,128)(2,1)S(1)}, u32[]{:S(2)}, u32[]{:S(2)}) collective-permute-start(bf16[8,4096]{1,0:T(8,128)(2,1)} %param.9), channel_id=1, source_target_pairs={{0,4},{4,0},{8,12},{12,8},{16,20},{20,16},{24,28},{28,24},{1,5},{5... | collective-permute-start | bytes 196616 | tf_op jit(solution)/shard_map/ppermute | solution.py:33
  32.3 31.0 %all-to-all-start.1 = ((f32[16,32,256]{2,1,0:T(8,128)}), f32[16,32,256]{2,1,0:T(8,128)S(1)}, u32[]{:S(2)}, u32[]{:S(2)}) async-start(f32[16,32,256]{2,1,0:T(8,128)} %bitcast.14), calls=%async_computation.1 | async-start | bytes 1048576 | tf_op jit(solution)/shard_map/all_to_all | solution.py:224
  42.8 8.9 %collective-permute-start.1 = (bf16[2,8,4096]{2,1,0:T(8,128)(2,1)S(1)}, bf16[2,8,4096]{2,1,0:T(8,128)(2,1)S(1)}, u32[]{:S(2)}, u32[]{:S(2)}) collective-permute-start(bf16[2,8,4096]{2,1,0:T(8,128)(2,1)S(1)} %pad_maximum_fusion.2), channel_id=1, source_target_pairs={{0,28},{4,8},{8,4},{12,16},{16,12},{20,24},{24,20},{28,0},{1,29},{... | collective-permute-start | bytes 393224 | tf_op jit(solution)/shard_map/ppermute | solution.py:36
  51.7 17.2 %collective-permute-start.2 = (bf16[4,8,4096]{2,1,0:T(8,128)(2,1)S(1)}, bf16[4,8,4096]{2,1,0:T(8,128)(2,1)S(1)}, u32[]{:S(2)}, u32[]{:S(2)}) collective-permute-start(bf16[4,8,4096]{2,1,0:T(8,128)(2,1)S(1)} %pad_maximum_fusion.1), channel_id=1, source_target_pairs={{0,12},{4,24},{8,20},{12,0},{16,28},{20,8},{24,4},{28,16},{1,13},{... | collective-permute-start | bytes 786440 | tf_op jit(solution)/shard_map/ppermute | solution.py:39
  64.3 17.1 %all-to-all-start.2 = ((f32[8,32,256]{2,1,0:T(8,128)}), f32[8,32,256]{2,1,0:T(8,128)S(1)}, u32[]{:S(2)}, u32[]{:S(2)}) async-start(f32[8,32,256]{2,1,0:T(8,128)} %broadcast_in_dim.10), calls=%async_computation.2 | async-start | bytes 524288 | tf_op jit(solution)/shard_map/all_to_all | solution.py:29
  69.0 31.7 %copy-start.1 = (bf16[8,8,4096]{2,1,0:T(8,128)(2,1)}, bf16[8,8,4096]{2,1,0:T(8,128)(2,1)S(1)}, u32[]{:S(2)}) copy-start(bf16[8,8,4096]{2,1,0:T(8,128)(2,1)S(1)} %pad_maximum_fusion.refs_0_) | copy-start | bytes 1572868
  69.0 20.4 %collective-permute-start.3 = (bf16[8,8,4096]{2,1,0:T(8,128)(2,1)S(1)}, bf16[8,8,4096]{2,1,0:T(8,128)(2,1)S(1)}, u32[]{:S(2)}, u32[]{:S(2)}) collective-permute-start(bf16[8,8,4096]{2,1,0:T(8,128)(2,1)S(1)} %pad_maximum_fusion.refs_0_), channel_id=1, source_target_pairs={{0,1},{1,2},{2,3},{3,0},{4,5},{5,6},{6,7},{7,4},{8,9},{9,10},{10,1... | collective-permute-start | bytes 1572872 | tf_op jit(solution)/shard_map/ppermute | solution.py:202
  72.9 27.8 %collective-permute-start.4 = (bf16[8,8,4096]{2,1,0:T(8,128)(2,1)S(1)}, bf16[8,8,4096]{2,1,0:T(8,128)(2,1)S(1)}, u32[]{:S(2)}, u32[]{:S(2)}) collective-permute-start(bf16[8,8,4096]{2,1,0:T(8,128)(2,1)S(1)} %pad_maximum_fusion.refs_0_), channel_id=1, source_target_pairs={{0,3},{1,0},{2,1},{3,2},{4,7},{5,4},{6,5},{7,6},{8,11},{9,8},{10,9... | collective-permute-start | bytes 1572872 | tf_op jit(solution)/shard_map/ppermute | solution.py:202
  74.8 25.8 %collective-permute-start.5 = (bf16[8,8,4096]{2,1,0:T(8,128)(2,1)S(1)}, bf16[8,8,4096]{2,1,0:T(8,128)(2,1)S(1)}, u32[]{:S(2)}, u32[]{:S(2)}) collective-permute-start(bf16[8,8,4096]{2,1,0:T(8,128)(2,1)S(1)} %pad_maximum_fusion.refs_0_), channel_id=1, source_target_pairs={{0,2},{1,3},{2,0},{3,1},{4,6},{5,7},{6,4},{7,5},{8,10},{9,11},{10,... | collective-permute-start | bytes 1572872 | tf_op jit(solution)/shard_map/ppermute | solution.py:202
  81.4 5.4 %copy-start.2 = (f32[8,32,256]{2,1,0:T(8,128)}, f32[8,32,256]{2,1,0:T(8,128)S(1)}, u32[]{:S(2)}) copy-start(f32[8,32,256]{2,1,0:T(8,128)S(1)} %all-to-all-done.2.own_ref) | copy-start | bytes 786436
  81.4 5.4 %collective-permute-start.6 = (f32[8,32,256]{2,1,0:T(8,128)S(1)}, f32[8,32,256]{2,1,0:T(8,128)S(1)}, u32[]{:S(2)}, u32[]{:S(2)}) collective-permute-start(f32[8,32,256]{2,1,0:T(8,128)S(1)} %all-to-all-done.2.own_ref), channel_id=1, source_target_pairs={{0,32},{32,0},{1,33},{33,1},{2,34},{34,2},{3,35},{35,3},{4,36},{36... | collective-permute-start | bytes 786440 | tf_op jit(solution)/shard_map/ppermute | solution.py:228
  86.8 0.7 copy-start.7
  89.4 11.4 %copy-start.4 = (bf16[8,8,4096]{2,1,0:T(8,128)(2,1)}, bf16[8,8,4096]{2,1,0:T(8,128)(2,1)S(1)}, u32[]{:S(2)}) copy-start(bf16[8,8,4096]{2,1,0:T(8,128)(2,1)S(1)} %collective-permute-done.3.refs_1_) | copy-start | bytes 1572868
  100.7 0.8 copy-start.5
  100.7 1.0 copy-start.6
Sparse Core Ops, SparseCore 0:
  10.1 58.5 all-gather.2

commit v5 on v3

--- a/solution.py
+++ b/solution.py
@@ -85,6 +85,58 @@
     )(index, count)
 
 
+STEPS = 16384.0
+VMEM = pl.BlockSpec(memory_space=pltpu.VMEM)
+
+
+def update_kernel(total_ref, table_ref, coded_ref):
+    workers = coded_ref.shape[0]
+    share, length = total_ref.shape
+    update = jnp.dot(
+        total_ref[...] * (1.0 / workers),
+        table_ref[...],
+        precision=lax.Precision.HIGHEST,
+        preferred_element_type=jnp.float32,
+    )
+    largest = jnp.max(jnp.abs(update), axis=0, keepdims=True)
+    exponent = jnp.ceil(jnp.log2(jnp.maximum(largest, 1e-30)))
+    value = jnp.round(update * (jnp.exp2(-exponent) * STEPS))
+    exponent = jnp.broadcast_to(exponent, (coded_ref.shape[1] - share, length))
+    rows = jnp.concatenate([value, exponent], axis=0).astype(jnp.int32).astype(jnp.int16)
+    for w in range(workers):
+        coded_ref[w] = rows
+
+
+def coded_update(total, table, workers):
+    share, length = total.shape
+    return pl.pallas_call(
+        update_kernel,
+        in_specs=[VMEM, VMEM],
+        out_specs=VMEM,
+        out_shape=jax.ShapeDtypeStruct((workers, share + 8, length), jnp.int16),
+    )(total, table)
+
+
+def decode_kernel(coded_ref, update_ref):
+    share = coded_ref.shape[1] - 8
+    for w in range(coded_ref.shape[0]):
+        first = w * share
+        last = min(first + share, update_ref.shape[0])
+        if first < last:
+            rows = coded_ref[w].astype(jnp.int32).astype(jnp.float32)
+            scale = jnp.exp2(rows[share : share + 1]) * (1.0 / STEPS)
+            update_ref[first:last] = (rows[:share] * scale)[: last - first]
+
+
+def decoded(coded, rows):
+    return pl.pallas_call(
+        decode_kernel,
+        in_specs=[VMEM],
+        out_specs=VMEM,
+        out_shape=jax.ShapeDtypeStruct((rows, coded.shape[2]), jnp.float32),
+    )(coded)
+
+
 def product_kernel(order_ref, *refs):
     pieces, refs = refs[:4], refs[4:]
     weight_ref, gate_ref, up_ref, gate_grad_ref, up_grad_ref, total_ref, act_ref, slope_ref, rows_ref = refs
@@ -193,9 +245,9 @@
     new_momentum = mixed - jnp.dot(sent[:block_count], cosine_table, precision=lax.Precision.HIGH)
 
     parts = lax.all_to_all(sent.reshape(workers, share, length), DP, 0, 0)
-    averaged = parts.sum(0) / workers
-    own_update = jnp.dot(averaged, cosine_table, precision=lax.Precision.HIGH)
-    update = gathered(own_update, DP).reshape(rows, length)[:block_count]
+    coded = coded_update(parts.sum(0), cosine_table, workers)
+    arrived = lax.all_to_all(coded, DP, 0, 0)
+    update = decoded(arrived, block_count)
 
     gate_grad, up_grad = product(order, pieces, weight, gate_pre.T, up_pre.T)
     return (gate_grad.T, up_grad.T, new_momentum[None], update)

time: 115 us -> 117 us (1.017)
  the two profiles are of different devices: /device:TPU:6 before, /device:TPU:1 now
where the time goes in v5:
time: 117 us; the launch traced here: 115 us
  starting transfers between devices  43.2 us (37%)
  waiting for transfers between devices  35.4 us (30%)
  between operations  14.2 us (12%)
  Pallas kernels  11.1 us (9%)
  matrix products  6.11 us (5%)
  local copies, waits for them, and re-layouts  4.3 us (4%)
    ppermute x3, waiting for transfers between devices, per_device_body(): lax.ppermute(own_piece, 'x', [(i, (i + s) % 4) for i in range(4)])  13.1 us
    all_to_all x1, starting transfers between devices, per_device_body(): parts = lax.all_to_all(sent.reshape(workers, share, length), DP, 0, 0)  12.6 us
    all_to_all x1, waiting for transfers between devices, per_device_body(): parts = lax.all_to_all(sent.reshape(workers, share, length), DP, 0, 0)  10.6 us
    all_to_all x1, starting transfers between devices, gathered(): return lax.all_to_all(copies, axis, 0, 0)  10.5 us
    ppermute x3, starting transfers between devices, per_device_body(): lax.ppermute(own_piece, 'x', [(i, (i + s) % 4) for i in range(4)])  8.7 us
    ppermute x1, waiting for transfers between devices, gathered_over_y(): second = lax.ppermute(pair, 'y', links)  6.03 us
    pallas_call x1, Pallas kernels, product(): pl.pallas_call(product_kernel, grid_spec=pltpu.PrefetchScalarGridSpec(num...  5.45 us
    all_to_all x1, waiting for transfers between devices, gathered(): return lax.all_to_all(copies, axis, 0, 0)  4.33 us
  transfers between devices with their start and end apart: 10, of which 6 were waited for; matrix products, arithmetic and copies ran while one was open for 8% of the time, Pallas kernels for 5%

profile of v5, /device:TPU:1, one launch (start us, length us, event | category | flops | bytes accessed | tf_op | source)
XLA Modules:
  0.0 115.1 jit_solution(10199387837838819564)
XLA Ops:
  9.3 10.5 %all-to-all-start = ((bf16[32,8,256]{2,1,0:T(8,128)(2,1)}), bf16[32,8,256]{2,1,0:T(8,128)(2,1)S(1)}, u32[]{:S(2)}, u32[]{:S(2)}) async-start(bf16[32,8,256]{2,1,0:T(8,128)(2,1)} %broadcast_in_dim.6), calls=%async_computation | async-start | bytes 262144 | tf_op jit(solution)/shard_map/all_to_all | solution.py:29
  19.8 3.1 %collective-permute-start = (bf16[8,4096]{1,0:T(8,128)(2,1)}, bf16[8,4096]{1,0:T(8,128)(2,1)S(1)}, u32[]{:S(2)}, u32[]{:S(2)}) collective-permute-start(bf16[8,4096]{1,0:T(8,128)(2,1)} %param.9), channel_id=1, source_target_pairs={{0,4},{4,0},{8,12},{12,8},{16,20},{20,16},{24,28},{28,24},{1,5},{5... | collective-permute-start | bytes 196616 | tf_op jit(solution)/shard_map/ppermute | solution.py:33
  22.9 1.9 %shard_map.121 = f32[512,256]{1,0:T(8,128)} custom-call(s32[32,464]{1,0:T(8,128)} %bitcast.31, s32[1,464]{1,0:T(1,128)} %count_ref.1), custom_call_target="tpu_custom_call" | custom-call | flops 7602176 | bytes 524288 | tf_op jit(solution)/shard_map/pallas_call | solution.py:79
  24.8 4.3 %all-to-all-done = bf16[32,8,256]{2,1,0:T(8,128)(2,1)S(1)} async-done(((bf16[32,8,256]{2,1,0:T(8,128)(2,1)}), bf16[32,8,256]{2,1,0:T(8,128)(2,1)S(1)}, u32[]{:S(2)}, u32[]{:S(2)}) %all-to-all-start) | async-done | bytes 131104 | tf_op jit(solution)/shard_map/all_to_all | solution.py:29
  29.1 1.6 %fusion = f32[464,256]{1,0:T(8,128)S(1)} fusion(f32[1,464,256]{2,1,0:T(8,128)} %param.13, bf16[256,464]{0,1:T(8,128)(2,1)} %param.11, bf16[256,464]{0,1:T(8,128)(2,1)} %param.10, bf16[32,8,256]{2,1,0:T(8,128)(2,1)S(1)} %all-to-all-done), kind=kOutput, calls=%fused_computation.2 | convolution fusion | flops 62124032 | bytes 1556480 | tf_op jit(solution)/shard_map/dot_general | solution.py:232
  30.8 2.3 %convolution_select_fusion = f32[512,256]{1,0:T(8,128)} fusion(f32[256,256]{1,0:T(8,128)S(1)} %copy-done, f32[464,256]{1,0:T(8,128)S(1)} %fusion, f32[512,256]{1,0:T(8,128)} %shard_map.121), kind=kOutput, calls=%fused_computation | convolution fusion | flops 201588736 | bytes 1785856 | tf_op jit(solution)/shard_map/dot_general | solution.py:243
  33.1 12.6 %all-to-all-start.1 = ((f32[16,32,256]{2,1,0:T(8,128)}), f32[16,32,256]{2,1,0:T(8,128)S(1)}, u32[]{:S(2)}, u32[]{:S(2)}) async-start(f32[16,32,256]{2,1,0:T(8,128)} %bitcast.13), calls=%async_computation.1 | async-start | bytes 1048576 | tf_op jit(solution)/shard_map/all_to_all | solution.py:247
  45.7 2.1 %collective-permute-start.1 = (bf16[2,8,4096]{2,1,0:T(8,128)(2,1)S(1)}, bf16[2,8,4096]{2,1,0:T(8,128)(2,1)S(1)}, u32[]{:S(2)}, u32[]{:S(2)}) collective-permute-start(bf16[2,8,4096]{2,1,0:T(8,128)(2,1)S(1)} %pad_maximum_fusion.2), channel_id=1, source_target_pairs={{0,28},{4,8},{8,4},{12,16},{16,12},{20,24},{24,20},{28,0},{1,29},{... | collective-permute-start | bytes 393224 | tf_op jit(solution)/shard_map/ppermute | solution.py:36
  47.9 6.0 %collective-permute-done.1 = bf16[2,8,4096]{2,1,0:T(8,128)(2,1)S(1)} collective-permute-done((bf16[2,8,4096]{2,1,0:T(8,128)(2,1)S(1)}, bf16[2,8,4096]{2,1,0:T(8,128)(2,1)S(1)}, u32[]{:S(2)}, u32[]{:S(2)}) %collective-permute-start.1) | collective-permute-done | bytes 131104 | tf_op jit(solution)/shard_map/ppermute | solution.py:36
  53.9 2.4 %collective-permute-start.2 = (bf16[4,8,4096]{2,1,0:T(8,128)(2,1)S(1)}, bf16[4,8,4096]{2,1,0:T(8,128)(2,1)S(1)}, u32[]{:S(2)}, u32[]{:S(2)}) collective-permute-start(bf16[4,8,4096]{2,1,0:T(8,128)(2,1)S(1)} %pad_maximum_fusion.1), channel_id=1, source_target_pairs={{0,12},{4,24},{8,20},{12,0},{16,28},{20,8},{24,4},{28,16},{1,13},{... | collective-permute-start | bytes 786440 | tf_op jit(solution)/shard_map/ppermute | solution.py:39
  56.4 10.6 %all-to-all-done.1 = f32[16,32,256]{2,1,0:T(8,128)S(1)} async-done(((f32[16,32,256]{2,1,0:T(8,128)}), f32[16,32,256]{2,1,0:T(8,128)S(1)}, u32[]{:S(2)}, u32[]{:S(2)}) %all-to-all-start.1) | async-done | bytes 524320 | tf_op jit(solution)/shard_map/all_to_all | solution.py:247
  67.6 2.0 %shard_map.122 = s16[16,40,256]{2,1,0:T(8,128)(2,1)} custom-call(f32[32,256]{1,0:T(8,128)} %reduce_sum.9.total_ref, f32[256,256]{1,0:T(8,128)} %constant.30.clone.table_ref), custom_call_target="tpu_custom_call" | custom-call | tf_op jit(solution)/shard_map/pallas_call | solution.py:112
  69.6 3.6 %all-to-all-start.2 = ((s16[16,40,256]{2,1,0:T(8,128)(2,1)}), s16[16,40,256]{2,1,0:T(8,128)(2,1)S(1)}, u32[]{:S(2)}, u32[]{:S(2)}) async-start(s16[16,40,256]{2,1,0:T(8,128)(2,1)} %shard_map.122), calls=%async_computation.2 | async-start | bytes 655360 | tf_op jit(solution)/shard_map/all_to_all | solution.py:249
  73.3 2.0 %collective-permute-start.3 = (bf16[8,8,4096]{2,1,0:T(8,128)(2,1)S(1)}, bf16[8,8,4096]{2,1,0:T(8,128)(2,1)S(1)}, u32[]{:S(2)}, u32[]{:S(2)}) collective-permute-start(bf16[8,8,4096]{2,1,0:T(8,128)(2,1)S(1)} %pad_maximum_fusion.refs_0_), channel_id=1, source_target_pairs={{0,1},{1,2},{2,3},{3,0},{4,5},{5,6},{6,7},{7,4},{8,9},{9,10},{10,1... | collective-permute-start | bytes 1572872 | tf_op jit(solution)/shard_map/ppermute | solution.py:225
  75.3 4.5 %collective-permute-start.4 = (bf16[8,8,4096]{2,1,0:T(8,128)(2,1)S(1)}, bf16[8,8,4096]{2,1,0:T(8,128)(2,1)S(1)}, u32[]{:S(2)}, u32[]{:S(2)}) collective-permute-start(bf16[8,8,4096]{2,1,0:T(8,128)(2,1)S(1)} %pad_maximum_fusion.refs_0_), channel_id=1, source_target_pairs={{0,3},{1,0},{2,1},{3,2},{4,7},{5,4},{6,5},{7,6},{8,11},{9,8},{10,9... | collective-permute-start | bytes 1572872 | tf_op jit(solution)/shard_map/ppermute | solution.py:225
  79.8 2.2 %collective-permute-start.5 = (bf16[8,8,4096]{2,1,0:T(8,128)(2,1)S(1)}, bf16[8,8,4096]{2,1,0:T(8,128)(2,1)S(1)}, u32[]{:S(2)}, u32[]{:S(2)}) collective-permute-start(bf16[8,8,4096]{2,1,0:T(8,128)(2,1)S(1)} %pad_maximum_fusion.refs_0_), channel_id=1, source_target_pairs={{0,2},{1,3},{2,0},{3,1},{4,6},{5,7},{6,4},{7,5},{8,10},{9,11},{10,... | collective-permute-start | bytes 1572872 | tf_op jit(solution)/shard_map/ppermute | solution.py:225
  82.0 1.2 %dynamic-slice_bitcast_fusion.order_ref = s32[12]{0:T(128)} fusion(s32[32,12]{1,0:T(8,128)} %constant.29.clone, s32[]{:T(128)S(6)} %select_n.7), kind=kLoop, calls=%fused_computation.19 | loop fusion | bytes 100 | tf_op jit(solution)/shard_map/squeeze | solution.py:57
  83.2 2.2 %fusion.1 = f32[1,464,256]{2,1,0:T(8,128)} fusion(f32[464,256]{1,0:T(8,128)S(1)} %fusion, f32[256,256]{1,0:T(8,128)S(1)} %copy-done.1, f32[512,256]{1,0:T(8,128)} %convolution_select_fusion), kind=kOutput, calls=%fused_computation.4 | convolution fusion | flops 182571008 | bytes 1687552 | tf_op jit(solution)/shard_map/dot_general | solution.py:245
  85.4 0.8 all-to-all-done.2.coded_ref
  86.9 1.8 %shard_map.123 = f32[464,256]{1,0:T(8,128)} custom-call(s16[16,40,256]{2,1,0:T(8,128)(2,1)} %copy-done.3), custom_call_target="tpu_custom_call" | custom-call | tf_op jit(solution)/shard_map/pallas_call | solution.py:132
  88.7 1.1 collective-permute-done.3.refs_1_
  89.8 11.9 %collective-permute-done.4.refs_2_ = bf16[8,8,4096]{2,1,0:T(8,128)(2,1)S(1)} collective-permute-done((bf16[8,8,4096]{2,1,0:T(8,128)(2,1)S(1)}, bf16[8,8,4096]{2,1,0:T(8,128)(2,1)S(1)}, u32[]{:S(2)}, u32[]{:S(2)}) %collective-permute-start.4) | collective-permute-done | bytes 524320 | tf_op jit(solution)/shard_map/ppermute | solution.py:225
  101.8 0.8 copy-done.6
  102.8 5.4 %shard_map.120 = (bf16[464,256]{1,0:T(8,128)(2,1)}, bf16[464,256]{1,0:T(8,128)(2,1)}) custom-call(s32[12]{0:T(128)} %dynamic-slice_bitcast_fusion.order_ref, bf16[8,8,4096]{2,1,0:T(8,128)(2,1)} %copy-done.2, bf16[8,8,4096]{2,1,0:T(8,128)(2,1)} %copy-done.5, bf16[8,8,4096]{2,1,0:T(8,128)(2,1)} %copy-done.6, bf16[8,8,4096]{2,1,0:T(8,128)(2,1)} %copy-done.7, ...), custom_call_target="tpu_custom_call" | custom-call | flops 973078528 | bytes 6848512 | tf_op jit(solution)/shard_map/pallas_call | solution.py:190
  (27 shorter events, 3.8 us)
Async XLA Ops:
  7.2 23.6 %copy-start = (f32[256,256]{1,0:T(8,128)S(1)}, f32[256,256]{1,0:T(8,128)}, u32[]{:S(2)}) copy-start(f32[256,256]{1,0:T(8,128)} %constant.30.clone.table_ref) | copy-start | bytes 786436
  7.2 38.5 %copy-start.4 = (bf16[8,4096]{1,0:T(8,128)(2,1)S(1)}, bf16[8,4096]{1,0:T(8,128)(2,1)}, u32[]{:S(2)}) copy-start(bf16[8,4096]{1,0:T(8,128)(2,1)} %param.9) | copy-start | bytes 196612
  7.2 94.6 %all-gather.3.cloned.1.call-start = ((), (), s32[]{:S(2)}) async-start(), calls=%async_computation.3 | async-start | bytes 4038656 | tf_op jit(solution)/shard_map/all_gather | solution.py:220
  9.3 19.8 %all-to-all-start = ((bf16[32,8,256]{2,1,0:T(8,128)(2,1)}), bf16[32,8,256]{2,1,0:T(8,128)(2,1)S(1)}, u32[]{:S(2)}, u32[]{:S(2)}) async-start(bf16[32,8,256]{2,1,0:T(8,128)(2,1)} %broadcast_in_dim.6), calls=%async_computation | async-start | bytes 262144 | tf_op jit(solution)/shard_map/all_to_all | solution.py:29
  19.8 25.9 %collective-permute-start = (bf16[8,4096]{1,0:T(8,128)(2,1)}, bf16[8,4096]{1,0:T(8,128)(2,1)S(1)}, u32[]{:S(2)}, u32[]{:S(2)}) collective-permute-start(bf16[8,4096]{1,0:T(8,128)(2,1)} %param.9), channel_id=1, source_target_pairs={{0,4},{4,0},{8,12},{12,8},{16,20},{20,16},{24,28},{28,24},{1,5},{5... | collective-permute-start | bytes 196616 | tf_op jit(solution)/shard_map/ppermute | solution.py:33
  30.8 52.5 %copy-start.1 = (f32[256,256]{1,0:T(8,128)S(1)}, f32[256,256]{1,0:T(8,128)}, u32[]{:S(2)}) copy-start(f32[256,256]{1,0:T(8,128)} %constant.30.clone.table_ref) | copy-start | bytes 786436
  33.1 33.8 %all-to-all-start.1 = ((f32[16,32,256]{2,1,0:T(8,128)}), f32[16,32,256]{2,1,0:T(8,128)S(1)}, u32[]{:S(2)}, u32[]{:S(2)}) async-start(f32[16,32,256]{2,1,0:T(8,128)} %bitcast.13), calls=%async_computation.1 | async-start | bytes 1048576 | tf_op jit(solution)/shard_map/all_to_all | solution.py:247
  45.7 8.2 %collective-permute-start.1 = (bf16[2,8,4096]{2,1,0:T(8,128)(2,1)S(1)}, bf16[2,8,4096]{2,1,0:T(8,128)(2,1)S(1)}, u32[]{:S(2)}, u32[]{:S(2)}) collective-permute-start(bf16[2,8,4096]{2,1,0:T(8,128)(2,1)S(1)} %pad_maximum_fusion.2), channel_id=1, source_target_pairs={{0,28},{4,8},{8,4},{12,16},{16,12},{20,24},{24,20},{28,0},{1,29},{... | collective-permute-start | bytes 393224 | tf_op jit(solution)/shard_map/ppermute | solution.py:36
  53.9 19.3 %collective-permute-start.2 = (bf16[4,8,4096]{2,1,0:T(8,128)(2,1)S(1)}, bf16[4,8,4096]{2,1,0:T(8,128)(2,1)S(1)}, u32[]{:S(2)}, u32[]{:S(2)}) collective-permute-start(bf16[4,8,4096]{2,1,0:T(8,128)(2,1)S(1)} %pad_maximum_fusion.1), channel_id=1, source_target_pairs={{0,12},{4,24},{8,20},{12,0},{16,28},{20,8},{24,4},{28,16},{1,13},{... | collective-permute-start | bytes 786440 | tf_op jit(solution)/shard_map/ppermute | solution.py:39
  69.6 16.6 %all-to-all-start.2 = ((s16[16,40,256]{2,1,0:T(8,128)(2,1)}), s16[16,40,256]{2,1,0:T(8,128)(2,1)S(1)}, u32[]{:S(2)}, u32[]{:S(2)}) async-start(s16[16,40,256]{2,1,0:T(8,128)(2,1)} %shard_map.122), calls=%async_computation.2 | async-start | bytes 655360 | tf_op jit(solution)/shard_map/all_to_all | solution.py:249
  73.3 28.5 %copy-start.2 = (bf16[8,8,4096]{2,1,0:T(8,128)(2,1)}, bf16[8,8,4096]{2,1,0:T(8,128)(2,1)S(1)}, u32[]{:S(2)}) copy-start(bf16[8,8,4096]{2,1,0:T(8,128)(2,1)S(1)} %pad_maximum_fusion.refs_0_) | copy-start | bytes 1572868
  73.3 16.6 %collective-permute-start.3 = (bf16[8,8,4096]{2,1,0:T(8,128)(2,1)S(1)}, bf16[8,8,4096]{2,1,0:T(8,128)(2,1)S(1)}, u32[]{:S(2)}, u32[]{:S(2)}) collective-permute-start(bf16[8,8,4096]{2,1,0:T(8,128)(2,1)S(1)} %pad_maximum_fusion.refs_0_), channel_id=1, source_target_pairs={{0,1},{1,2},{2,3},{3,0},{4,5},{5,6},{6,7},{7,4},{8,9},{9,10},{10,1... | collective-permute-start | bytes 1572872 | tf_op jit(solution)/shard_map/ppermute | solution.py:225
  75.3 26.5 %collective-permute-start.4 = (bf16[8,8,4096]{2,1,0:T(8,128)(2,1)S(1)}, bf16[8,8,4096]{2,1,0:T(8,128)(2,1)S(1)}, u32[]{:S(2)}, u32[]{:S(2)}) collective-permute-start(bf16[8,8,4096]{2,1,0:T(8,128)(2,1)S(1)} %pad_maximum_fusion.refs_0_), channel_id=1, source_target_pairs={{0,3},{1,0},{2,1},{3,2},{4,7},{5,4},{6,5},{7,6},{8,11},{9,8},{10,9... | collective-permute-start | bytes 1572872 | tf_op jit(solution)/shard_map/ppermute | solution.py:225
  79.8 22.0 %collective-permute-start.5 = (bf16[8,8,4096]{2,1,0:T(8,128)(2,1)S(1)}, bf16[8,8,4096]{2,1,0:T(8,128)(2,1)S(1)}, u32[]{:S(2)}, u32[]{:S(2)}) collective-permute-start(bf16[8,8,4096]{2,1,0:T(8,128)(2,1)S(1)} %pad_maximum_fusion.refs_0_), channel_id=1, source_target_pairs={{0,2},{1,3},{2,0},{3,1},{4,6},{5,7},{6,4},{7,5},{8,10},{9,11},{10,... | collective-permute-start | bytes 1572872 | tf_op jit(solution)/shard_map/ppermute | solution.py:225
  86.2 0.7 copy-start.3
  89.8 12.0 %copy-start.5 = (bf16[8,8,4096]{2,1,0:T(8,128)(2,1)}, bf16[8,8,4096]{2,1,0:T(8,128)(2,1)S(1)}, u32[]{:S(2)}) copy-start(bf16[8,8,4096]{2,1,0:T(8,128)(2,1)S(1)} %collective-permute-done.3.refs_1_) | copy-start | bytes 1572868
  101.8 0.8 copy-start.6
  101.8 1.0 copy-start.7
Sparse Core Ops, SparseCore 0:
  10.1 59.6 all-gather.2

commit v6 on v5

--- a/solution.py
+++ b/solution.py
@@ -71,14 +71,14 @@
         ones = lax.shift_right_logical(jnp.broadcast_to(value, place.shape), place) & 1
         parts.append(ones.astype(jnp.float32))
     mask_ref[...] = jnp.zeros_like(mask_ref)
-    mask_ref[:blocks] = jnp.concatenate(parts, axis=0).T
+    mask_ref[:blocks] = jnp.concatenate(parts, axis=0).T.astype(mask_ref.dtype)
 
 
 def band_mask(index, count, rows, length):
     slots, blocks = index.shape
     return pl.pallas_call(
         mask_kernel,
-        out_shape=jax.ShapeDtypeStruct((rows, length), jnp.float32),
+        out_shape=jax.ShapeDtypeStruct((rows, length), jnp.bfloat16),
         cost_estimate=pl.CostEstimate(
             flops=2 * slots * blocks * length, bytes_accessed=4 * rows * length, transcendentals=0
         ),
@@ -114,7 +114,7 @@
         in_specs=[VMEM, VMEM],
         out_specs=VMEM,
         out_shape=jax.ShapeDtypeStruct((workers, share + 8, length), jnp.int16),
-    )(total, table)
+    )(*[pltpu.with_memory_space_constraint(v, pltpu.VMEM) for v in (total, table)])
 
 
 def decode_kernel(coded_ref, update_ref):
@@ -134,7 +134,7 @@
         in_specs=[VMEM],
         out_specs=VMEM,
         out_shape=jax.ShapeDtypeStruct((rows, coded.shape[2]), jnp.float32),
-    )(coded)
+    )(pltpu.with_memory_space_constraint(coded, pltpu.VMEM))
 
 
 def product_kernel(order_ref, *refs):
@@ -228,6 +228,7 @@
     hidden = (gate_float * jax.nn.sigmoid(gate_float) * up_pre.astype(jnp.float32)).astype(
         jnp.bfloat16
     )
+    hidden = lax.optimization_barrier(hidden)
     grad_scale = 1.0 / math.sqrt(worker_rows)
     worker_grad = grad_scale * lax.dot_general(
         hidden, window_grad, (((0,), (0,)), ((), ())), preferred_element_type=jnp.float32

time: 117 us -> 115 us (0.983)
  the two profiles are of different devices: /device:TPU:1 before, /device:TPU:6 now
where the time goes in v6:
time: 115 us; the launch traced here: 114 us
  starting transfers between devices  43.7 us (38%)
  waiting for transfers between devices  36.3 us (32%)
  between operations  14.2 us (12%)
  Pallas kernels  9.06 us (8%)
  matrix products  5.66 us (5%)
  local copies, waits for them, and re-layouts  3.56 us (3%)
  other arithmetic  1.35 us (1%)
    ppermute x3, waiting for transfers between devices, per_device_body(): lax.ppermute(own_piece, 'x', [(i, (i + s) % 4) for i in range(4)])  18.1 us
    all_to_all x1, starting transfers between devices, per_device_body(): parts = lax.all_to_all(sent.reshape(workers, share, length), DP, 0, 0)  10.4 us
    all_to_all x1, starting transfers between devices, gathered(): return lax.all_to_all(copies, axis, 0, 0)  10.2 us
    ppermute x3, starting transfers between devices, per_device_body(): lax.ppermute(own_piece, 'x', [(i, (i + s) % 4) for i in range(4)])  9.17 us
    all_to_all x1, waiting for transfers between devices, per_device_body(): parts = lax.all_to_all(sent.reshape(workers, share, length), DP, 0, 0)  8.13 us
    ppermute x1, waiting for transfers between devices, gathered_over_y(): second = lax.ppermute(pair, 'y', links)  6.79 us
    all_to_all x1, starting transfers between devices, per_device_body(): arrived = lax.all_to_all(coded, DP, 0, 0)  5.75 us
    pallas_call x1, Pallas kernels, product(): pl.pallas_call(product_kernel, grid_spec=pltpu.PrefetchScalarGridSpec(num...  5.45 us
  transfers between devices with their start and end apart: 10, of which 5 were waited for; matrix products, arithmetic and copies ran while one was open for 8% of the time, Pallas kernels for 3%

profile of v6, /device:TPU:6, one launch (start us, length us, event | category | flops | bytes accessed | tf_op | source)
XLA Modules:
  0.0 113.8 jit_solution(13142404039430667567)
XLA Ops:
  9.3 10.2 %all-to-all-start = ((bf16[32,8,256]{2,1,0:T(8,128)(2,1)}), bf16[32,8,256]{2,1,0:T(8,128)(2,1)S(1)}, u32[]{:S(2)}, u32[]{:S(2)}) async-start(bf16[32,8,256]{2,1,0:T(8,128)(2,1)} %broadcast_in_dim.13), calls=%async_computation | async-start | bytes 262144 | tf_op jit(solution)/shard_map/all_to_all | solution.py:29
  19.5 3.4 %collective-permute-start = (bf16[8,4096]{1,0:T(8,128)(2,1)}, bf16[8,4096]{1,0:T(8,128)(2,1)S(1)}, u32[]{:S(2)}, u32[]{:S(2)}) collective-permute-start(bf16[8,4096]{1,0:T(8,128)(2,1)} %param.9), channel_id=1, source_target_pairs={{0,4},{4,0},{8,12},{12,8},{16,20},{20,16},{24,28},{28,24},{1,5},{5... | collective-permute-start | bytes 196616 | tf_op jit(solution)/shard_map/ppermute | solution.py:33
  22.9 1.2 %fusion.8 = bf16[256,464]{0,1:T(8,128)(2,1)S(1)} fusion(bf16[256,464]{0,1:T(8,128)(2,1)} %param.11, bf16[256,464]{0,1:T(8,128)(2,1)} %param.10), kind=kLoop, calls=%fused_computation.14 | loop fusion | flops 950272 | bytes 712704 | tf_op jit(solution)/shard_map/convert_element_type | solution.py:228
  24.1 1.8 %shard_map.121 = bf16[512,256]{1,0:T(8,128)(2,1)} custom-call(s32[32,464]{1,0:T(8,128)} %bitcast.32, s32[1,464]{1,0:T(1,128)} %count_ref.1), custom_call_target="tpu_custom_call" | custom-call | flops 7602176 | bytes 524288 | tf_op jit(solution)/shard_map/pallas_call | solution.py:79
  25.9 2.6 %all-to-all-done = bf16[32,8,256]{2,1,0:T(8,128)(2,1)S(1)} async-done(((bf16[32,8,256]{2,1,0:T(8,128)(2,1)}), bf16[32,8,256]{2,1,0:T(8,128)(2,1)S(1)}, u32[]{:S(2)}, u32[]{:S(2)}) %all-to-all-start) | async-done | bytes 131104 | tf_op jit(solution)/shard_map/all_to_all | solution.py:29
  28.5 1.2 %fusion = f32[464,256]{1,0:T(8,128)S(1)} fusion(bf16[256,464]{0,1:T(8,128)(2,1)S(1)} %fusion.8, f32[1,464,256]{2,1,0:T(8,128)} %param.13, bf16[32,8,256]{2,1,0:T(8,128)(2,1)S(1)} %all-to-all-done), kind=kOutput, calls=%fused_computation.2 | convolution fusion | flops 61173760 | bytes 1318912 | tf_op jit(solution)/shard_map/dot_general | solution.py:233
  29.7 2.3 %convolution_select_fusion = f32[512,256]{1,0:T(8,128)} fusion(f32[256,256]{1,0:T(8,128)} %constant.31.clone.table_ref, f32[464,256]{1,0:T(8,128)S(1)} %fusion, bf16[512,256]{1,0:T(8,128)(2,1)} %shard_map.121), kind=kOutput, calls=%fused_computation | convolution fusion | flops 201588736 | bytes 1523712 | tf_op jit(solution)/shard_map/dot_general | solution.py:244
  32.0 10.4 %all-to-all-start.1 = ((f32[16,32,256]{2,1,0:T(8,128)}), f32[16,32,256]{2,1,0:T(8,128)S(1)}, u32[]{:S(2)}, u32[]{:S(2)}) async-start(f32[16,32,256]{2,1,0:T(8,128)} %bitcast.13), calls=%async_computation.1 | async-start | bytes 1048576 | tf_op jit(solution)/shard_map/all_to_all | solution.py:248
  42.5 2.1 %collective-permute-start.1 = (bf16[2,8,4096]{2,1,0:T(8,128)(2,1)S(1)}, bf16[2,8,4096]{2,1,0:T(8,128)(2,1)S(1)}, u32[]{:S(2)}, u32[]{:S(2)}) collective-permute-start(bf16[2,8,4096]{2,1,0:T(8,128)(2,1)S(1)} %pad_maximum_fusion.2), channel_id=1, source_target_pairs={{0,28},{4,8},{8,4},{12,16},{16,12},{20,24},{24,20},{28,0},{1,29},{... | collective-permute-start | bytes 393224 | tf_op jit(solution)/shard_map/ppermute | solution.py:36
  44.6 6.8 %collective-permute-done.1 = bf16[2,8,4096]{2,1,0:T(8,128)(2,1)S(1)} collective-permute-done((bf16[2,8,4096]{2,1,0:T(8,128)(2,1)S(1)}, bf16[2,8,4096]{2,1,0:T(8,128)(2,1)S(1)}, u32[]{:S(2)}, u32[]{:S(2)}) %collective-permute-start.1) | collective-permute-done | bytes 131104 | tf_op jit(solution)/shard_map/ppermute | solution.py:36
  51.4 2.6 %collective-permute-start.2 = (bf16[4,8,4096]{2,1,0:T(8,128)(2,1)S(1)}, bf16[4,8,4096]{2,1,0:T(8,128)(2,1)S(1)}, u32[]{:S(2)}, u32[]{:S(2)}) collective-permute-start(bf16[4,8,4096]{2,1,0:T(8,128)(2,1)S(1)} %pad_maximum_fusion.1), channel_id=1, source_target_pairs={{0,12},{4,24},{8,20},{12,0},{16,28},{20,8},{24,4},{28,16},{1,13},{... | collective-permute-start | bytes 786440 | tf_op jit(solution)/shard_map/ppermute | solution.py:39
  54.0 8.1 %all-to-all-done.1 = f32[16,32,256]{2,1,0:T(8,128)S(1)} async-done(((f32[16,32,256]{2,1,0:T(8,128)}), f32[16,32,256]{2,1,0:T(8,128)S(1)}, u32[]{:S(2)}, u32[]{:S(2)}) %all-to-all-start.1) | async-done | bytes 524320 | tf_op jit(solution)/shard_map/all_to_all | solution.py:248
  62.2 1.0 shard_map.122
  63.2 5.7 %all-to-all-start.2 = ((s16[16,40,256]{2,1,0:T(8,128)(2,1)}), s16[16,40,256]{2,1,0:T(8,128)(2,1)S(1)}, u32[]{:S(2)}, u32[]{:S(2)}) async-start(s16[16,40,256]{2,1,0:T(8,128)(2,1)} %shard_map.122), calls=%async_computation.2 | async-start | bytes 655360 | tf_op jit(solution)/shard_map/all_to_all | solution.py:250
  69.0 3.5 %collective-permute-start.3 = (bf16[8,8,4096]{2,1,0:T(8,128)(2,1)S(1)}, bf16[8,8,4096]{2,1,0:T(8,128)(2,1)S(1)}, u32[]{:S(2)}, u32[]{:S(2)}) collective-permute-start(bf16[8,8,4096]{2,1,0:T(8,128)(2,1)S(1)} %pad_maximum_fusion.refs_0_), channel_id=1, source_target_pairs={{0,1},{1,2},{2,3},{3,0},{4,5},{5,6},{6,7},{7,4},{8,9},{9,10},{10,1... | collective-permute-start | bytes 1572872 | tf_op jit(solution)/shard_map/ppermute | solution.py:225
  72.5 2.3 %collective-permute-start.4 = (bf16[8,8,4096]{2,1,0:T(8,128)(2,1)S(1)}, bf16[8,8,4096]{2,1,0:T(8,128)(2,1)S(1)}, u32[]{:S(2)}, u32[]{:S(2)}) collective-permute-start(bf16[8,8,4096]{2,1,0:T(8,128)(2,1)S(1)} %pad_maximum_fusion.refs_0_), channel_id=1, source_target_pairs={{0,3},{1,0},{2,1},{3,2},{4,7},{5,4},{6,5},{7,6},{8,11},{9,8},{10,9... | collective-permute-start | bytes 1572872 | tf_op jit(solution)/shard_map/ppermute | solution.py:225
  74.9 3.3 %collective-permute-start.5 = (bf16[8,8,4096]{2,1,0:T(8,128)(2,1)S(1)}, bf16[8,8,4096]{2,1,0:T(8,128)(2,1)S(1)}, u32[]{:S(2)}, u32[]{:S(2)}) collective-permute-start(bf16[8,8,4096]{2,1,0:T(8,128)(2,1)S(1)} %pad_maximum_fusion.refs_0_), channel_id=1, source_target_pairs={{0,2},{1,3},{2,0},{3,1},{4,6},{5,7},{6,4},{7,5},{8,10},{9,11},{10,... | collective-permute-start | bytes 1572872 | tf_op jit(solution)/shard_map/ppermute | solution.py:225
  78.2 1.2 %dynamic-slice_bitcast_fusion.order_ref = s32[12]{0:T(128)} fusion(s32[32,12]{1,0:T(8,128)} %constant.30.clone, s32[]{:T(128)S(6)} %select_n.7), kind=kLoop, calls=%fused_computation.18 | loop fusion | bytes 100 | tf_op jit(solution)/shard_map/squeeze | solution.py:57
  79.5 2.2 %fusion.1 = f32[1,464,256]{2,1,0:T(8,128)} fusion(f32[464,256]{1,0:T(8,128)S(1)} %fusion, f32[256,256]{1,0:T(8,128)S(1)} %copy-done, f32[512,256]{1,0:T(8,128)} %convolution_select_fusion), kind=kOutput, calls=%fused_computation.4 | convolution fusion | flops 182571008 | bytes 1687552 | tf_op jit(solution)/shard_map/dot_general | solution.py:246
  81.6 0.8 shard_map.123
  82.5 3.2 %collective-permute-done.3.refs_1_ = bf16[8,8,4096]{2,1,0:T(8,128)(2,1)S(1)} collective-permute-done((bf16[8,8,4096]{2,1,0:T(8,128)(2,1)S(1)}, bf16[8,8,4096]{2,1,0:T(8,128)(2,1)S(1)}, u32[]{:S(2)}, u32[]{:S(2)}) %collective-permute-start.3) | collective-permute-done | bytes 524320 | tf_op jit(solution)/shard_map/ppermute | solution.py:225
  85.7 14.8 %collective-permute-done.4.refs_2_ = bf16[8,8,4096]{2,1,0:T(8,128)(2,1)S(1)} collective-permute-done((bf16[8,8,4096]{2,1,0:T(8,128)(2,1)S(1)}, bf16[8,8,4096]{2,1,0:T(8,128)(2,1)S(1)}, u32[]{:S(2)}, u32[]{:S(2)}) %collective-permute-start.4) | collective-permute-done | bytes 524320 | tf_op jit(solution)/shard_map/ppermute | solution.py:225
  100.6 0.7 copy-done.4
  101.5 5.4 %shard_map.120 = (bf16[464,256]{1,0:T(8,128)(2,1)}, bf16[464,256]{1,0:T(8,128)(2,1)}) custom-call(s32[12]{0:T(128)} %dynamic-slice_bitcast_fusion.order_ref, bf16[8,8,4096]{2,1,0:T(8,128)(2,1)} %copy-done.1, bf16[8,8,4096]{2,1,0:T(8,128)(2,1)} %copy-done.3, bf16[8,8,4096]{2,1,0:T(8,128)(2,1)} %copy-done.4, bf16[8,8,4096]{2,1,0:T(8,128)(2,1)} %copy-done.5, ...), custom_call_target="tpu_custom_call" | custom-call | flops 973078528 | bytes 6848512 | tf_op jit(solution)/shard_map/pallas_call | solution.py:190
  (24 shorter events, 2.5 us)
Async XLA Ops:
  7.2 55.0 %copy-start = (f32[256,256]{1,0:T(8,128)S(1)}, f32[256,256]{1,0:T(8,128)}, u32[]{:S(2)}) copy-start(f32[256,256]{1,0:T(8,128)} %constant.31.clone.table_ref) | copy-start | bytes 786436
  7.2 35.3 %copy-start.2 = (bf16[8,4096]{1,0:T(8,128)(2,1)S(1)}, bf16[8,4096]{1,0:T(8,128)(2,1)}, u32[]{:S(2)}) copy-start(bf16[8,4096]{1,0:T(8,128)(2,1)} %param.9) | copy-start | bytes 196612
  7.2 93.4 %all-gather.3.cloned.1.call-start = ((), (), s32[]{:S(2)}) async-start(), calls=%async_computation.3 | async-start | bytes 4038656 | tf_op jit(solution)/shard_map/all_gather | solution.py:220
  9.3 19.2 %all-to-all-start = ((bf16[32,8,256]{2,1,0:T(8,128)(2,1)}), bf16[32,8,256]{2,1,0:T(8,128)(2,1)S(1)}, u32[]{:S(2)}, u32[]{:S(2)}) async-start(bf16[32,8,256]{2,1,0:T(8,128)(2,1)} %broadcast_in_dim.13), calls=%async_computation | async-start | bytes 262144 | tf_op jit(solution)/shard_map/all_to_all | solution.py:29
  19.5 22.9 %collective-permute-start = (bf16[8,4096]{1,0:T(8,128)(2,1)}, bf16[8,4096]{1,0:T(8,128)(2,1)S(1)}, u32[]{:S(2)}, u32[]{:S(2)}) collective-permute-start(bf16[8,4096]{1,0:T(8,128)(2,1)} %param.9), channel_id=1, source_target_pairs={{0,4},{4,0},{8,12},{12,8},{16,20},{20,16},{24,28},{28,24},{1,5},{5... | collective-permute-start | bytes 196616 | tf_op jit(solution)/shard_map/ppermute | solution.py:33
  32.0 30.2 %all-to-all-start.1 = ((f32[16,32,256]{2,1,0:T(8,128)}), f32[16,32,256]{2,1,0:T(8,128)S(1)}, u32[]{:S(2)}, u32[]{:S(2)}) async-start(f32[16,32,256]{2,1,0:T(8,128)} %bitcast.13), calls=%async_computation.1 | async-start | bytes 1048576 | tf_op jit(solution)/shard_map/all_to_all | solution.py:248
  42.5 8.9 %collective-permute-start.1 = (bf16[2,8,4096]{2,1,0:T(8,128)(2,1)S(1)}, bf16[2,8,4096]{2,1,0:T(8,128)(2,1)S(1)}, u32[]{:S(2)}, u32[]{:S(2)}) collective-permute-start(bf16[2,8,4096]{2,1,0:T(8,128)(2,1)S(1)} %pad_maximum_fusion.2), channel_id=1, source_target_pairs={{0,28},{4,8},{8,4},{12,16},{16,12},{20,24},{24,20},{28,0},{1,29},{... | collective-permute-start | bytes 393224 | tf_op jit(solution)/shard_map/ppermute | solution.py:36
  51.4 17.6 %collective-permute-start.2 = (bf16[4,8,4096]{2,1,0:T(8,128)(2,1)S(1)}, bf16[4,8,4096]{2,1,0:T(8,128)(2,1)S(1)}, u32[]{:S(2)}, u32[]{:S(2)}) collective-permute-start(bf16[4,8,4096]{2,1,0:T(8,128)(2,1)S(1)} %pad_maximum_fusion.1), channel_id=1, source_target_pairs={{0,12},{4,24},{8,20},{12,0},{16,28},{20,8},{24,4},{28,16},{1,13},{... | collective-permute-start | bytes 786440 | tf_op jit(solution)/shard_map/ppermute | solution.py:39
  63.2 18.4 %all-to-all-start.2 = ((s16[16,40,256]{2,1,0:T(8,128)(2,1)}), s16[16,40,256]{2,1,0:T(8,128)(2,1)S(1)}, u32[]{:S(2)}, u32[]{:S(2)}) async-start(s16[16,40,256]{2,1,0:T(8,128)(2,1)} %shard_map.122), calls=%async_computation.2 | async-start | bytes 655360 | tf_op jit(solution)/shard_map/all_to_all | solution.py:250
  69.0 31.5 %copy-start.1 = (bf16[8,8,4096]{2,1,0:T(8,128)(2,1)}, bf16[8,8,4096]{2,1,0:T(8,128)(2,1)S(1)}, u32[]{:S(2)}) copy-start(bf16[8,8,4096]{2,1,0:T(8,128)(2,1)S(1)} %pad_maximum_fusion.refs_0_) | copy-start | bytes 1572868
  69.0 16.7 %collective-permute-start.3 = (bf16[8,8,4096]{2,1,0:T(8,128)(2,1)S(1)}, bf16[8,8,4096]{2,1,0:T(8,128)(2,1)S(1)}, u32[]{:S(2)}, u32[]{:S(2)}) collective-permute-start(bf16[8,8,4096]{2,1,0:T(8,128)(2,1)S(1)} %pad_maximum_fusion.refs_0_), channel_id=1, source_target_pairs={{0,1},{1,2},{2,3},{3,0},{4,5},{5,6},{6,7},{7,4},{8,9},{9,10},{10,1... | collective-permute-start | bytes 1572872 | tf_op jit(solution)/shard_map/ppermute | solution.py:225
  72.5 28.0 %collective-permute-start.4 = (bf16[8,8,4096]{2,1,0:T(8,128)(2,1)S(1)}, bf16[8,8,4096]{2,1,0:T(8,128)(2,1)S(1)}, u32[]{:S(2)}, u32[]{:S(2)}) collective-permute-start(bf16[8,8,4096]{2,1,0:T(8,128)(2,1)S(1)} %pad_maximum_fusion.refs_0_), channel_id=1, source_target_pairs={{0,3},{1,0},{2,1},{3,2},{4,7},{5,4},{6,5},{7,6},{8,11},{9,8},{10,9... | collective-permute-start | bytes 1572872 | tf_op jit(solution)/shard_map/ppermute | solution.py:225
  74.9 25.6 %collective-permute-start.5 = (bf16[8,8,4096]{2,1,0:T(8,128)(2,1)S(1)}, bf16[8,8,4096]{2,1,0:T(8,128)(2,1)S(1)}, u32[]{:S(2)}, u32[]{:S(2)}) collective-permute-start(bf16[8,8,4096]{2,1,0:T(8,128)(2,1)S(1)} %pad_maximum_fusion.refs_0_), channel_id=1, source_target_pairs={{0,2},{1,3},{2,0},{3,1},{4,6},{5,7},{6,4},{7,5},{8,10},{9,11},{10,... | collective-permute-start | bytes 1572872 | tf_op jit(solution)/shard_map/ppermute | solution.py:225
  85.7 14.9 %copy-start.3 = (bf16[8,8,4096]{2,1,0:T(8,128)(2,1)}, bf16[8,8,4096]{2,1,0:T(8,128)(2,1)S(1)}, u32[]{:S(2)}) copy-start(bf16[8,8,4096]{2,1,0:T(8,128)(2,1)S(1)} %collective-permute-done.3.refs_1_) | copy-start | bytes 1572868
  100.5 0.8 copy-start.4
  100.5 1.0 copy-start.5
Sparse Core Ops, SparseCore 0:
  10.1 58.3 all-gather.2

commit v7 on v6

--- a/solution.py
+++ b/solution.py
@@ -13,6 +13,7 @@
 DP = ("z", "core")
 FSDP = ("y", "x")
 momentum_decay = 0.9
+VMEM = pl.BlockSpec(memory_space=pltpu.VMEM)
 SHIFTS = (0, 1, 3, 2)
 
 
@@ -78,7 +79,8 @@
     slots, blocks = index.shape
     return pl.pallas_call(
         mask_kernel,
-        out_shape=jax.ShapeDtypeStruct((rows, length), jnp.bfloat16),
+        out_specs=VMEM,
+        out_shape=pltpu.VMEM((rows, length), jnp.float32),
         cost_estimate=pl.CostEstimate(
             flops=2 * slots * blocks * length, bytes_accessed=4 * rows * length, transcendentals=0
         ),
@@ -86,7 +88,6 @@
 
 
 STEPS = 16384.0
-VMEM = pl.BlockSpec(memory_space=pltpu.VMEM)
 
 
 def update_kernel(total_ref, table_ref, coded_ref):
@@ -150,9 +151,11 @@
         act_ref[...] = gate * sigmoid
         slope_ref[...] = up_ref[...].astype(jnp.float32) * sigmoid * (1.0 + gate * (1.0 - sigmoid))
 
+    depth = rows_ref.shape[3]
+    columns = pl.ds(pl.multiple_of(step * depth, depth), depth)
     for i, piece in enumerate(pieces):
         for j in range(piece.shape[0]):
-            rows_ref[order_ref[4 + j], order_ref[i]] = piece[j]
+            rows_ref[order_ref[4 + j], order_ref[i]] = piece[j, :, columns]
     width = weight_ref.shape[2]
     rows = rows_ref[...].reshape(-1, rows_ref.shape[3])
     total = None
@@ -186,13 +189,13 @@
     groups, depth, features = pieces[0].shape
     per_step = blocks // 2
     whole = pl.BlockSpec((rows, tokens), lambda k, order: (0, 0))
-    piece = pl.BlockSpec((groups, depth, per_step * width), lambda k, order: (0, 0, k))
+    pieces = [pltpu.with_memory_space_constraint(piece, pltpu.VMEM) for piece in pieces]
     return pl.pallas_call(
         product_kernel,
         grid_spec=pltpu.PrefetchScalarGridSpec(
             num_scalar_prefetch=1,
             grid=(blocks // per_step,),
-            in_specs=[piece] * 4
+            in_specs=[VMEM] * 4
             + [pl.BlockSpec((per_step, rows, width), lambda k, order: (k, 0, 0)), whole, whole],
             out_specs=[whole, whole],
             scratch_shapes=[pltpu.VMEM((rows, tokens), jnp.float32)] * 3

time: 115 us -> 113 us (0.983)
  the two profiles are of different devices: /device:TPU:6 before, /device:TPU:1 now
where the time goes in v7:
time: 113 us; the launch traced here: 111 us
  starting transfers between devices  43.3 us (38%)
  waiting for transfers between devices  36 us (32%)
  between operations  14.2 us (13%)
  Pallas kernels  7.82 us (7%)
  matrix products  5.67 us (5%)
  local copies, waits for them, and re-layouts  2.57 us (2%)
  other arithmetic  1.35 us (1%)
    ppermute x3, waiting for transfers between devices, per_device_body(): lax.ppermute(own_piece, 'x', [(i, (i + s) % 4) for i in range(4)])  14.2 us
    all_to_all x1, starting transfers between devices, per_device_body(): parts = lax.all_to_all(sent.reshape(workers, share, length), DP, 0, 0)  12.6 us
    all_to_all x1, waiting for transfers between devices, per_device_body(): parts = lax.all_to_all(sent.reshape(workers, share, length), DP, 0, 0)  10.7 us
    all_to_all x1, starting transfers between devices, gathered(): return lax.all_to_all(copies, axis, 0, 0)  10.5 us
    ppermute x3, starting transfers between devices, per_device_body(): lax.ppermute(own_piece, 'x', [(i, (i + s) % 4) for i in range(4)])  9.01 us
    ppermute x1, waiting for transfers between devices, gathered_over_y(): second = lax.ppermute(pair, 'y', links)  6.01 us
    pallas_call x1, Pallas kernels, product(): pl.pallas_call(product_kernel, grid_spec=pltpu.PrefetchScalarGridSpec(num...  4.92 us
    all_to_all x1, waiting for transfers between devices, gathered(): return lax.all_to_all(copies, axis, 0, 0)  3.92 us
  transfers between devices with their start and end apart: 10, of which 7 were waited for; matrix products, arithmetic and copies ran while one was open for 9% of the time, Pallas kernels for 3%

profile of v7, /device:TPU:1, one launch (start us, length us, event | category | flops | bytes accessed | tf_op | source)
XLA Modules:
  0.0 110.8 jit_solution(2354975284174149281)
XLA Ops:
  9.3 10.5 %all-to-all-start = ((bf16[32,8,256]{2,1,0:T(8,128)(2,1)}), bf16[32,8,256]{2,1,0:T(8,128)(2,1)S(1)}, u32[]{:S(2)}, u32[]{:S(2)}) async-start(bf16[32,8,256]{2,1,0:T(8,128)(2,1)} %broadcast_in_dim.6), calls=%async_computation | async-start | bytes 262144 | tf_op jit(solution)/shard_map/all_to_all | solution.py:30
  19.8 3.1 %collective-permute-start = (bf16[8,4096]{1,0:T(8,128)(2,1)}, bf16[8,4096]{1,0:T(8,128)(2,1)S(1)}, u32[]{:S(2)}, u32[]{:S(2)}) collective-permute-start(bf16[8,4096]{1,0:T(8,128)(2,1)} %param.9), channel_id=1, source_target_pairs={{0,4},{4,0},{8,12},{12,8},{16,20},{20,16},{24,28},{28,24},{1,5},{5... | collective-permute-start | bytes 196616 | tf_op jit(solution)/shard_map/ppermute | solution.py:34
  22.9 1.2 %fusion.8 = bf16[256,464]{0,1:T(8,128)(2,1)S(1)} fusion(bf16[256,464]{0,1:T(8,128)(2,1)} %param.11, bf16[256,464]{0,1:T(8,128)(2,1)} %param.10), kind=kLoop, calls=%fused_computation.14 | loop fusion | flops 950272 | bytes 712704 | tf_op jit(solution)/shard_map/convert_element_type | solution.py:231
  24.1 1.1 shard_map.121
  25.2 3.9 %all-to-all-done = bf16[32,8,256]{2,1,0:T(8,128)(2,1)S(1)} async-done(((bf16[32,8,256]{2,1,0:T(8,128)(2,1)}), bf16[32,8,256]{2,1,0:T(8,128)(2,1)S(1)}, u32[]{:S(2)}, u32[]{:S(2)}) %all-to-all-start) | async-done | bytes 131104 | tf_op jit(solution)/shard_map/all_to_all | solution.py:30
  29.1 1.3 %fusion = f32[464,256]{1,0:T(8,128)S(1)} fusion(bf16[256,464]{0,1:T(8,128)(2,1)S(1)} %fusion.8, f32[1,464,256]{2,1,0:T(8,128)} %param.13, bf16[32,8,256]{2,1,0:T(8,128)(2,1)S(1)} %all-to-all-done), kind=kOutput, calls=%fused_computation.2 | convolution fusion | flops 61173760 | bytes 1318912 | tf_op jit(solution)/shard_map/dot_general | solution.py:236
  30.5 2.2 %convolution_select_fusion = f32[512,256]{1,0:T(8,128)} fusion(f32[256,256]{1,0:T(8,128)} %constant.30.clone.table_ref, f32[464,256]{1,0:T(8,128)S(1)} %fusion, f32[512,256]{1,0:T(8,128)S(1)} %shard_map.121), kind=kOutput, calls=%fused_computation | convolution fusion | flops 201588736 | bytes 1785856 | tf_op jit(solution)/shard_map/dot_general | solution.py:247
  32.6 12.6 %all-to-all-start.1 = ((f32[16,32,256]{2,1,0:T(8,128)}), f32[16,32,256]{2,1,0:T(8,128)S(1)}, u32[]{:S(2)}, u32[]{:S(2)}) async-start(f32[16,32,256]{2,1,0:T(8,128)} %bitcast.13), calls=%async_computation.1 | async-start | bytes 1048576 | tf_op jit(solution)/shard_map/all_to_all | solution.py:251
  45.3 2.1 %collective-permute-start.1 = (bf16[2,8,4096]{2,1,0:T(8,128)(2,1)S(1)}, bf16[2,8,4096]{2,1,0:T(8,128)(2,1)S(1)}, u32[]{:S(2)}, u32[]{:S(2)}) collective-permute-start(bf16[2,8,4096]{2,1,0:T(8,128)(2,1)S(1)} %pad_maximum_fusion.2), channel_id=1, source_target_pairs={{0,28},{4,8},{8,4},{12,16},{16,12},{20,24},{24,20},{28,0},{1,29},{... | collective-permute-start | bytes 393224 | tf_op jit(solution)/shard_map/ppermute | solution.py:37
  47.4 6.0 %collective-permute-done.1 = bf16[2,8,4096]{2,1,0:T(8,128)(2,1)S(1)} collective-permute-done((bf16[2,8,4096]{2,1,0:T(8,128)(2,1)S(1)}, bf16[2,8,4096]{2,1,0:T(8,128)(2,1)S(1)}, u32[]{:S(2)}, u32[]{:S(2)}) %collective-permute-start.1) | collective-permute-done | bytes 131104 | tf_op jit(solution)/shard_map/ppermute | solution.py:37
  53.4 2.5 %collective-permute-start.2 = (bf16[4,8,4096]{2,1,0:T(8,128)(2,1)S(1)}, bf16[4,8,4096]{2,1,0:T(8,128)(2,1)S(1)}, u32[]{:S(2)}, u32[]{:S(2)}) collective-permute-start(bf16[4,8,4096]{2,1,0:T(8,128)(2,1)S(1)} %pad_maximum_fusion.1), channel_id=1, source_target_pairs={{0,12},{4,24},{8,20},{12,0},{16,28},{20,8},{24,4},{28,16},{1,13},{... | collective-permute-start | bytes 786440 | tf_op jit(solution)/shard_map/ppermute | solution.py:40
  55.9 10.7 %all-to-all-done.1 = f32[16,32,256]{2,1,0:T(8,128)S(1)} async-done(((f32[16,32,256]{2,1,0:T(8,128)}), f32[16,32,256]{2,1,0:T(8,128)S(1)}, u32[]{:S(2)}, u32[]{:S(2)}) %all-to-all-start.1) | async-done | bytes 524320 | tf_op jit(solution)/shard_map/all_to_all | solution.py:251
  66.6 1.0 shard_map.122
  67.6 3.4 %all-to-all-start.2 = ((s16[16,40,256]{2,1,0:T(8,128)(2,1)}), s16[16,40,256]{2,1,0:T(8,128)(2,1)S(1)}, u32[]{:S(2)}, u32[]{:S(2)}) async-start(s16[16,40,256]{2,1,0:T(8,128)(2,1)} %shard_map.122), calls=%async_computation.2 | async-start | bytes 655360 | tf_op jit(solution)/shard_map/all_to_all | solution.py:253
  71.2 2.2 %collective-permute-start.3 = (bf16[8,8,4096]{2,1,0:T(8,128)(2,1)S(1)}, bf16[8,8,4096]{2,1,0:T(8,128)(2,1)S(1)}, u32[]{:S(2)}, u32[]{:S(2)}) collective-permute-start(bf16[8,8,4096]{2,1,0:T(8,128)(2,1)S(1)} %pad_maximum_fusion.refs_0_), channel_id=1, source_target_pairs={{0,1},{1,2},{2,3},{3,0},{4,5},{5,6},{6,7},{7,4},{8,9},{9,10},{10,1... | collective-permute-start | bytes 1572872 | tf_op jit(solution)/shard_map/ppermute | solution.py:228
  73.4 4.3 %collective-permute-start.4 = (bf16[8,8,4096]{2,1,0:T(8,128)(2,1)S(1)}, bf16[8,8,4096]{2,1,0:T(8,128)(2,1)S(1)}, u32[]{:S(2)}, u32[]{:S(2)}) collective-permute-start(bf16[8,8,4096]{2,1,0:T(8,128)(2,1)S(1)} %pad_maximum_fusion.refs_0_), channel_id=1, source_target_pairs={{0,3},{1,0},{2,1},{3,2},{4,7},{5,4},{6,5},{7,6},{8,11},{9,8},{10,9... | collective-permute-start | bytes 1572872 | tf_op jit(solution)/shard_map/ppermute | solution.py:228
  77.7 2.5 %collective-permute-start.5 = (bf16[8,8,4096]{2,1,0:T(8,128)(2,1)S(1)}, bf16[8,8,4096]{2,1,0:T(8,128)(2,1)S(1)}, u32[]{:S(2)}, u32[]{:S(2)}) collective-permute-start(bf16[8,8,4096]{2,1,0:T(8,128)(2,1)S(1)} %pad_maximum_fusion.refs_0_), channel_id=1, source_target_pairs={{0,2},{1,3},{2,0},{3,1},{4,6},{5,7},{6,4},{7,5},{8,10},{9,11},{10,... | collective-permute-start | bytes 1572872 | tf_op jit(solution)/shard_map/ppermute | solution.py:228
  80.2 1.2 %dynamic-slice_bitcast_fusion.order_ref = s32[12]{0:T(128)} fusion(s32[32,12]{1,0:T(8,128)} %constant.29.clone, s32[]{:T(128)S(6)} %select_n.7), kind=kLoop, calls=%fused_computation.18 | loop fusion | bytes 100 | tf_op jit(solution)/shard_map/squeeze | solution.py:58
  81.4 2.2 %fusion.1 = f32[1,464,256]{2,1,0:T(8,128)} fusion(f32[464,256]{1,0:T(8,128)S(1)} %fusion, f32[256,256]{1,0:T(8,128)S(1)} %copy-done, f32[512,256]{1,0:T(8,128)} %convolution_select_fusion), kind=kOutput, calls=%fused_computation.4 | convolution fusion | flops 182571008 | bytes 1687552 | tf_op jit(solution)/shard_map/dot_general | solution.py:249
  84.0 0.8 shard_map.123
  84.9 2.5 %collective-permute-done.3.refs_1_ = bf16[8,8,4096]{2,1,0:T(8,128)(2,1)S(1)} collective-permute-done((bf16[8,8,4096]{2,1,0:T(8,128)(2,1)S(1)}, bf16[8,8,4096]{2,1,0:T(8,128)(2,1)S(1)}, u32[]{:S(2)}, u32[]{:S(2)}) %collective-permute-start.3) | collective-permute-done | bytes 524320 | tf_op jit(solution)/shard_map/ppermute | solution.py:228
  87.4 1.3 %collective-permute-done.4.refs_2_ = bf16[8,8,4096]{2,1,0:T(8,128)(2,1)S(1)} collective-permute-done((bf16[8,8,4096]{2,1,0:T(8,128)(2,1)S(1)}, bf16[8,8,4096]{2,1,0:T(8,128)(2,1)S(1)}, u32[]{:S(2)}, u32[]{:S(2)}) %collective-permute-start.4) | collective-permute-done | bytes 524320 | tf_op jit(solution)/shard_map/ppermute | solution.py:228
  88.7 10.4 %collective-permute-done.5.refs_3_ = bf16[8,8,4096]{2,1,0:T(8,128)(2,1)S(1)} collective-permute-done((bf16[8,8,4096]{2,1,0:T(8,128)(2,1)S(1)}, bf16[8,8,4096]{2,1,0:T(8,128)(2,1)S(1)}, u32[]{:S(2)}, u32[]{:S(2)}) %collective-permute-start.5) | collective-permute-done | bytes 524320 | tf_op jit(solution)/shard_map/ppermute | solution.py:228
  99.1 4.9 %shard_map.120 = (bf16[464,256]{1,0:T(8,128)(2,1)}, bf16[464,256]{1,0:T(8,128)(2,1)}) custom-call(s32[12]{0:T(128)} %dynamic-slice_bitcast_fusion.order_ref, bf16[8,8,4096]{2,1,0:T(8,128)(2,1)S(1)} %pad_maximum_fusion.refs_0_, bf16[8,8,4096]{2,1,0:T(8,128)(2,1)S(1)} %collective-permute-done.3.refs_1_, ...), custom_call_target="tpu_custom_call" | custom-call | flops 973078528 | bytes 6848512 | tf_op jit(solution)/shard_map/pallas_call | solution.py:193
  (16 shorter events, 2.7 us)
Async XLA Ops:
  7.2 59.5 %copy-start = (f32[256,256]{1,0:T(8,128)S(1)}, f32[256,256]{1,0:T(8,128)}, u32[]{:S(2)}) copy-start(f32[256,256]{1,0:T(8,128)} %constant.30.clone.table_ref) | copy-start | bytes 786436
  7.2 38.0 %copy-start.1 = (bf16[8,4096]{1,0:T(8,128)(2,1)S(1)}, bf16[8,4096]{1,0:T(8,128)(2,1)}, u32[]{:S(2)}) copy-start(bf16[8,4096]{1,0:T(8,128)(2,1)} %param.9) | copy-start | bytes 196612
  7.2 91.9 %all-gather.3.cloned.1.call-start = ((), (), s32[]{:S(2)}) async-start(), calls=%async_computation.3 | async-start | bytes 4038656 | tf_op jit(solution)/shard_map/all_gather | solution.py:223
  9.3 19.8 %all-to-all-start = ((bf16[32,8,256]{2,1,0:T(8,128)(2,1)}), bf16[32,8,256]{2,1,0:T(8,128)(2,1)S(1)}, u32[]{:S(2)}, u32[]{:S(2)}) async-start(bf16[32,8,256]{2,1,0:T(8,128)(2,1)} %broadcast_in_dim.6), calls=%async_computation | async-start | bytes 262144 | tf_op jit(solution)/shard_map/all_to_all | solution.py:30
  19.8 25.4 %collective-permute-start = (bf16[8,4096]{1,0:T(8,128)(2,1)}, bf16[8,4096]{1,0:T(8,128)(2,1)S(1)}, u32[]{:S(2)}, u32[]{:S(2)}) collective-permute-start(bf16[8,4096]{1,0:T(8,128)(2,1)} %param.9), channel_id=1, source_target_pairs={{0,4},{4,0},{8,12},{12,8},{16,20},{20,16},{24,28},{28,24},{1,5},{5... | collective-permute-start | bytes 196616 | tf_op jit(solution)/shard_map/ppermute | solution.py:34
  32.6 34.0 %all-to-all-start.1 = ((f32[16,32,256]{2,1,0:T(8,128)}), f32[16,32,256]{2,1,0:T(8,128)S(1)}, u32[]{:S(2)}, u32[]{:S(2)}) async-start(f32[16,32,256]{2,1,0:T(8,128)} %bitcast.13), calls=%async_computation.1 | async-start | bytes 1048576 | tf_op jit(solution)/shard_map/all_to_all | solution.py:251
  45.3 8.2 %collective-permute-start.1 = (bf16[2,8,4096]{2,1,0:T(8,128)(2,1)S(1)}, bf16[2,8,4096]{2,1,0:T(8,128)(2,1)S(1)}, u32[]{:S(2)}, u32[]{:S(2)}) collective-permute-start(bf16[2,8,4096]{2,1,0:T(8,128)(2,1)S(1)} %pad_maximum_fusion.2), channel_id=1, source_target_pairs={{0,28},{4,8},{8,4},{12,16},{16,12},{20,24},{24,20},{28,0},{1,29},{... | collective-permute-start | bytes 393224 | tf_op jit(solution)/shard_map/ppermute | solution.py:37
  53.4 17.6 %collective-permute-start.2 = (bf16[4,8,4096]{2,1,0:T(8,128)(2,1)S(1)}, bf16[4,8,4096]{2,1,0:T(8,128)(2,1)S(1)}, u32[]{:S(2)}, u32[]{:S(2)}) collective-permute-start(bf16[4,8,4096]{2,1,0:T(8,128)(2,1)S(1)} %pad_maximum_fusion.1), channel_id=1, source_target_pairs={{0,12},{4,24},{8,20},{12,0},{16,28},{20,8},{24,4},{28,16},{1,13},{... | collective-permute-start | bytes 786440 | tf_op jit(solution)/shard_map/ppermute | solution.py:40
  67.6 16.4 %all-to-all-start.2 = ((s16[16,40,256]{2,1,0:T(8,128)(2,1)}), s16[16,40,256]{2,1,0:T(8,128)(2,1)S(1)}, u32[]{:S(2)}, u32[]{:S(2)}) async-start(s16[16,40,256]{2,1,0:T(8,128)(2,1)} %shard_map.122), calls=%async_computation.2 | async-start | bytes 655360 | tf_op jit(solution)/shard_map/all_to_all | solution.py:253
  71.2 16.2 %collective-permute-start.3 = (bf16[8,8,4096]{2,1,0:T(8,128)(2,1)S(1)}, bf16[8,8,4096]{2,1,0:T(8,128)(2,1)S(1)}, u32[]{:S(2)}, u32[]{:S(2)}) collective-permute-start(bf16[8,8,4096]{2,1,0:T(8,128)(2,1)S(1)} %pad_maximum_fusion.refs_0_), channel_id=1, source_target_pairs={{0,1},{1,2},{2,3},{3,0},{4,5},{5,6},{6,7},{7,4},{8,9},{9,10},{10,1... | collective-permute-start | bytes 1572872 | tf_op jit(solution)/shard_map/ppermute | solution.py:228
  73.4 15.3 %collective-permute-start.4 = (bf16[8,8,4096]{2,1,0:T(8,128)(2,1)S(1)}, bf16[8,8,4096]{2,1,0:T(8,128)(2,1)S(1)}, u32[]{:S(2)}, u32[]{:S(2)}) collective-permute-start(bf16[8,8,4096]{2,1,0:T(8,128)(2,1)S(1)} %pad_maximum_fusion.refs_0_), channel_id=1, source_target_pairs={{0,3},{1,0},{2,1},{3,2},{4,7},{5,4},{6,5},{7,6},{8,11},{9,8},{10,9... | collective-permute-start | bytes 1572872 | tf_op jit(solution)/shard_map/ppermute | solution.py:228
  77.7 21.4 %collective-permute-start.5 = (bf16[8,8,4096]{2,1,0:T(8,128)(2,1)S(1)}, bf16[8,8,4096]{2,1,0:T(8,128)(2,1)S(1)}, u32[]{:S(2)}, u32[]{:S(2)}) collective-permute-start(bf16[8,8,4096]{2,1,0:T(8,128)(2,1)S(1)} %pad_maximum_fusion.refs_0_), channel_id=1, source_target_pairs={{0,2},{1,3},{2,0},{3,1},{4,6},{5,7},{6,4},{7,5},{8,10},{9,11},{10,... | collective-permute-start | bytes 1572872 | tf_op jit(solution)/shard_map/ppermute | solution.py:228
Sparse Core Ops, SparseCore 0:
  10.1 59.6 all-gather.2

commit v8 on v7

--- a/solution.py
+++ b/solution.py
@@ -90,32 +90,78 @@
 STEPS = 16384.0
 
 
-def update_kernel(total_ref, table_ref, coded_ref):
+def coded_rows(values):
+    parts, _, length = values.shape
+    largest = jnp.max(jnp.abs(values), axis=1)
+    exponent = jnp.ceil(jnp.log2(jnp.maximum(largest, 1e-30)))
+    steps = jnp.round(values * (jnp.exp2(-exponent) * STEPS)[:, None, :])
+    exponent = jnp.broadcast_to(exponent[:, None, :], (parts, 8, length))
+    return jnp.concatenate([steps, exponent], axis=1).astype(jnp.int32).astype(jnp.int16)
+
+
+def values_of(coded):
+    rows = coded.astype(jnp.int32).astype(jnp.float32)
+    share = rows.shape[1] - 8
+    return rows[:, :share] * (jnp.exp2(rows[:, share : share + 1]) * (1.0 / STEPS))
+
+
+def spectrum_kernel(mixed_ref, table_ref, mask_ref, coded_ref, sent_ref):
+    def split(x):
+        high = x.astype(jnp.bfloat16)
+        return high, (x - high.astype(jnp.float32)).astype(jnp.bfloat16)
+
+    def dot(x, y):
+        return lax.dot_general(
+            x, y, (((1,), (1,)), ((), ())), preferred_element_type=jnp.float32
+        )
+
+    blocks, length = mixed_ref.shape
+    high, low = split(mixed_ref[...])
+    table_high, table_low = split(table_ref[...])
+    spectrum = dot(high, table_high) + (dot(low, table_high) + dot(high, table_low))
+    sent_ref[:blocks] = jnp.where(mask_ref[:blocks] > 0.0, spectrum, 0.0)
+    sent_ref[blocks:] = jnp.zeros((sent_ref.shape[0] - blocks, length), jnp.float32)
+    workers, height, _ = coded_ref.shape
+    coded_ref[...] = coded_rows(sent_ref[...].reshape(workers, height - 8, length))
+
+
+def coded_spectrum(mixed, table, mask, workers):
+    rows, length = mask.shape
+    operands = [pltpu.with_memory_space_constraint(v, pltpu.VMEM) for v in (mixed, table, mask)]
+    return pl.pallas_call(
+        spectrum_kernel,
+        in_specs=[VMEM] * 3,
+        out_specs=[VMEM, VMEM],
+        out_shape=[
+            jax.ShapeDtypeStruct((workers, rows // workers + 8, length), jnp.int16),
+            jax.ShapeDtypeStruct((rows, length), jnp.float32),
+        ],
+        cost_estimate=pl.CostEstimate(
+            flops=6 * rows * length * length, bytes_accessed=4 * rows * length, transcendentals=0
+        ),
+    )(*operands)
+
+
+def update_kernel(parts_ref, table_ref, coded_ref):
     workers = coded_ref.shape[0]
-    share, length = total_ref.shape
     update = jnp.dot(
-        total_ref[...] * (1.0 / workers),
+        jnp.sum(values_of(parts_ref[...]), axis=0) * (1.0 / workers),
         table_ref[...],
         precision=lax.Precision.HIGHEST,
         preferred_element_type=jnp.float32,
     )
-    largest = jnp.max(jnp.abs(update), axis=0, keepdims=True)
-    exponent = jnp.ceil(jnp.log2(jnp.maximum(largest, 1e-30)))
-    value = jnp.round(update * (jnp.exp2(-exponent) * STEPS))
-    exponent = jnp.broadcast_to(exponent, (coded_ref.shape[1] - share, length))
-    rows = jnp.concatenate([value, exponent], axis=0).astype(jnp.int32).astype(jnp.int16)
+    rows = coded_rows(update[None])[0]
     for w in range(workers):
         coded_ref[w] = rows
 
 
-def coded_update(total, table, workers):
-    share, length = total.shape
+def coded_update(parts, table):
     return pl.pallas_call(
         update_kernel,
         in_specs=[VMEM, VMEM],
         out_specs=VMEM,
-        out_shape=jax.ShapeDtypeStruct((workers, share + 8, length), jnp.int16),
-    )(*[pltpu.with_memory_space_constraint(v, pltpu.VMEM) for v in (total, table)])
+        out_shape=jax.ShapeDtypeStruct(parts.shape, jnp.int16),
+    )(*[pltpu.with_memory_space_constraint(v, pltpu.VMEM) for v in (parts, table)])
 
 
 def decode_kernel(coded_ref, update_ref):
@@ -243,13 +289,11 @@
 
     cosine_table = jnp.asarray(cosine_matrix(length))
     mixed = momentum_decay * momentum[0] + worker_grad
-    spread = jnp.pad(mixed, ((0, rows - block_count), (0, 0)))
-    spectrum = jnp.dot(spread, cosine_table.T, precision=lax.Precision.HIGH)
-    sent = jnp.where(mask > 0.0, spectrum, 0.0)
+    coded_sent, sent = coded_spectrum(mixed, cosine_table, mask, workers)
     new_momentum = mixed - jnp.dot(sent[:block_count], cosine_table, precision=lax.Precision.HIGH)
 
-    parts = lax.all_to_all(sent.reshape(workers, share, length), DP, 0, 0)
-    coded = coded_update(parts.sum(0), cosine_table, workers)
+    parts = lax.all_to_all(coded_sent, DP, 0, 0)
+    coded = coded_update(parts, cosine_table)
     arrived = lax.all_to_all(coded, DP, 0, 0)
     update = decoded(arrived, block_count)
 

time: 113 us -> 110 us (0.973)
  waiting for transfers between devices: 36 us -> 30.8 us
  matrix products: 5.67 us -> 2.37 us
  starting transfers between devices: 43.3 us -> 45.4 us
  Pallas kernels: 7.82 us -> 9.44 us
    ppermute x1, waiting for transfers between devices: 6.01 us -> 0.01 us  [gathered_over_y(): second = lax.ppermute(pair, 'y', links)]
    ppermute x1, starting transfers between devices: 2.14 us -> 4.42 us  [gathered_over_y(): second = lax.ppermute(pair, 'y', links)]
    dot_general x1 -> x0, matrix products: 2.17 us -> none  [per_device_body(): spectrum = jnp.dot(spread, cosine_table.T, precision=lax.Precision.HIGH)]
    all_to_all x1, waiting for transfers between devices: 3.92 us -> 1.83 us  [gathered(): return lax.all_to_all(copies, axis, 0, 0)]
    all_to_all x1, starting transfers between devices: 10.5 us -> 8.77 us  [gathered(): return lax.all_to_all(copies, axis, 0, 0)]
    all_to_all x1, waiting for transfers between devices: 10.7 us -> 12.3 us  [per_device_body(): parts = lax.all_to_all(coded_sent, DP, 0, 0)]
    pallas_call x0 -> x1, Pallas kernels: none -> 1.34 us  [coded_spectrum(): pl.pallas_call(spectrum_kernel, in_specs=[VMEM] * 3, out_specs=[VMEM, VME...]
  transfers between devices with their start and end apart: 10 -> 10, of which waited for: 7 -> 6; matrix products, arithmetic and copies ran while one was open for 9% -> 7% of each run, Pallas kernels for 3% -> 4%
where the time goes in v8:
time: 110 us; the launch traced here: 108 us
  starting transfers between devices  45.4 us (41%)
  waiting for transfers between devices  30.8 us (28%)
  between operations  14.2 us (13%)
  Pallas kernels  9.44 us (9%)
  local copies, waits for them, and re-layouts  3.6 us (3%)
  matrix products  2.37 us (2%)
  other arithmetic  2.15 us (2%)
    ppermute x3, waiting for transfers between devices, per_device_body(): lax.ppermute(own_piece, 'x', [(i, (i + s) % 4) for i in range(4)])  14.6 us
    all_to_all x1, starting transfers between devices, per_device_body(): parts = lax.all_to_all(coded_sent, DP, 0, 0)  12.9 us
    all_to_all x1, waiting for transfers between devices, per_device_body(): parts = lax.all_to_all(coded_sent, DP, 0, 0)  12.3 us
    ppermute x3, starting transfers between devices, per_device_body(): lax.ppermute(own_piece, 'x', [(i, (i + s) % 4) for i in range(4)])  9.05 us
    all_to_all x1, starting transfers between devices, gathered(): return lax.all_to_all(copies, axis, 0, 0)  8.77 us
    pallas_call x1, Pallas kernels, product(): pl.pallas_call(product_kernel, grid_spec=pltpu.PrefetchScalarGridSpec(num...  5.09 us
    ppermute x1, starting transfers between devices, gathered_over_y(): second = lax.ppermute(pair, 'y', links)  4.42 us
    ppermute x1, starting transfers between devices, gathered_over_y(): near = lax.ppermute(value, 'y', [(i, i ^ 1) for i in range(8)])  4.02 us
  transfers between devices with their start and end apart: 10, of which 6 were waited for; matrix products, arithmetic and copies ran while one was open for 7% of the time, Pallas kernels for 4%

profile of v8, /device:TPU:1, one launch (start us, length us, event | category | flops | bytes accessed | tf_op | source)
XLA Modules:
  0.0 108.0 jit_solution(2940840186270209465)
XLA Ops:
  7.9 4.0 %collective-permute-start = (bf16[8,4096]{1,0:T(8,128)(2,1)}, bf16[8,4096]{1,0:T(8,128)(2,1)S(1)}, u32[]{:S(2)}, u32[]{:S(2)}) collective-permute-start(bf16[8,4096]{1,0:T(8,128)(2,1)} %param.9), channel_id=1, source_target_pairs={{0,4},{4,0},{8,12},{12,8},{16,20},{20,16},{24,28},{28,24},{1,5},{5... | collective-permute-start | bytes 196616 | tf_op jit(solution)/shard_map/ppermute | solution.py:34
  13.3 8.8 %all-to-all-start = ((bf16[32,8,256]{2,1,0:T(8,128)(2,1)}), bf16[32,8,256]{2,1,0:T(8,128)(2,1)S(1)}, u32[]{:S(2)}, u32[]{:S(2)}) async-start(bf16[32,8,256]{2,1,0:T(8,128)(2,1)} %broadcast_in_dim.4), calls=%async_computation | async-start | bytes 262144 | tf_op jit(solution)/shard_map/all_to_all | solution.py:30
  22.1 1.2 %fusion.7 = bf16[256,464]{0,1:T(8,128)(2,1)S(1)} fusion(bf16[256,464]{0,1:T(8,128)(2,1)} %param.11, bf16[256,464]{0,1:T(8,128)(2,1)} %param.10), kind=kLoop, calls=%fused_computation.12 | loop fusion | flops 950272 | bytes 712704 | tf_op jit(solution)/shard_map/convert_element_type | solution.py:277
  23.3 1.1 shard_map.121.mask_ref
  25.3 4.4 %collective-permute-start.1 = (bf16[2,8,4096]{2,1,0:T(8,128)(2,1)S(1)}, bf16[2,8,4096]{2,1,0:T(8,128)(2,1)S(1)}, u32[]{:S(2)}, u32[]{:S(2)}) collective-permute-start(bf16[2,8,4096]{2,1,0:T(8,128)(2,1)S(1)} %pad_maximum_fusion.2), channel_id=1, source_target_pairs={{0,28},{4,8},{8,4},{12,16},{16,12},{20,24},{24,20},{28,0},{1,29},{... | collective-permute-start | bytes 393224 | tf_op jit(solution)/shard_map/ppermute | solution.py:37
  29.7 1.8 %all-to-all-done = bf16[32,8,256]{2,1,0:T(8,128)(2,1)S(1)} async-done(((bf16[32,8,256]{2,1,0:T(8,128)(2,1)}), bf16[32,8,256]{2,1,0:T(8,128)(2,1)S(1)}, u32[]{:S(2)}, u32[]{:S(2)}) %all-to-all-start) | async-done | bytes 131104 | tf_op jit(solution)/shard_map/all_to_all | solution.py:30
  31.5 1.2 %fusion.mixed_ref = f32[464,256]{1,0:T(8,128)S(1)} fusion(bf16[256,464]{0,1:T(8,128)(2,1)S(1)} %fusion.7, f32[1,464,256]{2,1,0:T(8,128)} %param.13, bf16[32,8,256]{2,1,0:T(8,128)(2,1)S(1)} %all-to-all-done), kind=kOutput, calls=%fused_computation.1 | convolution fusion | flops 61173760 | bytes 1318912 | tf_op jit(solution)/shard_map/dot_general | solution.py:282
  32.8 0.9 copy-done
  33.7 1.3 %shard_map.122 = (s16[16,40,256]{2,1,0:T(8,128)(2,1)}, f32[512,256]{1,0:T(8,128)}) custom-call(f32[464,256]{1,0:T(8,128)S(1)} %fusion.mixed_ref, f32[256,256]{1,0:T(8,128)S(1)} %copy-done, f32[512,256]{1,0:T(8,128)S(1)} %shard_map.121.mask_ref), custom_call_target="tpu_custom_call" | custom-call | flops 201326592 | bytes 524288 | tf_op jit(solution)/shard_map/pallas_call | solution.py:131
  35.1 12.9 %all-to-all-start.1 = ((s16[16,40,256]{2,1,0:T(8,128)(2,1)}), s16[16,40,256]{2,1,0:T(8,128)(2,1)S(1)}, u32[]{:S(2)}, u32[]{:S(2)}) async-start(s16[16,40,256]{2,1,0:T(8,128)(2,1)} %get-tuple-element.11), calls=%async_computation.1 | async-start | bytes 655360 | tf_op jit(solution)/shard_map/all_to_all | solution.py:295
  48.0 2.7 %collective-permute-start.2 = (bf16[4,8,4096]{2,1,0:T(8,128)(2,1)S(1)}, bf16[4,8,4096]{2,1,0:T(8,128)(2,1)S(1)}, u32[]{:S(2)}, u32[]{:S(2)}) collective-permute-start(bf16[4,8,4096]{2,1,0:T(8,128)(2,1)S(1)} %pad_maximum_fusion.1), channel_id=1, source_target_pairs={{0,12},{4,24},{8,20},{12,0},{16,28},{20,8},{24,4},{28,16},{1,13},{... | collective-permute-start | bytes 786440 | tf_op jit(solution)/shard_map/ppermute | solution.py:40
  50.6 12.3 %all-to-all-done.1.parts_ref = s16[16,40,256]{2,1,0:T(8,128)(2,1)S(1)} async-done(((s16[16,40,256]{2,1,0:T(8,128)(2,1)}), s16[16,40,256]{2,1,0:T(8,128)(2,1)S(1)}, u32[]{:S(2)}, u32[]{:S(2)}) %all-to-all-start.1) | async-done | bytes 327712 | tf_op jit(solution)/shard_map/all_to_all | solution.py:295
  62.9 1.1 %shard_map.123 = s16[16,40,256]{2,1,0:T(8,128)(2,1)} custom-call(s16[16,40,256]{2,1,0:T(8,128)(2,1)S(1)} %all-to-all-done.1.parts_ref, f32[256,256]{1,0:T(8,128)S(1)} %copy-done.1), custom_call_target="tpu_custom_call" | custom-call | tf_op jit(solution)/shard_map/pallas_call | solution.py:159
  64.0 3.6 %all-to-all-start.2 = ((s16[16,40,256]{2,1,0:T(8,128)(2,1)}), s16[16,40,256]{2,1,0:T(8,128)(2,1)S(1)}, u32[]{:S(2)}, u32[]{:S(2)}) async-start(s16[16,40,256]{2,1,0:T(8,128)(2,1)} %shard_map.123), calls=%async_computation.2 | async-start | bytes 655360 | tf_op jit(solution)/shard_map/all_to_all | solution.py:297
  67.7 2.9 %collective-permute-start.3 = (bf16[8,8,4096]{2,1,0:T(8,128)(2,1)S(1)}, bf16[8,8,4096]{2,1,0:T(8,128)(2,1)S(1)}, u32[]{:S(2)}, u32[]{:S(2)}) collective-permute-start(bf16[8,8,4096]{2,1,0:T(8,128)(2,1)S(1)} %pad_maximum_fusion.refs_0_), channel_id=1, source_target_pairs={{0,1},{1,2},{2,3},{3,0},{4,5},{5,6},{6,7},{7,4},{8,9},{9,10},{10,1... | collective-permute-start | bytes 1572872 | tf_op jit(solution)/shard_map/ppermute | solution.py:274
  70.6 3.6 %collective-permute-start.4 = (bf16[8,8,4096]{2,1,0:T(8,128)(2,1)S(1)}, bf16[8,8,4096]{2,1,0:T(8,128)(2,1)S(1)}, u32[]{:S(2)}, u32[]{:S(2)}) collective-permute-start(bf16[8,8,4096]{2,1,0:T(8,128)(2,1)S(1)} %pad_maximum_fusion.refs_0_), channel_id=1, source_target_pairs={{0,3},{1,0},{2,1},{3,2},{4,7},{5,4},{6,5},{7,6},{8,11},{9,8},{10,9... | collective-permute-start | bytes 1572872 | tf_op jit(solution)/shard_map/ppermute | solution.py:274
  74.2 2.6 %collective-permute-start.5 = (bf16[8,8,4096]{2,1,0:T(8,128)(2,1)S(1)}, bf16[8,8,4096]{2,1,0:T(8,128)(2,1)}, u32[]{:S(2)}, u32[]{:S(2)}) collective-permute-start(bf16[8,8,4096]{2,1,0:T(8,128)(2,1)S(1)} %pad_maximum_fusion.refs_0_), channel_id=1, source_target_pairs={{0,2},{1,3},{2,0},{3,1},{4,6},{5,7},{6,4},{7,5},{8,10},{9,11},{10,... | collective-permute-start | bytes 1572872 | tf_op jit(solution)/shard_map/ppermute | solution.py:274
  76.8 1.3 %dynamic-slice_bitcast_fusion.order_ref = s32[12]{0:T(128)} fusion(s32[32,12]{1,0:T(8,128)} %constant.25.clone, s32[]{:T(128)S(6)} %select_n.3), kind=kLoop, calls=%fused_computation.16 | loop fusion | bytes 100 | tf_op jit(solution)/shard_map/squeeze | solution.py:58
  78.1 1.1 %fusion.1 = f32[1,464,256]{2,1,0:T(8,128)} fusion(f32[464,256]{1,0:T(8,128)S(1)} %fusion.mixed_ref, f32[256,256]{1,0:T(8,128)S(1)} %copy-done.1, f32[512,256]{1,0:T(8,128)S(1)} %copy-done.3), kind=kOutput, calls=%fused_computation.3 | convolution fusion | flops 182571008 | bytes 1687552 | tf_op jit(solution)/shard_map/dot_general | solution.py:293
  79.2 1.4 %all-to-all-done.2.coded_ref = s16[16,40,256]{2,1,0:T(8,128)(2,1)S(1)} async-done(((s16[16,40,256]{2,1,0:T(8,128)(2,1)}), s16[16,40,256]{2,1,0:T(8,128)(2,1)S(1)}, u32[]{:S(2)}, u32[]{:S(2)}) %all-to-all-start.2) | async-done | bytes 327712 | tf_op jit(solution)/shard_map/all_to_all | solution.py:297
  81.5 2.7 %collective-permute-done.3.refs_1_ = bf16[8,8,4096]{2,1,0:T(8,128)(2,1)S(1)} collective-permute-done((bf16[8,8,4096]{2,1,0:T(8,128)(2,1)S(1)}, bf16[8,8,4096]{2,1,0:T(8,128)(2,1)S(1)}, u32[]{:S(2)}, u32[]{:S(2)}) %collective-permute-start.3) | collective-permute-done | bytes 524320 | tf_op jit(solution)/shard_map/ppermute | solution.py:274
  84.2 1.3 %collective-permute-done.4.refs_2_ = bf16[8,8,4096]{2,1,0:T(8,128)(2,1)S(1)} collective-permute-done((bf16[8,8,4096]{2,1,0:T(8,128)(2,1)S(1)}, bf16[8,8,4096]{2,1,0:T(8,128)(2,1)S(1)}, u32[]{:S(2)}, u32[]{:S(2)}) %collective-permute-start.4) | collective-permute-done | bytes 524320 | tf_op jit(solution)/shard_map/ppermute | solution.py:274
  85.5 10.6 %collective-permute-done.5.refs_3_ = bf16[8,8,4096]{2,1,0:T(8,128)(2,1)} collective-permute-done((bf16[8,8,4096]{2,1,0:T(8,128)(2,1)S(1)}, bf16[8,8,4096]{2,1,0:T(8,128)(2,1)}, u32[]{:S(2)}, u32[]{:S(2)}) %collective-permute-start.5) | collective-permute-done | bytes 524320 | tf_op jit(solution)/shard_map/ppermute | solution.py:274
  96.1 5.1 %shard_map.120 = (bf16[464,256]{1,0:T(8,128)(2,1)}, bf16[464,256]{1,0:T(8,128)(2,1)}) custom-call(s32[12]{0:T(128)} %dynamic-slice_bitcast_fusion.order_ref, bf16[8,8,4096]{2,1,0:T(8,128)(2,1)S(1)} %pad_maximum_fusion.refs_0_, bf16[8,8,4096]{2,1,0:T(8,128)(2,1)S(1)} %collective-permute-done.3.refs_1_, ...), custom_call_target="tpu_custom_call" | custom-call | flops 973078528 | bytes 6848512 | tf_op jit(solution)/shard_map/pallas_call | solution.py:239
  (19 shorter events, 3.9 us)
Async XLA Ops:
  7.2 55.8 %copy-start.1 = (f32[256,256]{1,0:T(8,128)S(1)}, f32[256,256]{1,0:T(8,128)}, u32[]{:S(2)}) copy-start(f32[256,256]{1,0:T(8,128)} %constant.26.clone.table_ref) | copy-start | bytes 786436
  7.2 40.8 %copy-start.2 = (bf16[8,4096]{1,0:T(8,128)(2,1)S(1)}, bf16[8,4096]{1,0:T(8,128)(2,1)}, u32[]{:S(2)}) copy-start(bf16[8,4096]{1,0:T(8,128)(2,1)} %param.9) | copy-start | bytes 196612
  7.2 88.9 %all-gather.3.cloned.1.call-start = ((), (), s32[]{:S(2)}) async-start(), calls=%async_computation.3 | async-start | bytes 4038656 | tf_op jit(solution)/shard_map/all_gather | solution.py:269
  7.9 16.5 %collective-permute-start = (bf16[8,4096]{1,0:T(8,128)(2,1)}, bf16[8,4096]{1,0:T(8,128)(2,1)S(1)}, u32[]{:S(2)}, u32[]{:S(2)}) collective-permute-start(bf16[8,4096]{1,0:T(8,128)(2,1)} %param.9), channel_id=1, source_target_pairs={{0,4},{4,0},{8,12},{12,8},{16,20},{20,16},{24,28},{28,24},{1,5},{5... | collective-permute-start | bytes 196616 | tf_op jit(solution)/shard_map/ppermute | solution.py:34
  13.3 18.2 %all-to-all-start = ((bf16[32,8,256]{2,1,0:T(8,128)(2,1)}), bf16[32,8,256]{2,1,0:T(8,128)(2,1)S(1)}, u32[]{:S(2)}, u32[]{:S(2)}) async-start(bf16[32,8,256]{2,1,0:T(8,128)(2,1)} %broadcast_in_dim.4), calls=%async_computation | async-start | bytes 262144 | tf_op jit(solution)/shard_map/all_to_all | solution.py:30
  25.3 22.7 %collective-permute-start.1 = (bf16[2,8,4096]{2,1,0:T(8,128)(2,1)S(1)}, bf16[2,8,4096]{2,1,0:T(8,128)(2,1)S(1)}, u32[]{:S(2)}, u32[]{:S(2)}) collective-permute-start(bf16[2,8,4096]{2,1,0:T(8,128)(2,1)S(1)} %pad_maximum_fusion.2), channel_id=1, source_target_pairs={{0,28},{4,8},{8,4},{12,16},{16,12},{20,24},{24,20},{28,0},{1,29},{... | collective-permute-start | bytes 393224 | tf_op jit(solution)/shard_map/ppermute | solution.py:37
  32.8 1.0 copy-start
  35.0 43.0 %copy-start.3 = (f32[512,256]{1,0:T(8,128)S(1)}, f32[512,256]{1,0:T(8,128)}, u32[]{:S(2)}) copy-start(f32[512,256]{1,0:T(8,128)} %get-tuple-element.10) | copy-start | bytes 1572868
  35.1 27.9 %all-to-all-start.1 = ((s16[16,40,256]{2,1,0:T(8,128)(2,1)}), s16[16,40,256]{2,1,0:T(8,128)(2,1)S(1)}, u32[]{:S(2)}, u32[]{:S(2)}) async-start(s16[16,40,256]{2,1,0:T(8,128)(2,1)} %get-tuple-element.11), calls=%async_computation.1 | async-start | bytes 655360 | tf_op jit(solution)/shard_map/all_to_all | solution.py:295
  48.0 19.7 %collective-permute-start.2 = (bf16[4,8,4096]{2,1,0:T(8,128)(2,1)S(1)}, bf16[4,8,4096]{2,1,0:T(8,128)(2,1)S(1)}, u32[]{:S(2)}, u32[]{:S(2)}) collective-permute-start(bf16[4,8,4096]{2,1,0:T(8,128)(2,1)S(1)} %pad_maximum_fusion.1), channel_id=1, source_target_pairs={{0,12},{4,24},{8,20},{12,0},{16,28},{20,8},{24,4},{28,16},{1,13},{... | collective-permute-start | bytes 786440 | tf_op jit(solution)/shard_map/ppermute | solution.py:40
  64.0 16.6 %all-to-all-start.2 = ((s16[16,40,256]{2,1,0:T(8,128)(2,1)}), s16[16,40,256]{2,1,0:T(8,128)(2,1)S(1)}, u32[]{:S(2)}, u32[]{:S(2)}) async-start(s16[16,40,256]{2,1,0:T(8,128)(2,1)} %shard_map.123), calls=%async_computation.2 | async-start | bytes 655360 | tf_op jit(solution)/shard_map/all_to_all | solution.py:297
  67.7 16.5 %collective-permute-start.3 = (bf16[8,8,4096]{2,1,0:T(8,128)(2,1)S(1)}, bf16[8,8,4096]{2,1,0:T(8,128)(2,1)S(1)}, u32[]{:S(2)}, u32[]{:S(2)}) collective-permute-start(bf16[8,8,4096]{2,1,0:T(8,128)(2,1)S(1)} %pad_maximum_fusion.refs_0_), channel_id=1, source_target_pairs={{0,1},{1,2},{2,3},{3,0},{4,5},{5,6},{6,7},{7,4},{8,9},{9,10},{10,1... | collective-permute-start | bytes 1572872 | tf_op jit(solution)/shard_map/ppermute | solution.py:274
  70.6 14.9 %collective-permute-start.4 = (bf16[8,8,4096]{2,1,0:T(8,128)(2,1)S(1)}, bf16[8,8,4096]{2,1,0:T(8,128)(2,1)S(1)}, u32[]{:S(2)}, u32[]{:S(2)}) collective-permute-start(bf16[8,8,4096]{2,1,0:T(8,128)(2,1)S(1)} %pad_maximum_fusion.refs_0_), channel_id=1, source_target_pairs={{0,3},{1,0},{2,1},{3,2},{4,7},{5,4},{6,5},{7,6},{8,11},{9,8},{10,9... | collective-permute-start | bytes 1572872 | tf_op jit(solution)/shard_map/ppermute | solution.py:274
  74.2 21.8 %collective-permute-start.5 = (bf16[8,8,4096]{2,1,0:T(8,128)(2,1)S(1)}, bf16[8,8,4096]{2,1,0:T(8,128)(2,1)}, u32[]{:S(2)}, u32[]{:S(2)}) collective-permute-start(bf16[8,8,4096]{2,1,0:T(8,128)(2,1)S(1)} %pad_maximum_fusion.refs_0_), channel_id=1, source_target_pairs={{0,2},{1,3},{2,0},{3,1},{4,6},{5,7},{6,4},{7,5},{8,10},{9,11},{10,... | collective-permute-start | bytes 1572872 | tf_op jit(solution)/shard_map/ppermute | solution.py:274
Sparse Core Ops, SparseCore 0:
  10.1 56.4 all-gather.2
